TPU v7x, 32 devices: a whole 2x2x4 slice. The times are simulated.
32 devices in a mesh: row: 4 (over y, core), col: 8 (over z, x).
Axes of the slice: x: 2, y: 2, z: 4, core: 2. Of those that a mesh axis runs over, the one named last changes fastest.
Arguments:
- hidden_in: float32 [1280, 8192], P('col', 'row'), may hold values from -6 to 6
- lengths: int32 [8], replicated, may hold values from 256 to 1024, as said below
- ln1_gain: float32 [1280], P('col'), may hold values from 0.25 to 1.75
- ln1_shift: float32 [1280], P('col'), may hold values from -1.5 to 1.5
- qkv_weight: bfloat16 [3, 1280, 1280], P(None, 'row', 'col'), may hold values from -0.21875 to 0.21875
- qv_bias: float32 [2, 1280], P(None, 'col'), may hold values from -2.5 to 2.5
- out_weight: bfloat16 [1280, 1280], P('col', 'row'), may hold values from -1.25 to 1.25
- out_bias: float32 [1280], P('col'), may hold values from -1.5 to 1.5
- ln2_gain: float32 [1280], P('col'), may hold values from 0.25 to 1.75
- ln2_shift: float32 [1280], P('col'), may hold values from -1.5 to 1.5
- in_weight: bfloat16 [1280, 5120], P('row', 'col'), may hold values from -0.15625 to 0.15625
- in_bias: float32 [5120], P('col'), may hold values from -2.5 to 2.5
- down_weight: bfloat16 [5120, 1280], P('col', 'row'), may hold values from -0.078125 to 0.078125
- down_bias: float32 [1280], P('col'), may hold values from -1.5 to 1.5
- cotangent: float32 [1280, 8192], P('col', 'row'), may hold values from -6 to 6
Outputs:
- hidden_out: float32 [1280, 8192], P('col', 'row')
- hidden_grad: float32 [1280, 8192], P('col', 'row')
- ln1_gain_grad: float32 [1280], P('col')
- ln1_shift_grad: float32 [1280], P('col')
- qkv_weight_grad: float32 [3, 1280, 1280], P(None, 'row', 'col')
- qv_bias_grad: float32 [2, 1280], P(None, 'col')
- out_weight_grad: float32 [1280, 1280], P('col', 'row')
- out_bias_grad: float32 [1280], P('col')
- ln2_gain_grad: float32 [1280], P('col')
- ln2_shift_grad: float32 [1280], P('col')
- in_weight_grad: float32 [1280, 5120], P('row', 'col')
- in_bias_grad: float32 [5120], P('col')
- down_weight_grad: float32 [5120, 1280], P('col', 'row')
- down_bias_grad: float32 [1280], P('col')
Inputs may be any that keep to these rules, and one draw needn't show every extreme that they name: lengths[c] is the number of valid tokens at the start of clip c; later positions of the clip are padding.
All inputs are finite; a program needn't handle non-finite values.
Results may differ from a plain program's by a relative error of at most 0.012.
The roundings to bfloat16 on the way count: a program that leaves them out, or rounds other values in their place, can miss the bound.
Values may be sent and summed in bfloat16 or wider, within the bound.
No kernel may reach another device: no remote copies, remote signals or barrier semaphores. Data moves between devices by JAX's collectives and lax.ppermute only.
A program may use at most 320 MiB of HBM per device.

v0:
```python
import jax
import jax.numpy as jnp
from jax import lax
from jax.sharding import PartitionSpec as P

HEADS = 16
HEAD_DIM = 80
D = 1280
MICRO = 2
GROUP = 8


EPS = 1e-05


def partner(block, axis, distance):
    count = lax.axis_size(axis)
    route = []
    for low in range(count):
        high = low | 1 << distance
        if high != low and high < count:
            route += [(low, high), (high, low)]
    return lax.ppermute(block, axis, route)


def row_totals(first_sum, second_sum):
    return lax.psum((first_sum, second_sum), "col")


def widen(values):
    return lax.all_gather(values, "col", axis=1, tiled=True)


def narrow(values):
    return lax.psum_scatter(values, "col", scatter_dimension=1, tiled=True)


def to_clips(stacked):
    return lax.all_to_all(stacked, "col", split_axis=1, concat_axis=2, tiled=True)


def to_columns(stacked):
    return lax.all_to_all(stacked, "col", split_axis=2, concat_axis=1, tiled=True)


def contract_rows(left, right):
    return lax.dot_general(
        left, right, (((0,), (0,)), ((), ())), preferred_element_type=jnp.float32
    )


def contract_cols(left, right):
    return lax.dot_general(
        left, right, (((1,), (1,)), ((), ())), preferred_element_type=jnp.float32
    )


def exact_gelu(values):
    return jax.nn.gelu(values, approximate=False)


def norm_forward(values, norm_gain, norm_shift):
    first_sum, second_sum = row_totals(jnp.sum(values, axis=1), jnp.sum(values * values, axis=1))
    mean_rows = first_sum / D
    inv_std = lax.rsqrt(second_sum / D - mean_rows * mean_rows + EPS)
    normed = (values - mean_rows[:, None]) * inv_std[:, None]
    return (normed, inv_std, normed * norm_gain + norm_shift)


def norm_backward(grad_out, normed, inv_std, norm_gain):
    scaled = grad_out * norm_gain
    first_sum, second_sum = row_totals(jnp.sum(scaled, axis=1), jnp.sum(scaled * normed, axis=1))
    grad_input = inv_std[:, None] * (
        scaled - first_sum[:, None] / D - normed * (second_sum[:, None] / D)
    )
    return (grad_input, jnp.sum(grad_out * normed, axis=0), jnp.sum(grad_out, axis=0))


def split_heads(values):
    return values.reshape(values.shape[0], HEADS, HEAD_DIM)


def gather_clip(key_rows, value_rows):
    position = lax.axis_index("col")
    for bit_index in range(GROUP.bit_length() - 1):
        other_keys, other_values = partner((key_rows, value_rows), "col", bit_index)
        upper_half = position >> bit_index & 1 == 1
        key_rows = jnp.where(
            upper_half,
            jnp.concatenate([other_keys, key_rows]),
            jnp.concatenate([key_rows, other_keys]),
        )
        value_rows = jnp.where(
            upper_half,
            jnp.concatenate([other_values, value_rows]),
            jnp.concatenate([value_rows, other_values]),
        )
    return (key_rows, value_rows)


def scatter_clip(grad_keys, grad_values):
    position = lax.axis_index("col")
    for bit_index in reversed(range(GROUP.bit_length() - 1)):
        half_rows = grad_keys.shape[0] // 2
        upper_half = position >> bit_index & 1 == 1
        keep_keys = jnp.where(upper_half, grad_keys[half_rows:], grad_keys[:half_rows])
        send_keys = jnp.where(upper_half, grad_keys[:half_rows], grad_keys[half_rows:])
        keep_values = jnp.where(upper_half, grad_values[half_rows:], grad_values[:half_rows])
        send_values = jnp.where(upper_half, grad_values[:half_rows], grad_values[half_rows:])
        got_keys, got_values = partner((send_keys, send_values), "col", bit_index)
        grad_keys = keep_keys + got_keys
        grad_values = keep_values + got_values
    return (grad_keys, grad_values)


def clip_scores(queries, key_rows, valid_len):
    scale_factor = HEAD_DIM ** (-0.5)
    scores = (
        jnp.einsum(
            "qhe,khe->hqk",
            split_heads(queries),
            split_heads(key_rows),
            preferred_element_type=jnp.float32,
        )
        * scale_factor
    )
    live_keys = lax.broadcasted_iota(jnp.int32, (1, 1, key_rows.shape[0]), 2) < valid_len
    return jnp.where(live_keys, scores, -1e30)


def attend(queries, key_rows, value_rows, valid_len):
    scores = clip_scores(queries, key_rows, valid_len)
    top_score = jnp.max(scores, axis=2, keepdims=True)
    weights = jnp.exp(scores - top_score)
    weight_sum = jnp.sum(weights, axis=2, keepdims=True)
    prob_low = (weights / weight_sum).astype(jnp.bfloat16)
    attended = jnp.einsum(
        "hqk,khe->qhe", prob_low, split_heads(value_rows), preferred_element_type=jnp.float32
    )
    return (attended.reshape(queries.shape[0], -1), top_score + jnp.log(weight_sum))


def attend_back(queries, key_rows, value_rows, valid_len, log_sum, grad_low):
    scale_factor = HEAD_DIM ** (-0.5)
    scores = clip_scores(queries, key_rows, valid_len)
    probs_full = jnp.exp(scores - log_sum)
    grad_heads = split_heads(grad_low)
    grad_value = jnp.einsum(
        "hqk,qhe->khe",
        probs_full.astype(jnp.bfloat16),
        grad_heads,
        preferred_element_type=jnp.float32,
    )
    grad_probs = jnp.einsum(
        "qhe,khe->hqk", grad_heads, split_heads(value_rows), preferred_element_type=jnp.float32
    )
    row_dot = jnp.sum(probs_full * grad_probs, axis=2, keepdims=True)
    grad_scores = (probs_full * (grad_probs - row_dot)).astype(jnp.bfloat16)
    grad_query = (
        jnp.einsum(
            "hqk,khe->qhe", grad_scores, split_heads(key_rows), preferred_element_type=jnp.float32
        )
        * scale_factor
    )
    grad_key = (
        jnp.einsum(
            "hqk,qhe->khe", grad_scores, split_heads(queries), preferred_element_type=jnp.float32
        )
        * scale_factor
    )
    return (
        grad_query.reshape(queries.shape[0], -1),
        grad_key.reshape(key_rows.shape[0], -1),
        grad_value.reshape(key_rows.shape[0], -1),
    )


def layer_pass(input_rows, grad_rows, weights, vectors, valid_len):
    qkv_full, out_full, in_full, down_full = weights
    gain_one, shift_one, qv_full, out_shift, gain_two, shift_two, in_shift, down_shift = vectors
    bias_three = jnp.stack([qv_full[0], jnp.zeros_like(qv_full[0]), qv_full[1]])[:, None, :]
    normed_one, inv_one, ln_one = norm_forward(input_rows, gain_one, shift_one)
    wide_one = widen(ln_one.astype(jnp.bfloat16))
    projected = (
        jnp.einsum("td,sdc->stc", wide_one, qkv_full, preferred_element_type=jnp.float32)
        + bias_three
    )
    projected = to_clips(projected.astype(jnp.bfloat16))
    key_rows, value_rows = gather_clip(projected[1], projected[2])
    attended, log_sum = attend(projected[0], key_rows, value_rows, valid_len)
    attended_low = to_columns(attended.astype(jnp.bfloat16)[None])[0]
    hidden_mid = (
        input_rows
        + narrow(jnp.dot(attended_low, out_full, preferred_element_type=jnp.float32))
        + out_shift
    )
    normed_two, inv_two, ln_two = norm_forward(hidden_mid, gain_two, shift_two)
    wide_two = widen(ln_two.astype(jnp.bfloat16))
    pre_act = jnp.dot(wide_two, in_full, preferred_element_type=jnp.float32) + in_shift
    act_value, gelu_back = jax.vjp(exact_gelu, pre_act)
    act_low = act_value.astype(jnp.bfloat16)
    hidden_out = (
        hidden_mid
        + narrow(jnp.dot(act_low, down_full, preferred_element_type=jnp.float32))
        + down_shift
    )
    grad_wide = widen(grad_rows.astype(jnp.bfloat16))
    grad_down = contract_rows(act_low, grad_wide)
    grad_pre = gelu_back(contract_cols(grad_wide, down_full))[0].astype(jnp.bfloat16)
    grad_in = contract_rows(wide_two, grad_pre)
    grad_ln_two = narrow(contract_cols(grad_pre, in_full))
    grad_norm_two, grad_gain_two, grad_shift_two = norm_backward(
        grad_ln_two, normed_two, inv_two, gain_two
    )
    grad_mid = grad_rows + grad_norm_two
    grad_mid_wide = widen(grad_mid.astype(jnp.bfloat16))
    grad_out = contract_rows(attended_low, grad_mid_wide)
    grad_attended = to_clips(contract_cols(grad_mid_wide, out_full).astype(jnp.bfloat16)[None])[0]
    grad_query, grad_key, grad_value = attend_back(
        projected[0], key_rows, value_rows, valid_len, log_sum, grad_attended
    )
    grad_key, grad_value = scatter_clip(grad_key, grad_value)
    grad_proj = to_columns(jnp.stack([grad_query, grad_key, grad_value]).astype(jnp.bfloat16))
    grad_qkv = jnp.einsum("td,stc->sdc", wide_one, grad_proj, preferred_element_type=jnp.float32)
    grad_ln_one = narrow(
        jnp.einsum("stc,sdc->td", grad_proj, qkv_full, preferred_element_type=jnp.float32)
    )
    grad_norm_one, grad_gain_one, grad_shift_one = norm_backward(
        grad_ln_one, normed_one, inv_one, gain_one
    )
    grad_input = grad_mid + grad_norm_one
    proj_sums = jnp.sum(grad_proj, axis=1, dtype=jnp.float32)
    vector_parts = (
        grad_gain_one,
        grad_shift_one,
        jnp.stack([proj_sums[0], proj_sums[2]]),
        jnp.sum(grad_mid, axis=0),
        grad_gain_two,
        grad_shift_two,
        jnp.sum(grad_pre, axis=0, dtype=jnp.float32),
        jnp.sum(grad_rows, axis=0),
    )
    return (hidden_out, grad_input, (grad_qkv, grad_out, grad_in, grad_down), vector_parts)


def tile_grid(vector, row_count):
    return jnp.broadcast_to(vector[None], (row_count,) + vector.shape)


def grid_reduce(partials, vector_parts):
    row_count = lax.axis_size("row")
    qkv_part, out_part, in_part, down_part = partials
    qkv_blocks = qkv_part.reshape(3, row_count, -1, qkv_part.shape[2]).transpose(1, 0, 2, 3)
    out_blocks = out_part.reshape(out_part.shape[0], row_count, -1).transpose(1, 0, 2)
    in_blocks = in_part.reshape(row_count, -1, in_part.shape[1])
    down_blocks = down_part.reshape(down_part.shape[0], row_count, -1).transpose(1, 0, 2)
    tiled = [tile_grid(vector, row_count) for vector in vector_parts]
    reduced = (
        lax.psum_scatter(qkv_blocks, "row", scatter_dimension=0, tiled=True),
        lax.psum_scatter(out_blocks, "row", scatter_dimension=0, tiled=True),
        lax.psum_scatter(in_blocks, "row", scatter_dimension=0, tiled=True),
        lax.psum_scatter(down_blocks, "row", scatter_dimension=0, tiled=True),
        lax.psum_scatter(tiled[0], "row", scatter_dimension=0, tiled=True),
        lax.psum_scatter(tiled[1], "row", scatter_dimension=0, tiled=True),
        lax.psum_scatter(tiled[2], "row", scatter_dimension=0, tiled=True),
        lax.psum_scatter(tiled[3], "row", scatter_dimension=0, tiled=True),
        lax.psum_scatter(tiled[4], "row", scatter_dimension=0, tiled=True),
        lax.psum_scatter(tiled[5], "row", scatter_dimension=0, tiled=True),
        lax.psum_scatter(tiled[6], "row", scatter_dimension=0, tiled=True),
        lax.psum_scatter(tiled[7], "row", scatter_dimension=0, tiled=True),
    )
    return tuple((piece[0] for piece in reduced))


def local(
    hidden_in,
    lengths,
    ln1_gain,
    ln1_shift,
    qkv_weight,
    qv_bias,
    out_weight,
    out_bias,
    ln2_gain,
    ln2_shift,
    in_weight,
    in_bias,
    down_weight,
    down_bias,
    cotangent,
):
    col_count = lax.axis_size("col")
    token_rows = jnp.transpose(hidden_in)
    cot_rows = jnp.transpose(cotangent)
    rows_block = token_rows.shape[0] // MICRO
    weights = (
        lax.all_gather(qkv_weight, "row", axis=1, tiled=True),
        lax.all_gather(out_weight, "row", axis=1, tiled=True),
        lax.all_gather(in_weight, "row", axis=0, tiled=True),
        lax.all_gather(down_weight, "row", axis=1, tiled=True),
    )
    vectors = (ln1_gain, ln1_shift, qv_bias, out_bias, ln2_gain, ln2_shift, in_bias, down_bias)
    clip_slot = lax.axis_index("col") // GROUP
    outputs = []
    input_grads = []
    totals = None
    running = None
    for micro_index in range(MICRO):
        input_rows = token_rows[micro_index * rows_block : (micro_index + 1) * rows_block]
        grad_rows = cot_rows[micro_index * rows_block : (micro_index + 1) * rows_block]
        clip_id = (lax.axis_index("row") * MICRO + micro_index) * (col_count // GROUP) + clip_slot
        valid_len = lax.dynamic_index_in_dim(lengths, clip_id, keepdims=False)
        out_rows, back_rows, partials, vector_parts = layer_pass(
            input_rows, grad_rows, weights, vectors, valid_len
        )
        outputs.append(out_rows)
        input_grads.append(back_rows)
        current = (partials, vector_parts)
        running = current if running is None else jax.tree.map(jnp.add, running, current)
    totals = grid_reduce(running[0], running[1])
    (
        grad_qkv,
        grad_out,
        grad_in,
        grad_down,
        grad_gain_one,
        grad_shift_one,
        grad_qv,
        grad_out_shift,
        grad_gain_two,
        grad_shift_two,
        grad_in_shift,
        grad_down_shift,
    ) = totals
    hidden_out = jnp.transpose(jnp.concatenate(outputs, axis=0))
    hidden_grad = jnp.transpose(jnp.concatenate(input_grads, axis=0))
    return (
        hidden_out,
        hidden_grad,
        grad_gain_one,
        grad_shift_one,
        grad_qkv,
        grad_qv,
        grad_out,
        grad_out_shift,
        grad_gain_two,
        grad_shift_two,
        grad_in,
        grad_in_shift,
        grad_down,
        grad_down_shift,
    )


def solution(mesh):
    return jax.shard_map(
        local,
        mesh=mesh,
        in_specs=(
            P("col", "row"),
            P(),
            P("col"),
            P("col"),
            P(None, "row", "col"),
            P(None, "col"),
            P("col", "row"),
            P("col"),
            P("col"),
            P("col"),
            P("row", "col"),
            P("col"),
            P("col", "row"),
            P("col"),
            P("col", "row"),
        ),
        out_specs=(
            P("col", "row"),
            P("col", "row"),
            P("col"),
            P("col"),
            P(None, "row", "col"),
            P(None, "col"),
            P("col", "row"),
            P("col"),
            P("col"),
            P("col"),
            P("row", "col"),
            P("col"),
            P("col", "row"),
            P("col"),
        ),
        check_vma=False,
    )
```

profile of v0, /device:TPU:1, one launch (start us, length us, event | category | flops | bytes accessed | tf_op | source)
XLA Modules:
  0.0 2613.4 jit_solution(1795778001554701899)
XLA Ops:
  11.0 31.0 %all-reduce.11 = (f32[1024]{0:T(1024)S(1)}, f32[1024]{0:T(1024)S(1)}, f32[1024]{0:T(1024)S(1)}, f32[1024]{0:T(1024)S(1)}) all-reduce(f32[1024]{0:T(1024)S(1)} %get-tuple-element.28, f32[1024]{0:T(1024)S(1)} %get-tuple-element.29, f32[1024]{0:T(1024)S(1)} %get-tuple-element.27, ...), channel_id=1, replica_groups=mesh['row'=4,'col'=8] {'col'}, use_global_device_ids=true, to_apply=%region_15.16 | all-reduce | flops 4096 | bytes 32768 | tf_op jit(solution)/shard_map/psum | solution.py:27
  48.7 52.6 %all-gather.23.cloned.1.call-done = bf16[1024,1280]{0,1:T(8,128)(2,1)} async-done(((bf16[1024,160]{0,1:T(8,128)(2,1)}), bf16[1024,1280]{0,1:T(8,128)(2,1)}) %all-gather.23.cloned.1.call-update) | async-done | bytes 2621456 | tf_op jit(solution)/shard_map/all_gather | solution.py:31
  105.8 51.3 %all-gather.13.cloned.1.call-done = bf16[1024,1280]{0,1:T(8,128)(2,1)} async-done(((bf16[1024,160]{0,1:T(8,128)(2,1)}), bf16[1024,1280]{0,1:T(8,128)(2,1)}) %all-gather.13.cloned.1.call-update) | async-done | bytes 2621456 | tf_op jit(solution)/shard_map/all_gather | solution.py:31
  168.1 27.8 %all_to_all.126 = bf16[8,2,30720]{2,1,0:T(2,128)(2,1)} all-to-all(bf16[8,2,30720]{2,1,0:T(2,128)(2,1)} %reshape.326), channel_id=1, replica_groups=mesh['row'=4,'col'=8] {'col'}, dimensions={0} | all-to-all | bytes 1966080 | tf_op jit(solution)/shard_map/all_to_all | solution.py:39
  236.3 31.4 %collective-permute-done.7 = bf16[256,1280]{0,1:T(8,128)(2,1)} collective-permute-done((bf16[256,1280]{0,1:T(8,128)(2,1)S(1)}, bf16[256,1280]{0,1:T(8,128)(2,1)}, u32[]{:S(2)}, u32[]{:S(2)}) %collective-permute-start.7) | collective-permute-done | bytes 655392 | tf_op jit(solution)/shard_map/ppermute | solution.py:23
  274.7 39.2 %collective-permute-done.11 = bf16[512,1280]{0,1:T(8,128)(2,1)} collective-permute-done((bf16[512,1280]{0,1:T(8,128)(2,1)}, bf16[512,1280]{0,1:T(8,128)(2,1)}, u32[]{:S(2)}, u32[]{:S(2)}) %collective-permute-start.11) | collective-permute-done | bytes 1310752 | tf_op jit(solution)/shard_map/ppermute | solution.py:23
  386.3 54.4 %all_to_all.127 = bf16[8,2,30720]{2,1,0:T(2,128)(2,1)} all-to-all(bf16[8,2,30720]{2,1,0:T(2,128)(2,1)S(1)} %reshape.330), channel_id=1, replica_groups=mesh['row'=4,'col'=8] {'col'}, dimensions={0} | all-to-all | bytes 1966080 | tf_op jit(solution)/shard_map/all_to_all | solution.py:39
  480.6 55.9 %collective-permute-done.1 = bf16[256,1280]{0,1:T(8,128)(2,1)S(1)} collective-permute-done((bf16[256,1280]{0,1:T(8,128)(2,1)S(1)}, bf16[256,1280]{0,1:T(8,128)(2,1)S(1)}, u32[]{:S(2)}, u32[]{:S(2)}) %collective-permute-start.1) | collective-permute-done | bytes 655392 | tf_op jit(solution)/shard_map/ppermute | solution.py:23
  542.6 43.8 %collective-permute-done.5 = bf16[512,1280]{0,1:T(8,128)(2,1)S(1)} collective-permute-done((bf16[512,1280]{0,1:T(8,128)(2,1)S(1)}, bf16[512,1280]{0,1:T(8,128)(2,1)S(1)}, u32[]{:S(2)}, u32[]{:S(2)}) %collective-permute-start.5) | collective-permute-done | bytes 1310752 | tf_op jit(solution)/shard_map/ppermute | solution.py:23
  652.2 99.2 %reduce-scatter.13.cloned.1.call-done = f32[1024,160]{0,1:T(8,128)} async-done(((f32[1024,1280]{0,1:T(8,128)}), f32[1024,160]{0,1:T(8,128)}) %reduce-scatter.13.cloned.1.call-update) | async-done | bytes 655376 | tf_op jit(solution)/shard_map/reduce_scatter | solution.py:35
  753.1 29.1 %all-reduce.10 = (f32[1024]{0:T(1024)S(1)}, f32[1024]{0:T(1024)S(1)}, f32[1024]{0:T(1024)S(1)}, f32[1024]{0:T(1024)S(1)}) all-reduce(f32[1024]{0:T(1024)S(1)} %get-tuple-element.96, f32[1024]{0:T(1024)S(1)} %get-tuple-element.97, f32[1024]{0:T(1024)S(1)} %get-tuple-element.39, ...), channel_id=1, replica_groups=mesh['row'=4,'col'=8] {'col'}, use_global_device_ids=true, to_apply=%region_22.23 | all-reduce | flops 4096 | bytes 32768 | tf_op jit(solution)/shard_map/psum | solution.py:27
  784.8 43.1 %all-gather.31.cloned.1.call-done = bf16[1024,1280]{0,1:T(8,128)(2,1)} async-done(((bf16[1024,160]{0,1:T(8,128)(2,1)}), bf16[1024,1280]{0,1:T(8,128)(2,1)}) %all-gather.31.cloned.1.call-update) | async-done | bytes 2621456 | tf_op jit(solution)/shard_map/all_gather | solution.py:31
  850.1 55.2 %all-gather.25.cloned.1.call-done = bf16[1024,1280]{0,1:T(8,128)(2,1)} async-done(((bf16[1024,160]{0,1:T(8,128)(2,1)}), bf16[1024,1280]{0,1:T(8,128)(2,1)}) %all-gather.25.cloned.1.call-update) | async-done | bytes 2621456 | tf_op jit(solution)/shard_map/all_gather | solution.py:31
  911.2 49.7 %all-gather.17.cloned.1.call-done = bf16[1024,1280]{0,1:T(8,128)(2,1)} async-done(((bf16[1024,160]{0,1:T(8,128)(2,1)}), bf16[1024,1280]{0,1:T(8,128)(2,1)}) %all-gather.17.cloned.1.call-update) | async-done | bytes 2621456 | tf_op jit(solution)/shard_map/all_gather | solution.py:31
  966.9 49.7 %all-gather.27.cloned.1.call-done = bf16[1024,1280]{0,1:T(8,128)(2,1)} async-done(((bf16[1024,160]{0,1:T(8,128)(2,1)}), bf16[1024,1280]{0,1:T(8,128)(2,1)}) %all-gather.27.cloned.1.call-update) | async-done | bytes 2621456 | tf_op jit(solution)/shard_map/all_gather | solution.py:31
  1065.0 79.3 %reduce-scatter.25.cloned.1.call-done = f32[1024,160]{0,1:T(8,128)} async-done(((f32[1024,1280]{0,1:T(8,128)}), f32[1024,160]{0,1:T(8,128)}) %reduce-scatter.25.cloned.1.call-update) | async-done | bytes 655376 | tf_op jit(solution)/shard_map/reduce_scatter | solution.py:35
  1144.3 106.2 %reduce-scatter.21.cloned.1.call-done = f32[1024,160]{0,1:T(8,128)} async-done(((f32[1024,1280]{0,1:T(8,128)}), f32[1024,160]{0,1:T(8,128)}) %reduce-scatter.21.cloned.1.call-update) | async-done | bytes 655376 | tf_op jit(solution)/shard_map/reduce_scatter | solution.py:35
  1250.5 106.1 %reduce-scatter.19.cloned.1.call-done = f32[1024,160]{0,1:T(8,128)} async-done(((f32[1024,1280]{0,1:T(8,128)}), f32[1024,160]{0,1:T(8,128)}) %reduce-scatter.19.cloned.1.call-update) | async-done | bytes 655376 | tf_op jit(solution)/shard_map/reduce_scatter | solution.py:35
  1356.6 106.1 %reduce-scatter.15.cloned.1.call-done = f32[1024,160]{0,1:T(8,128)} async-done(((f32[1024,1280]{0,1:T(8,128)}), f32[1024,160]{0,1:T(8,128)}) %reduce-scatter.15.cloned.1.call-update) | async-done | bytes 655376 | tf_op jit(solution)/shard_map/reduce_scatter | solution.py:35
  1466.6 29.1 %all-reduce.9 = (f32[1024]{0:T(1024)S(1)}, f32[1024]{0:T(1024)S(1)}, f32[1024]{0:T(1024)S(1)}, f32[1024]{0:T(1024)S(1)}) all-reduce(f32[1024]{0:T(1024)S(1)} %get-tuple-element.19, f32[1024]{0:T(1024)S(1)} %get-tuple-element.33, f32[1024]{0:T(1024)S(1)} %get-tuple-element.135, ...), channel_id=1, replica_groups=mesh['row'=4,'col'=8] {'col'}, use_global_device_ids=true, to_apply=%region_39.40 | all-reduce | flops 4096 | bytes 32768 | tf_op jit(solution)/shard_map/psum | solution.py:27
  1498.9 57.2 %all-gather.29.cloned.1.call-done = bf16[1024,1280]{0,1:T(8,128)(2,1)} async-done(((bf16[1024,160]{0,1:T(8,128)(2,1)}), bf16[1024,1280]{0,1:T(8,128)(2,1)}) %all-gather.29.cloned.1.call-update) | async-done | bytes 2621456 | tf_op jit(solution)/shard_map/all_gather | solution.py:31
  1615.3 138.4 %all-gather.33.cloned.1.call-done = bf16[1024,1280]{0,1:T(8,128)(2,1)} async-done(((bf16[1024,160]{0,1:T(8,128)(2,1)}), bf16[1024,1280]{0,1:T(8,128)(2,1)}) %all-gather.33.cloned.1.call-update) | async-done | bytes 2621456 | tf_op jit(solution)/shard_map/all_gather | solution.py:31
  1764.6 94.8 %all-to-all-start.6 = ((bf16[8,2,10240]{2,1,0:T(2,128)(2,1)}), bf16[8,2,10240]{2,1,0:T(2,128)(2,1)S(1)}, u32[]{:S(2)}, u32[]{:S(2)}) async-start(bf16[8,2,10240]{2,1,0:T(2,128)(2,1)} %reshape.334), calls=%async_computation.13 | async-start | bytes 655360 | tf_op jit(solution)/shard_map/all_to_all | solution.py:39
  1960.7 115.7 %all-to-all-done.5 = bf16[3,128,1280]{1,0,2:T(4,128)(2,1)S(1)} async-done(((bf16[3,128,1280]{1,0,2:T(4,128)(2,1)}), bf16[3,128,1280]{1,0,2:T(4,128)(2,1)S(1)}, u32[]{:S(2)}, u32[]{:S(2)}) %all-to-all-start.5) | async-done | bytes 983072 | tf_op jit(solution)/shard_map/all_to_all | solution.py:43
  2104.7 144.9 %collective-permute-done.18 = f32[512,1280]{1,0:T(8,128)} collective-permute-done((f32[512,1280]{1,0:T(8,128)}, f32[512,1280]{1,0:T(8,128)}, u32[]{:S(2)}, u32[]{:S(2)}) %collective-permute-start.18) | collective-permute-done | bytes 2621472 | tf_op jit(solution)/shard_map/ppermute | solution.py:23
  2256.2 38.0 %collective-permute-done.19 = f32[256,1280]{1,0:T(8,128)S(1)} collective-permute-done((f32[256,1280]{1,0:T(8,128)S(1)}, f32[256,1280]{1,0:T(8,128)S(1)}, u32[]{:S(2)}, u32[]{:S(2)}) %collective-permute-start.19) | collective-permute-done | bytes 1310752 | tf_op jit(solution)/shard_map/ppermute | solution.py:23
  2314.4 33.5 %all_to_all.129 = bf16[3,128,1280]{1,0,2:T(4,128)(2,1)S(1)} all-to-all(bf16[3,128,1280]{1,0,2:T(4,128)(2,1)S(1)} %copy.172), channel_id=1, replica_groups=mesh['row'=4,'col'=8] {'col'}, dimensions={2} | all-to-all | bytes 1966080 | tf_op jit(solution)/shard_map/all_to_all | solution.py:43
  2396.8 59.1 %reduce-scatter.27.cloned.1.call-done = f32[1024,160]{0,1:T(8,128)} async-done(((f32[1024,1280]{0,1:T(8,128)}), f32[1024,160]{0,1:T(8,128)}) %reduce-scatter.27.cloned.1.call-update) | async-done | bytes 655376 | tf_op jit(solution)/shard_map/reduce_scatter | solution.py:35
  2470.3 28.7 %all-reduce.8 = (f32[1024]{0:T(1024)S(1)}, f32[1024]{0:T(1024)S(1)}, f32[1024]{0:T(1024)S(1)}, f32[1024]{0:T(1024)S(1)}) all-reduce(f32[1024]{0:T(1024)S(1)} %get-tuple-element.22, f32[1024]{0:T(1024)S(1)} %get-tuple-element.30, f32[1024]{0:T(1024)S(1)} %get-tuple-element.17, ...), channel_id=1, replica_groups=mesh['row'=4,'col'=8] {'col'}, use_global_device_ids=true, to_apply=%region_45.46 | all-reduce | flops 4096 | bytes 32768 | tf_op jit(solution)/shard_map/psum | solution.py:27
  2510.2 29.0 %reduce-scatter.33.cloned.1.call-done = f32[1,320,640]{2,1,0:T(8,128)} async-done(((f32[4,320,640]{2,1,0:T(8,128)}), f32[1,320,640]{2,1,0:T(8,128)}) %reduce-scatter.33.cloned.1.call-update) | async-done | bytes 819216 | tf_op jit(solution)/shard_map/reduce_scatter | solution.py:261
  2539.3 27.6 %reduce-scatter.31.cloned.1.call-done = f32[1,160,320]{2,1,0:T(8,128)} async-done(((f32[4,160,320]{2,1,0:T(8,128)}), f32[1,160,320]{2,1,0:T(8,128)}) %reduce-scatter.31.cloned.1.call-update) | async-done | bytes 204816 | tf_op jit(solution)/shard_map/reduce_scatter | solution.py:260
  2566.8 39.8 %reduce-scatter.29.cloned.1.call-done = f32[1,3,320,160]{2,3,1,0:T(8,128)} async-done(((f32[4,3,320,160]{2,3,1,0:T(8,128)}), f32[1,3,320,160]{2,3,1,0:T(8,128)}) %reduce-scatter.29.cloned.1.call-update) | async-done | bytes 614416 | tf_op jit(solution)/shard_map/reduce_scatter | solution.py:259
  (498 shorter events, 650.6 us)
Async XLA Ops:
  9.5 91.8 %all-gather.23.cloned.1.call-start = ((), (), s32[]{:S(2)}) async-start(), calls=%async_computation.27 | async-start | bytes 2949120 | tf_op jit(solution)/shard_map/all_gather | solution.py:31
  43.9 113.2 %all-gather.13.cloned.1.call-start = ((), (), s32[]{:S(2)}) async-start(), calls=%async_computation.20 | async-start | bytes 2949120 | tf_op jit(solution)/shard_map/all_gather | solution.py:31
  226.5 87.3 %collective-permute-start.11 = (bf16[512,1280]{0,1:T(8,128)(2,1)}, bf16[512,1280]{0,1:T(8,128)(2,1)}, u32[]{:S(2)}, u32[]{:S(2)}) collective-permute-start(bf16[512,1280]{0,1:T(8,128)(2,1)} %maximum_select_fusion.10), channel_id=1, source_target_pairs={{0,4},{4,0},{1,5},{5,1},{2,6},{6,2},{3,7},{7,3},{8,12},{12,8},{9,1... | collective-permute-start | bytes 3932168 | tf_op jit(solution)/shard_map/ppermute | solution.py:23
  366.2 285.9 %reduce-scatter.17.cloned.1.call-start = ((), (), s32[]{:S(2)}) async-start(), calls=%async_computation.28 | async-start | bytes 5898240 | tf_op jit(solution)/shard_map/reduce_scatter | solution.py:35
  378.6 372.8 %reduce-scatter.13.cloned.1.call-start = ((), (), s32[]{:S(2)}) async-start(), calls=%async_computation.22 | async-start | bytes 5898240 | tf_op jit(solution)/shard_map/reduce_scatter | solution.py:35
  477.5 108.9 %collective-permute-start.5 = (bf16[512,1280]{0,1:T(8,128)(2,1)S(1)}, bf16[512,1280]{0,1:T(8,128)(2,1)S(1)}, u32[]{:S(2)}, u32[]{:S(2)}) collective-permute-start(bf16[512,1280]{0,1:T(8,128)(2,1)S(1)} %maximum_select_fusion.6), channel_id=1, source_target_pairs={{0,4},{4,0},{1,5},{5,1},{2,6},{6,2},{3,7},{7,3},{8,12},{12,8},{9,1... | collective-permute-start | bytes 3932168 | tf_op jit(solution)/shard_map/ppermute | solution.py:23
  536.9 77.6 %collective-permute-start.2 = (bf16[512,1280]{0,1:T(8,128)(2,1)S(1)}, bf16[512,1280]{0,1:T(8,128)(2,1)S(1)}, u32[]{:S(2)}, u32[]{:S(2)}) collective-permute-start(bf16[512,1280]{0,1:T(8,128)(2,1)S(1)} %maximum_select_fusion.4), channel_id=1, source_target_pairs={{0,4},{4,0},{1,5},{5,1},{2,6},{6,2},{3,7},{7,3},{8,12},{12,8},{9,1... | collective-permute-start | bytes 3932168 | tf_op jit(solution)/shard_map/ppermute | solution.py:23
  649.1 135.7 %all-gather.21.cloned.1.call-start = ((), (), s32[]{:S(2)}) async-start(), calls=%async_computation.25 | async-start | bytes 2048000 | tf_op jit(solution)/shard_map/all_gather | solution.py:300
  649.7 178.2 %all-gather.31.cloned.1.call-start = ((), (), s32[]{:S(2)}) async-start(), calls=%async_computation.35 | async-start | bytes 2949120 | tf_op jit(solution)/shard_map/all_gather | solution.py:31
  651.4 198.7 %all-gather.19.cloned.1.call-start = ((), (), s32[]{:S(2)}) async-start(), calls=%async_computation.24 | async-start | bytes 2048000 | tf_op jit(solution)/shard_map/all_gather | solution.py:299
  652.1 253.1 %all-gather.25.cloned.1.call-start = ((), (), s32[]{:S(2)}) async-start(), calls=%async_computation.29 | async-start | bytes 2949120 | tf_op jit(solution)/shard_map/all_gather | solution.py:31
  783.4 177.4 %all-gather.17.cloned.1.call-start = ((), (), s32[]{:S(2)}) async-start(), calls=%async_computation.23 | async-start | bytes 2949120 | tf_op jit(solution)/shard_map/all_gather | solution.py:31
  784.0 232.6 %all-gather.27.cloned.1.call-start = ((), (), s32[]{:S(2)}) async-start(), calls=%async_computation.31 | async-start | bytes 2949120 | tf_op jit(solution)/shard_map/all_gather | solution.py:31
  784.8 359.5 %reduce-scatter.25.cloned.1.call-start = ((), (), s32[]{:S(2)}) async-start(), calls=%async_computation.36 | async-start | bytes 5898240 | tf_op jit(solution)/shard_map/reduce_scatter | solution.py:35
  1041.3 209.2 %reduce-scatter.21.cloned.1.call-start = ((), (), s32[]{:S(2)}) async-start(), calls=%async_computation.32 | async-start | bytes 5898240 | tf_op jit(solution)/shard_map/reduce_scatter | solution.py:35
  1047.4 309.1 %reduce-scatter.19.cloned.1.call-start = ((), (), s32[]{:S(2)}) async-start(), calls=%async_computation.30 | async-start | bytes 5898240 | tf_op jit(solution)/shard_map/reduce_scatter | solution.py:35
  1058.4 404.3 %reduce-scatter.15.cloned.1.call-start = ((), (), s32[]{:S(2)}) async-start(), calls=%async_computation.26 | async-start | bytes 5898240 | tf_op jit(solution)/shard_map/reduce_scatter | solution.py:35
  1064.5 491.6 %all-gather.29.cloned.1.call-start = ((), (), s32[]{:S(2)}) async-start(), calls=%async_computation.33 | async-start | bytes 2949120 | tf_op jit(solution)/shard_map/all_gather | solution.py:31
  1571.1 182.5 %all-gather.33.cloned.1.call-start = ((), (), s32[]{:S(2)}) async-start(), calls=%async_computation.37 | async-start | bytes 2949120 | tf_op jit(solution)/shard_map/all_gather | solution.py:31
  1591.3 270.1 %collective-permute-start.15 = (f32[512,1280]{1,0:T(8,128)}, f32[512,1280]{1,0:T(8,128)}, u32[]{:S(2)}, u32[]{:S(2)}) collective-permute-start(f32[512,1280]{1,0:T(8,128)} %copy.158), channel_id=1, source_target_pairs={{0,4},{4,0},{1,5},{5,1},{2,6},{6,2},{3,7},{7,3},{8,12},{12,8},{9,1... | collective-permute-start | bytes 7864328 | tf_op jit(solution)/shard_map/ppermute | solution.py:23
  1615.2 262.0 %collective-permute-start.12 = (f32[512,1280]{1,0:T(8,128)}, f32[512,1280]{1,0:T(8,128)}, u32[]{:S(2)}, u32[]{:S(2)}) collective-permute-start(f32[512,1280]{1,0:T(8,128)} %copy.156), channel_id=1, source_target_pairs={{0,4},{4,0},{1,5},{5,1},{2,6},{6,2},{3,7},{7,3},{8,12},{12,8},{9,1... | collective-permute-start | bytes 7864328 | tf_op jit(solution)/shard_map/ppermute | solution.py:23
  1764.6 104.9 %all-to-all-start.6 = ((bf16[8,2,10240]{2,1,0:T(2,128)(2,1)}), bf16[8,2,10240]{2,1,0:T(2,128)(2,1)S(1)}, u32[]{:S(2)}, u32[]{:S(2)}) async-start(bf16[8,2,10240]{2,1,0:T(2,128)(2,1)} %reshape.334), calls=%async_computation.13 | async-start | bytes 655360 | tf_op jit(solution)/shard_map/all_to_all | solution.py:39
  1932.3 162.7 %collective-permute-start.21 = (f32[512,1280]{1,0:T(8,128)}, f32[512,1280]{1,0:T(8,128)}, u32[]{:S(2)}, u32[]{:S(2)}) collective-permute-start(f32[512,1280]{1,0:T(8,128)} %copy.169), channel_id=1, source_target_pairs={{0,4},{4,0},{1,5},{5,1},{2,6},{6,2},{3,7},{7,3},{8,12},{12,8},{9,1... | collective-permute-start | bytes 7864328 | tf_op jit(solution)/shard_map/ppermute | solution.py:23
  1943.9 132.5 %all-to-all-start.5 = ((bf16[3,128,1280]{1,0,2:T(4,128)(2,1)}), bf16[3,128,1280]{1,0,2:T(4,128)(2,1)S(1)}, u32[]{:S(2)}, u32[]{:S(2)}) async-start(bf16[3,128,1280]{1,0,2:T(4,128)(2,1)} %copy.161), calls=%async_computation.10 | async-start | bytes 2621440 | tf_op jit(solution)/shard_map/all_to_all | solution.py:43
  1947.5 449.2 %reduce-scatter.23.cloned.1.call-start = ((), (), s32[]{:S(2)}) async-start(), calls=%async_computation.34 | async-start | bytes 5898240 | tf_op jit(solution)/shard_map/reduce_scatter | solution.py:35
  2082.2 373.6 %reduce-scatter.27.cloned.1.call-start = ((), (), s32[]{:S(2)}) async-start(), calls=%async_computation.38 | async-start | bytes 5898240 | tf_op jit(solution)/shard_map/reduce_scatter | solution.py:35
  2092.9 156.7 %collective-permute-start.18 = (f32[512,1280]{1,0:T(8,128)}, f32[512,1280]{1,0:T(8,128)}, u32[]{:S(2)}, u32[]{:S(2)}) collective-permute-start(f32[512,1280]{1,0:T(8,128)} %copy.167), channel_id=1, source_target_pairs={{0,4},{4,0},{1,5},{5,1},{2,6},{6,2},{3,7},{7,3},{8,12},{12,8},{9,1... | collective-permute-start | bytes 7864328 | tf_op jit(solution)/shard_map/ppermute | solution.py:23
  2099.2 153.6 %collective-permute-start.22 = (f32[256,1280]{1,0:T(8,128)}, f32[256,1280]{1,0:T(8,128)}, u32[]{:S(2)}, u32[]{:S(2)}) collective-permute-start(f32[256,1280]{1,0:T(8,128)} %slice_select_fusion.8), channel_id=1, source_target_pairs={{0,2},{2,0},{1,3},{3,1},{4,6},{6,4},{5,7},{7,5},{8,10},{10,8},{9,1... | collective-permute-start | bytes 3932168 | tf_op jit(solution)/shard_map/ppermute | solution.py:23
  2353.7 156.5 %reduce-scatter.35.cloned.1.call-start = ((), (), s32[]{:S(2)}) async-start(), calls=%async_computation.42 | async-start | bytes 4096000 | tf_op jit(solution)/shard_map/reduce_scatter | solution.py:262
  2364.0 175.3 %reduce-scatter.33.cloned.1.call-start = ((), (), s32[]{:S(2)}) async-start(), calls=%async_computation.41 | async-start | bytes 4096000 | tf_op jit(solution)/shard_map/reduce_scatter | solution.py:261
  2372.5 194.3 %reduce-scatter.31.cloned.1.call-start = ((), (), s32[]{:S(2)}) async-start(), calls=%async_computation.40 | async-start | bytes 1228800 | tf_op jit(solution)/shard_map/reduce_scatter | solution.py:260
  2381.0 225.7 %reduce-scatter.29.cloned.1.call-start = ((), (), s32[]{:S(2)}) async-start(), calls=%async_computation.39 | async-start | bytes 3686400 | tf_op jit(solution)/shard_map/reduce_scatter | solution.py:259
  (111 other events, 3498.4 us)
Sparse Core Ops, SparseCore 0:
  10.2 27.9 all-gather.14
  44.0 57.2 all-gather.22
  104.0 52.9 all-gather.12
  378.7 163.4 reduce-scatter.16
  649.2 102.1 reduce-scatter.12
  752.8 20.3 all-gather.20
  775.4 52.4 all-gather.30
  829.5 20.5 all-gather.18
  852.8 52.3 all-gather.24
  907.9 52.9 all-gather.16
  963.6 52.9 all-gather.26
  1041.4 102.7 reduce-scatter.24
  1147.9 102.5 reduce-scatter.20
  1253.9 102.5 reduce-scatter.18
  1360.0 102.5 reduce-scatter.14
  1499.0 57.0 all-gather.28
  1574.4 179.2 all-gather.32
  2082.3 190.3 reduce-scatter.22
  2353.9 101.9 reduce-scatter.26
  2458.8 38.5 reduce-scatter.34
  2500.5 38.6 reduce-scatter.32
  2542.4 24.3 reduce-scatter.30
  2570.0 36.6 reduce-scatter.28
where the time goes:
time: 2620 us; the launch traced here: 2610 us
  waiting for transfers between devices  1790 us (68%)
  blocking collectives  267 us (10%)
  matrix products  156 us (6%)
  starting transfers between devices  139 us (5%)
  local copies, waits for them, and re-layouts  129 us (5%)
  other arithmetic  120 us (5%)
    reduce_scatter x8, waiting for transfers between devices, narrow(): return lax.psum_scatter(values, 'col', scatter_dimension=1, tiled=True)  556 us
    all_gather x8, waiting for transfers between devices, widen(): return lax.all_gather(values, 'col', axis=1, tiled=True)  497 us
    ppermute x24, waiting for transfers between devices, partner(): return lax.ppermute(block, axis, route)  494 us
    psum x4, blocking collectives, row_totals(): return lax.psum((first_sum, second_sum), 'col')  118 us
    all_to_all x2, waiting for transfers between devices, to_columns(): lax.all_to_all(stacked, 'col', split_axis=2, concat_axis=1, tiled=True)  116 us
    all_to_all x2, starting transfers between devices, to_clips(): lax.all_to_all(stacked, 'col', split_axis=1, concat_axis=2, tiled=True)  98.8 us
    all_to_all x2, blocking collectives, to_clips(): lax.all_to_all(stacked, 'col', split_axis=1, concat_axis=2, tiled=True)  82.1 us
  transfers between devices with their start and end apart: 51, of which 37 were waited for; matrix products, arithmetic and copies ran while one was open for 12% of the time, Pallas kernels for 0%

commit v1 on v0

--- a/solution.py
+++ b/solution.py
@@ -1,6 +1,10 @@
+import functools
+
 import jax
 import jax.numpy as jnp
 from jax import lax
+from jax.experimental import pallas as pl
+from jax.experimental.pallas import tpu as pltpu
 from jax.sharding import PartitionSpec as P
 
 HEADS = 16
@@ -352,9 +356,1103 @@
     )
 
 
+CLIP = 1024
+FF = 5120
+OWN = D // 4
+UNITS = FF // 4
+HALF = D // 2
+BLOCK = 256
+STEPS = CLIP // BLOCK
+BF = jnp.bfloat16
+F32 = jnp.float32
+
+
+def swap_core(values):
+    return lax.ppermute(values, "row", [(i, i ^ 1) for i in range(4)])
+
+
+def swap_y(values):
+    return lax.ppermute(values, "row", [(i, i ^ 2) for i in range(4)])
+
+
+def swap_x(values):
+    return lax.ppermute(values, "col", [(i, i ^ 1) for i in range(8)])
+
+
+def swap_zl(values):
+    return lax.ppermute(values, "col", [(i, i ^ 2) for i in range(8)])
+
+
+def swap_zh(values):
+    return lax.ppermute(values, "col", [(i, i ^ 4) for i in range(8)])
+
+
+def pick(values, index, axis=0):
+    return lax.dynamic_index_in_dim(values, index, axis, keepdims=False)
+
+
+def mm(left, right, left_dim, right_dim):
+    return lax.dot_general(
+        left, right, (((left_dim,), (right_dim,)), ((), ())), preferred_element_type=F32
+    )
+
+
+def shaped(dims, kind=BF):
+    return jax.ShapeDtypeStruct(dims, kind)
+
+
+def spots_spec():
+    return pl.BlockSpec(memory_space=pltpu.SMEM)
+
+
+def fixed(array):
+    rank = len(array.shape)
+    return pl.BlockSpec(array.shape, lambda i: (0,) * rank)
+
+
+def tokens_spec(dims):
+    lead = tuple(dims[:-1])
+    return pl.BlockSpec(lead + (BLOCK,), lambda i: (0,) * len(lead) + (i,))
+
+
+def cost(flops, moved):
+    return pl.CostEstimate(flops=1, transcendentals=0, bytes_accessed=1)
+
+
+def attend_kernel(len_ref, q_ref, k_ref, v_ref, out_ref, lse_ref):
+    scores = mm(k_ref[...], q_ref[...], 0, 0) * (HEAD_DIM**-0.5)
+    live = lax.broadcasted_iota(jnp.int32, scores.shape, 0) < len_ref[0]
+    scores = jnp.where(live, scores, -1e30)
+    top = jnp.max(scores, axis=0, keepdims=True)
+    weights = jnp.exp(scores - top)
+    total = jnp.sum(weights, axis=0, keepdims=True)
+    prob_low = (weights * (1.0 / total)).astype(BF)
+    out_ref[...] = mm(v_ref[...], prob_low, 1, 0).astype(BF)
+    lse_ref[...] = top + jnp.log(total)
+
+
+def head_specs(block):
+    return [
+        pl.BlockSpec((None, None, HEAD_DIM, block), lambda h, i, n: (h, 0, 0, i)),
+        pl.BlockSpec((None, None, HEAD_DIM, CLIP), lambda h, i, n: (h, 1, 0, 0)),
+        pl.BlockSpec((None, HEAD_DIM, CLIP), lambda h, i, n: (h, 0, 0)),
+    ]
+
+
+def attend_clip(qk, values, clip_len, block):
+    return pl.pallas_call(
+        attend_kernel,
+        grid_spec=pltpu.PrefetchScalarGridSpec(
+            num_scalar_prefetch=1,
+            grid=(4, CLIP // block),
+            in_specs=head_specs(block),
+            out_specs=[
+                pl.BlockSpec((None, HEAD_DIM, block), lambda h, i, n: (h, 0, i)),
+                pl.BlockSpec((None, 1, block), lambda h, i, n: (h, 0, i)),
+            ],
+        ),
+        out_shape=[shaped((4, HEAD_DIM, CLIP)), shaped((4, 1, CLIP), F32)],
+        cost_estimate=cost(16 * CLIP * CLIP * HEAD_DIM, 16 * HEAD_DIM * CLIP * 2),
+        name="attend_clip",
+    )(clip_len, qk, qk, values)
+
+
+def attend_back_kernel(
+    len_ref, q_ref, k_ref, v_ref, lse_ref, grad_ref, gqk_ref, gv_ref, ksum_ref, vsum_ref
+):
+    step = pl.program_id(1)
+    scale = HEAD_DIM**-0.5
+    queries, keys, values, grad = q_ref[...], k_ref[...], v_ref[...], grad_ref[...]
+    block = queries.shape[1]
+    scores = mm(keys, queries, 0, 0) * scale
+    live = lax.broadcasted_iota(jnp.int32, scores.shape, 0) < len_ref[0]
+    scores = jnp.where(live, scores, -1e30)
+    probs = jnp.exp(scores - lse_ref[...])
+    grad_probs = mm(values, grad, 0, 0)
+    row_dot = jnp.sum(probs * grad_probs, axis=0, keepdims=True)
+    score_low = (probs * (grad_probs - row_dot)).astype(BF)
+    grad_query = mm(keys, score_low, 1, 0) * scale
+    grad_key = mm(queries, score_low, 1, 1)
+    grad_value = mm(grad, probs.astype(BF), 1, 1)
+    start = pl.multiple_of(step * block, block)
+    gqk_ref[0, :, pl.ds(start, block)] = grad_query.astype(BF)
+
+    @pl.when(step == 0)
+    def _():
+        ksum_ref[...] = grad_key
+        vsum_ref[...] = grad_value
+
+    @pl.when(step > 0)
+    def _():
+        ksum_ref[...] += grad_key
+        vsum_ref[...] += grad_value
+
+    @pl.when(step == pl.num_programs(1) - 1)
+    def _():
+        gqk_ref[1] = (ksum_ref[...] * scale).astype(BF)
+        gv_ref[...] = vsum_ref[...].astype(BF)
+
+
+def attend_clip_back(qk, values, log_sum, grad_attended, clip_len, block):
+    return pl.pallas_call(
+        attend_back_kernel,
+        grid_spec=pltpu.PrefetchScalarGridSpec(
+            num_scalar_prefetch=1,
+            grid=(4, CLIP // block),
+            in_specs=head_specs(block)
+            + [
+                pl.BlockSpec((None, 1, block), lambda h, i, n: (h, 0, i)),
+                pl.BlockSpec((None, HEAD_DIM, block), lambda h, i, n: (h, 0, i)),
+            ],
+            out_specs=[
+                pl.BlockSpec((None, 2, HEAD_DIM, CLIP), lambda h, i, n: (h, 0, 0, 0)),
+                pl.BlockSpec((None, HEAD_DIM, CLIP), lambda h, i, n: (h, 0, 0)),
+            ],
+            scratch_shapes=[pltpu.VMEM((HEAD_DIM, CLIP), F32)] * 2,
+        ),
+        out_shape=[shaped((4, 2, HEAD_DIM, CLIP)), shaped((4, HEAD_DIM, CLIP))],
+        cost_estimate=cost(40 * CLIP * CLIP * HEAD_DIM, 32 * HEAD_DIM * CLIP * 2),
+        name="attend_clip_back",
+    )(clip_len, qk, qk, values, log_sum, grad_attended)
+
+
+WIDE = 384
+
+
+def order_hot(core):
+    place = lax.broadcasted_iota(jnp.int32, (OWN, OWN), 1)
+    stored = lax.broadcasted_iota(jnp.int32, (OWN, OWN), 0)
+    hot = jnp.zeros((OWN, OWN), jnp.bool_)
+    for chunk in range(4):
+        source = (2 * (chunk >> 1) + (core ^ (chunk & 1))) * HEAD_DIM
+        inside = (place >= chunk * HEAD_DIM) & (place < (chunk + 1) * HEAD_DIM)
+        hot = hot | (inside & (stored - source == place - chunk * HEAD_DIM))
+    return jnp.where(hot, 1.0, 0.0).astype(BF)
+
+
+def whole():
+    return pl.BlockSpec(memory_space=pltpu.VMEM)
+
+
+def prepare_kernel(spots_ref, qkv_ref, out_ref, in_ref, down_ref, kept_ref, sent_ref):
+    c = spots_ref[0]
+    for ref, core in ((kept_ref, c), (sent_ref, 1 - c)):
+        hot = order_hot(core)
+
+        def half(value, count):
+            return jnp.where(core == 0, value[:count], value[count:])
+
+        for s in range(3):
+            value = half(mm(qkv_ref[s], hot, 1, 0), HEAD_DIM)
+            ref[s * HEAD_DIM : (s + 1) * HEAD_DIM, :OWN] = value.astype(BF)
+        value = half(mm(out_ref[...], hot, 1, 0), HEAD_DIM)
+        ref[3 * HEAD_DIM : OWN, :OWN] = value.astype(BF)
+        ref[OWN : 2 * OWN, :OWN] = half(mm(in_ref[...], hot, 0, 0), OWN).astype(BF)
+        ref[2 * OWN :, :OWN] = half(mm(down_ref[...], hot, 0, 0), OWN).astype(BF)
+        ref[:, OWN:] = jnp.zeros((3 * OWN, WIDE - OWN), BF)
+
+
+def prepare(spots, qkv_turned, out_weight, in_weight, down_turned):
+    return pl.pallas_call(
+        prepare_kernel,
+        in_specs=[spots_spec()] + [whole()] * 4,
+        out_specs=[whole()] * 2,
+        out_shape=[shaped((3 * OWN, WIDE))] * 2,
+        cost_estimate=cost(8 * 3 * OWN * OWN * OWN, 4 * 3 * OWN * OWN * 2),
+        name="prepare_weights",
+    )(spots, qkv_turned, out_weight, in_weight, down_turned)
+
+
+def lanes_kernel(spots_ref, kept_ref, got_ref, *out_refs):
+    def write(near_ref, far_ref):
+        start = 0
+        for ref in out_refs:
+            rows = slice(start, start + ref.shape[0])
+            ref[:, :OWN] = near_ref[rows, :OWN]
+            ref[:, OWN:] = far_ref[rows, :OWN]
+            start += ref.shape[0]
+
+    @pl.when(spots_ref[1] == 1)
+    def _():
+        write(kept_ref, got_ref)
+
+    @pl.when(spots_ref[1] == 0)
+    def _():
+        write(got_ref, kept_ref)
+
+
+def join_lanes(spots, kept, got):
+    return pl.pallas_call(
+        lanes_kernel,
+        in_specs=[spots_spec(), whole(), whole()],
+        out_specs=[whole()] * 4,
+        out_shape=[shaped((n, HALF)) for n in (OWN // 2, OWN // 2, OWN, OWN)],
+        cost_estimate=cost(0, 4 * 3 * OWN * OWN * 2),
+        name="join_lanes",
+    )(spots, kept, got)
+
+
+def two_terms(value):
+    high = value.astype(BF)
+    return high, (value - high.astype(F32)).astype(BF)
+
+
+def store_ff_kernel(spots_ref, up_ref, down_ref, kept_ref, sent_ref):
+    hot = order_hot(spots_ref[0])
+    is_near = spots_ref[1] == 1
+    for place, total_ref in ((0, up_ref), (1, down_ref)):
+        near, far = total_ref[:, :OWN], total_ref[:, OWN:]
+        lanes = slice(place * OWN, (place + 1) * OWN)
+        for ref, value in (
+            (kept_ref, jnp.where(is_near, near, far)),
+            (sent_ref, jnp.where(is_near, far, near)),
+        ):
+            high, rest = two_terms(value)
+            ref[:, lanes] = mm(hot, high, 1, 1) + mm(hot, rest, 1, 1)
+
+
+def store_ff(spots, up_total, down_total):
+    return pl.pallas_call(
+        store_ff_kernel,
+        in_specs=[spots_spec()] + [whole()] * 2,
+        out_specs=[whole()] * 2,
+        out_shape=[shaped((OWN, HALF), F32)] * 2,
+        cost_estimate=cost(16 * OWN * OWN * OWN, 16 * OWN * OWN * 4),
+        name="store_ff",
+    )(spots, up_total, down_total)
+
+
+def join_ff_kernel(spots_ref, kept_ref, got_ref, up_ref, down_ref):
+    def write(first_ref, second_ref):
+        for place, ref in ((0, up_ref), (1, down_ref)):
+            lanes = slice(place * OWN, (place + 1) * OWN)
+            ref[:, :OWN] = first_ref[:, lanes]
+            ref[:, OWN:] = second_ref[:, lanes]
+
+    @pl.when(spots_ref[0] == 0)
+    def _():
+        write(kept_ref, got_ref)
+
+    @pl.when(spots_ref[0] == 1)
+    def _():
+        write(got_ref, kept_ref)
+
+
+def join_ff(spots, kept, got):
+    return pl.pallas_call(
+        join_ff_kernel,
+        in_specs=[spots_spec()] + [whole()] * 2,
+        out_specs=[whole()] * 2,
+        out_shape=[shaped((OWN, HALF), F32)] * 2,
+        cost_estimate=cost(0, 16 * OWN * OWN * 4),
+        name="join_ff",
+    )(spots, kept, got)
+
+
+def store_qkvo_kernel(spots_ref, qk_ref, vo_ref, kept_ref, sent_ref):
+    hot = order_hot(spots_ref[0])
+    is_near = spots_ref[1] == 1
+    for place, total_ref in ((0, qk_ref), (1, vo_ref)):
+        near, far = total_ref[:, :OWN], total_ref[:, OWN:]
+        rows = slice(place * 2 * HEAD_DIM, (place + 1) * 2 * HEAD_DIM)
+        for ref, value in (
+            (kept_ref, jnp.where(is_near, near, far)),
+            (sent_ref, jnp.where(is_near, far, near)),
+        ):
+            high, rest = two_terms(value)
+            ref[rows, :OWN] = mm(high, hot, 1, 1) + mm(rest, hot, 1, 1)
+    kept_ref[:, OWN:] = jnp.zeros((OWN, WIDE - OWN), F32)
+    sent_ref[:, OWN:] = jnp.zeros((OWN, WIDE - OWN), F32)
+
+
+def store_qkvo(spots, qk_total, vo_total):
+    return pl.pallas_call(
+        store_qkvo_kernel,
+        in_specs=[spots_spec()] + [whole()] * 2,
+        out_specs=[whole()] * 2,
+        out_shape=[shaped((OWN, WIDE), F32)] * 2,
+        cost_estimate=cost(8 * OWN * OWN * OWN, 16 * OWN * OWN * 4),
+        name="store_qkvo",
+    )(spots, qk_total, vo_total)
+
+
+def join_qkvo_kernel(spots_ref, kept_ref, got_ref, qkv_ref, out_ref):
+    def write(first_ref, second_ref):
+        for place, ref in ((0, first_ref), (1, second_ref)):
+            rows = slice(place * HEAD_DIM, (place + 1) * HEAD_DIM)
+            for s in range(3):
+                qkv_ref[s, rows] = ref[s * HEAD_DIM : (s + 1) * HEAD_DIM, :OWN]
+            out_ref[rows] = ref[3 * HEAD_DIM : 4 * HEAD_DIM, :OWN]
+
+    @pl.when(spots_ref[0] == 0)
+    def _():
+        write(kept_ref, got_ref)
+
+    @pl.when(spots_ref[0] == 1)
+    def _():
+        write(got_ref, kept_ref)
+
+
+def join_qkvo(spots, kept, got):
+    return pl.pallas_call(
+        join_qkvo_kernel,
+        in_specs=[spots_spec()] + [whole()] * 2,
+        out_specs=[whole()] * 2,
+        out_shape=[shaped((3, 2 * HEAD_DIM, OWN), F32), shaped((2 * HEAD_DIM, OWN), F32)],
+        cost_estimate=cost(0, 8 * OWN * OWN * 4),
+        name="join_qkvo",
+    )(spots, kept, got)
+
+
+TAIL = 8
+
+
+def split_kernel(spots_ref, hid_ref, cot_ref, hk_ref, hs_ref, ck_ref, cs_ref):
+    c = spots_ref[0]
+    data, tails, cots = [], [], []
+    for half in (0, 1):
+        rows = slice(half * HEAD_DIM, (half + 1) * HEAD_DIM)
+        value = hid_ref[rows]
+        mean = jnp.mean(value, axis=0, keepdims=True)
+        data.append(value - mean)
+        high = mean.astype(BF).astype(F32)
+        middle = (mean - high).astype(BF).astype(F32)
+        low = mean - high - middle
+        spot = lax.broadcasted_iota(jnp.int32, (TAIL, value.shape[1]), 0)
+        tails.append(
+            jnp.where(
+                spot == 0, high, jnp.where(spot == 1, middle, jnp.where(spot == 2, low, 0.0))
+            )
+        )
+        cots.append(cot_ref[rows])
+    for ref, cot, first in ((hk_ref, ck_ref, c == 0), (hs_ref, cs_ref, c == 1)):
+        ref[:HEAD_DIM] = jnp.where(first, data[0], data[1]).astype(BF)
+        ref[HEAD_DIM:] = jnp.where(first, tails[0], tails[1]).astype(BF)
+        cot[...] = jnp.where(first, cots[0], cots[1]).astype(BF)
+
+
+def split(spots, hidden_in, cotangent):
+    block = pl.BlockSpec((2 * HEAD_DIM, CLIP // 2), lambda i: (0, i))
+    specs = [
+        pl.BlockSpec((n, CLIP // 2), lambda i: (0, i))
+        for n in (HEAD_DIM + TAIL, HEAD_DIM + TAIL, HEAD_DIM, HEAD_DIM)
+    ]
+    return pl.pallas_call(
+        split_kernel,
+        grid=(4,),
+        in_specs=[spots_spec(), block, block],
+        out_specs=specs,
+        out_shape=[
+            shaped((n, 2 * CLIP)) for n in (HEAD_DIM + TAIL, HEAD_DIM + TAIL, HEAD_DIM, HEAD_DIM)
+        ],
+        cost_estimate=cost(0, 8 * HEAD_DIM * 2 * CLIP * 4),
+        name="split_in",
+    )(spots, hidden_in, cotangent)
+
+
+def deal_kernel(spots_ref, kept_ref, got_ref, here_ref, send_ref):
+    for is_own in (0, 1):
+        for x in (0, 1):
+
+            @pl.when((spots_ref[2] == is_own) & (spots_ref[3] == x))
+            def _(is_own=is_own, x=x):
+                pair = (kept_ref, got_ref) if is_own else (got_ref, kept_ref)
+                near = slice(x * CLIP, (x + 1) * CLIP)
+                away = slice((1 - x) * CLIP, (2 - x) * CLIP)
+                for i in (0, 1):
+                    here_ref[i] = pair[i][:, near]
+                    send_ref[i] = pair[i][:, away]
+
+
+def deal(spots, kept, got):
+    return pl.pallas_call(
+        deal_kernel,
+        in_specs=[spots_spec(), whole(), whole()],
+        out_specs=[whole()] * 2,
+        out_shape=[shaped((2, kept.shape[0], CLIP))] * 2,
+        cost_estimate=cost(0, 8 * kept.shape[0] * CLIP * 2),
+        name="deal",
+    )(spots, kept, got)
+
+
+def place_kernel(spots_ref, here_ref, there_ref, far_ref, own_ref, *stats_ref):
+    grid = ((here_ref, 0), (there_ref, 0)), ((far_ref, 0), (far_ref, 1))
+    for same in (0, 1):
+        for x in (0, 1):
+
+            @pl.when((spots_ref[4] == same) & (spots_ref[3] == x))
+            def _(same=same, x=x):
+                for i in (0, 1):
+                    for j in (0, 1):
+                        ref, k = grid[i if same else 1 - i][j if x == 0 else 1 - j]
+                        if stats_ref:
+                            tail = ref[k, HEAD_DIM:].astype(F32)
+                            mean = tail[0:1] + tail[1:2] + tail[2:3]
+                            own_ref[i, j] = ref[k, :HEAD_DIM].astype(F32) + mean
+                        else:
+                            own_ref[i, j] = ref[k]
+
+    if stats_ref:
+        values = own_ref[...].reshape(OWN, own_ref.shape[-1])
+        mean = jnp.mean(values, axis=0, keepdims=True)
+        off = values - mean
+        stats_ref[0][0:1] = mean
+        stats_ref[0][1:2] = jnp.sum(off * off, axis=0, keepdims=True)
+
+
+def place(spots, here, there, far, with_stats):
+    rows = here.shape[1]
+    spec = pl.BlockSpec((2, rows, BLOCK), lambda i: (0, 0, i))
+    own = (2, 2, HEAD_DIM, CLIP)
+    outs = [(own, F32), ((2, CLIP), F32)] if with_stats else [(own, BF)]
+    return pl.pallas_call(
+        place_kernel,
+        grid=(STEPS,),
+        in_specs=[spots_spec()] + [spec] * 3,
+        out_specs=[tokens_spec(dims) for dims, _ in outs],
+        out_shape=[shaped(dims, kind) for dims, kind in outs],
+        cost_estimate=cost(0, 8 * rows * CLIP * 6),
+        name="place_in",
+    )(spots, here, there, far)
+
+
+def leave_kernel(spots_ref, own_ref, near_ref, far_ref):
+    for same in (0, 1):
+        for x in (0, 1):
+
+            @pl.when((spots_ref[4] == same) & (spots_ref[3] == x))
+            def _(same=same, x=x):
+                for j in (0, 1):
+                    k = j if x == 0 else 1 - j
+                    near_ref[j] = own_ref[1 - same, k].astype(BF)
+                    far_ref[j] = own_ref[same, k].astype(BF)
+
+
+def leave(spots, own):
+    dims = (2, HEAD_DIM, CLIP)
+    return pl.pallas_call(
+        leave_kernel,
+        grid=(STEPS,),
+        in_specs=[spots_spec(), tokens_spec(own.shape)],
+        out_specs=[tokens_spec(dims)] * 2,
+        out_shape=[shaped(dims)] * 2,
+        cost_estimate=cost(0, 4 * HEAD_DIM * CLIP * 6),
+        name="leave",
+    )(spots, own)
+
+
+def undeal_kernel(spots_ref, near_ref, far_ref, there_ref, kept_ref, sent_ref):
+    for is_own in (0, 1):
+        for x in (0, 1):
+
+            @pl.when((spots_ref[2] == is_own) & (spots_ref[3] == x))
+            def _(is_own=is_own, x=x):
+                own = slice(x * CLIP, (x + 1) * CLIP)
+                other = slice((1 - x) * CLIP, (2 - x) * CLIP)
+                pair = (kept_ref, sent_ref) if is_own else (sent_ref, kept_ref)
+                for k, ref in enumerate((near_ref, far_ref)):
+                    pair[k][:, own] = ref[0]
+                    pair[k][:, other] = there_ref[k]
+
+
+def undeal(spots, near, far, there):
+    dims = (HEAD_DIM, 2 * CLIP)
+    return pl.pallas_call(
+        undeal_kernel,
+        in_specs=[spots_spec()] + [whole()] * 3,
+        out_specs=[whole()] * 2,
+        out_shape=[shaped(dims)] * 2,
+        cost_estimate=cost(0, 16 * HEAD_DIM * CLIP * 2),
+        name="undeal",
+    )(spots, near, far, there)
+
+
+def finish_kernel(spots_ref, kept_ref, got_ref, base_ref, shift_ref, out_ref):
+    c = spots_ref[0]
+    kept, got = kept_ref[...].astype(F32), got_ref[...].astype(F32)
+    for half in (0, 1):
+        rows = slice(half * HEAD_DIM, (half + 1) * HEAD_DIM)
+        value = jnp.where(c == half, kept, got)
+        out_ref[rows] = base_ref[rows] + shift_ref[rows] + value
+
+
+def finish(spots, kept, got, base, shift):
+    spec = pl.BlockSpec((HEAD_DIM, CLIP // 2), lambda i: (0, i))
+    wide = pl.BlockSpec((2 * HEAD_DIM, CLIP // 2), lambda i: (0, i))
+    return pl.pallas_call(
+        finish_kernel,
+        grid=(4,),
+        in_specs=[spots_spec(), spec, spec, wide, fixed(shift)],
+        out_specs=wide,
+        out_shape=shaped(base.shape, F32),
+        cost_estimate=cost(0, 8 * HEAD_DIM * 2 * CLIP * 4),
+        name="finish",
+    )(spots, kept, got, base, shift)
+
+
+def y_last(pair, yr, rows=slice(None)):
+    return jnp.concatenate([pair[yr][xr, zhr, rows] for xr in (0, 1) for zhr in (0, 1)])
+
+
+def x_last(pair, yr, rows=slice(None)):
+    return jnp.concatenate([pair[xr][yr, zhr, rows] for xr in (0, 1) for zhr in (0, 1)])
+
+
+def wide_rows(half, pair, rows=slice(None)):
+    return jnp.concatenate([half(pair, 0, rows), half(pair, 1, rows)], axis=1)
+
+
+def join_blocks(refs):
+    return jnp.concatenate(
+        [
+            refs[2 * zlr + cr][yr, xr]
+            for yr in (0, 1)
+            for zlr in (0, 1)
+            for xr in (0, 1)
+            for cr in (0, 1)
+        ]
+    )
+
+
+HEAD_ROWS = slice(0, HEAD_DIM)
+OUT_ROWS = slice(HEAD_DIM, 2 * HEAD_DIM)
+
+
+def project_kernel(b0, b1, b2, b3, qk0, qk1, vo0, vo1, qs_ref, vs_ref, qk_ref, v_ref, wide_ref):
+    wide = join_blocks((b0, b1, b2, b3))
+    wide_ref[...] = wide
+    result = mm(wide_rows(y_last, (qk0, qk1)), wide, 1, 0)
+    for t in range(4):
+        first = t * 2 * HEAD_DIM
+        queries = result[first : first + HEAD_DIM] + qs_ref[t]
+        qk_ref[t, 0] = queries.astype(BF)
+        qk_ref[t, 1] = result[first + HEAD_DIM : first + 2 * HEAD_DIM].astype(BF)
+    result = mm(wide_rows(x_last, (vo0, vo1), HEAD_ROWS), wide, 1, 0)
+    for t in range(4):
+        v_ref[t] = (result[t * HEAD_DIM : (t + 1) * HEAD_DIM] + vs_ref[t]).astype(BF)
+
+
+def project(blocks, qk, vo, q_shift, v_shift):
+    operands = (*blocks, *qk, *vo, q_shift, v_shift)
+    outs = ((4, 2, HEAD_DIM, CLIP), (4, HEAD_DIM, CLIP), (D, CLIP))
+    return pl.pallas_call(
+        project_kernel,
+        grid=(STEPS,),
+        in_specs=[tokens_spec(b.shape) for b in blocks] + [fixed(a) for a in operands[4:]],
+        out_specs=[tokens_spec(dims) for dims in outs],
+        out_shape=[shaped(dims) for dims in outs],
+        cost_estimate=cost(2 * 3 * OWN * D * CLIP, 4 * D * CLIP * 2),
+        name="project",
+    )(*operands)
+
+
+def up_kernel(b0, b1, b2, b3, up0, up1, shift_ref, act_ref, slope_ref, wide_ref):
+    wide = join_blocks((b0, b1, b2, b3))
+    wide_ref[...] = wide
+    for xr in (0, 1):
+        for zhr in (0, 1):
+            first = (2 * xr + zhr) * OWN
+            rows = slice(first, first + OWN)
+            weight = jnp.concatenate([up0[xr, zhr], up1[xr, zhr]], axis=1)
+            pre = mm(weight, wide, 1, 0) + shift_ref[rows]
+            cdf = 0.5 * (1.0 + lax.erf(pre * (0.5**0.5)))
+            act_ref[rows] = (pre * cdf).astype(BF)
+            slope_ref[rows] = cdf + pre * jnp.exp(-0.5 * pre * pre) * 0.3989422804014327
+
+
+def up_project(blocks, up, in_shift):
+    operands = (*blocks, *up, in_shift)
+    outs = (((UNITS, CLIP), BF), ((UNITS, CLIP), F32), ((D, CLIP), BF))
+    return pl.pallas_call(
+        up_kernel,
+        grid=(STEPS,),
+        in_specs=[tokens_spec(b.shape) for b in blocks] + [fixed(a) for a in operands[4:]],
+        out_specs=[tokens_spec(dims) for dims, _ in outs],
+        out_shape=[shaped(dims, kind) for dims, kind in outs],
+        cost_estimate=cost(2 * UNITS * D * CLIP, 6 * D * CLIP * 2),
+        name="up_project",
+    )(*operands)
+
+
+def grad_act_kernel(b0, b1, b2, b3, down0, down1, slope_ref, out_ref, wide_ref):
+    wide = join_blocks((b0, b1, b2, b3))
+    wide_ref[...] = wide
+    for xr in (0, 1):
+        for zhr in (0, 1):
+            first = (2 * xr + zhr) * OWN
+            rows = slice(first, first + OWN)
+            pair = (down0, down1)[xr]
+            weight = jnp.concatenate([pair[0, zhr], pair[1, zhr]], axis=1)
+            out_ref[rows] = (mm(weight, wide, 1, 0) * slope_ref[rows]).astype(BF)
+
+
+def grad_act(blocks, down, slope):
+    operands = (*blocks, *down, slope)
+    outs = ((UNITS, CLIP), (D, CLIP))
+    return pl.pallas_call(
+        grad_act_kernel,
+        grid=(STEPS,),
+        in_specs=[tokens_spec(b.shape) for b in blocks]
+        + [fixed(a) for a in down]
+        + [tokens_spec(slope.shape)],
+        out_specs=[tokens_spec(dims) for dims in outs],
+        out_shape=[shaped(dims) for dims in outs],
+        cost_estimate=cost(2 * UNITS * D * CLIP, 6 * D * CLIP * 2),
+        name="grad_act",
+    )(*operands)
+
+
+def grad_attended_kernel(b0, b1, b2, b3, vo0, vo1, out_ref, wide_ref):
+    wide = join_blocks((b0, b1, b2, b3))
+    wide_ref[...] = wide
+    result = mm(wide_rows(x_last, (vo0, vo1), OUT_ROWS), wide, 1, 0)
+    for t in range(4):
+        out_ref[t] = result[t * HEAD_DIM : (t + 1) * HEAD_DIM].astype(BF)
+
+
+def grad_attended_of(blocks, vo):
+    outs = ((4, HEAD_DIM, CLIP), (D, CLIP))
+    return pl.pallas_call(
+        grad_attended_kernel,
+        grid=(STEPS,),
+        in_specs=[tokens_spec(b.shape) for b in blocks] + [fixed(a) for a in vo],
+        out_specs=[tokens_spec(dims) for dims in outs],
+        out_shape=[shaped(dims) for dims in outs],
+        cost_estimate=cost(2 * OWN * D * CLIP, 4 * D * CLIP * 2),
+        name="grad_attended",
+    )(*blocks, *vo)
+
+
+def fold_kernel(fill, counts, *refs):
+    sources, values = refs[: counts[0]], refs[counts[0] : sum(counts)]
+    keep_ref, send_ref, turned_ref = refs[sum(counts) :]
+
+    @pl.when(pl.program_id(0) == 0)
+    def _():
+        for yr in (0, 1):
+            turned_ref[yr * HALF : (yr + 1) * HALF] = jnp.transpose(fill(sources, yr))
+
+    value = jnp.concatenate([ref[...].reshape(-1, BLOCK) for ref in values])
+    for yr in (0, 1):
+        result = mm(turned_ref[yr * HALF : (yr + 1) * HALF], value, 1, 0)
+        for spot in range(8):
+            part = result[spot * HEAD_DIM : (spot + 1) * HEAD_DIM]
+            zlr, xr, cr = spot >> 2, spot >> 1 & 1, spot & 1
+            if cr == 0:
+                keep_ref[yr, zlr, xr] = part
+            else:
+                send_ref[yr, zlr, xr] = part.astype(BF)
+
+
+def fold(fill, sources, values, name):
+    depth = sum(v.size // CLIP for v in values)
+    dims = (2, 2, 2, HEAD_DIM, CLIP)
+    return pl.pallas_call(
+        functools.partial(fold_kernel, fill, (len(sources), len(values))),
+        grid=(STEPS,),
+        in_specs=[fixed(a) for a in sources] + [tokens_spec(v.shape) for v in values],
+        out_specs=[tokens_spec(dims)] * 2,
+        out_shape=[shaped(dims, F32), shaped(dims)],
+        scratch_shapes=[pltpu.VMEM((D, depth), BF)],
+        cost_estimate=cost(2 * D * depth * CLIP, 6 * D * CLIP * 2),
+        name=name,
+    )(*sources, *values)
+
+
+def fill_out(sources, yr):
+    return x_last(sources, yr, OUT_ROWS)
+
+
+def fill_up(sources, yr):
+    return y_last(sources, yr)
+
+
+def fill_down(sources, yr):
+    return x_last(sources, yr)
+
+
+def fill_project(sources, yr):
+    return jnp.concatenate([y_last(sources[:2], yr), x_last(sources[2:], yr, HEAD_ROWS)])
+
+
+def pair_y_kernel(left_ref, right_ref, keep_ref, send_ref):
+    result = mm(left_ref[0], right_ref[...], 1, 1)
+    keep_ref[0] = result[:, :HALF]
+    send_ref[0] = result[:, HALF:].astype(BF)
+
+
+def grad_y_first(left, right, name):
+    rows = left.shape[1]
+    dims = (4, rows, HALF)
+    spec = pl.BlockSpec((1, rows, HALF), lambda i: (i, 0, 0))
+    return pl.pallas_call(
+        pair_y_kernel,
+        grid=(4,),
+        in_specs=[pl.BlockSpec((1, rows, CLIP), lambda i: (i, 0, 0)), fixed(right)],
+        out_specs=[spec] * 2,
+        out_shape=[shaped(dims, F32), shaped(dims)],
+        cost_estimate=cost(2 * 4 * rows * D * CLIP, 4 * rows * D * 6),
+        name=name,
+    )(left, right)
+
+
+def pair_x_kernel(count, *refs):
+    keep_ref, send_ref = refs[2 * count :]
+    start = 0
+    for left_ref, right_ref in zip(refs[:count], refs[count : 2 * count]):
+        rows = slice(start, start + left_ref.shape[2])
+        start += left_ref.shape[2]
+        for xr in (0, 1):
+            result = mm(left_ref[xr, 0], right_ref[...], 1, 1)
+            for yr in (0, 1):
+                part = result[:, yr * HALF : (yr + 1) * HALF]
+                if xr == 0:
+                    keep_ref[yr, 0, rows] = part
+                else:
+                    send_ref[yr, 0, rows] = part.astype(BF)
+
+
+def grad_x_first(lefts, rights, name):
+    rows = sum(v.shape[2] for v in lefts)
+    dims = (2, 2, rows, HALF)
+    spec = pl.BlockSpec((2, 1, rows, HALF), lambda i: (0, i, 0, 0))
+    return pl.pallas_call(
+        functools.partial(pair_x_kernel, len(lefts)),
+        grid=(2,),
+        in_specs=[pl.BlockSpec((2, 1) + v.shape[2:], lambda i: (0, i, 0, 0)) for v in lefts]
+        + [fixed(v) for v in rights],
+        out_specs=[spec] * 2,
+        out_shape=[shaped(dims, F32), shaped(dims)],
+        cost_estimate=cost(2 * 4 * rows * D * CLIP, 4 * rows * D * 6),
+        name=name,
+    )(*lefts, *rights)
+
+
+def token_stats(values):
+    mean = jnp.mean(values, axis=0)
+    off = values - mean
+    return jnp.stack([mean, jnp.sum(off * off, axis=0)])
+
+
+def merge_stats(stats, count, swap):
+    other = swap(stats)
+    apart = other[0] - stats[0]
+    return jnp.stack(
+        [0.5 * (stats[0] + other[0]), stats[1] + other[1] + apart * apart * (0.5 * count)]
+    )
+
+
+def after(values, *others):
+    return lax.optimization_barrier((values, others))[0]
+
+
+def local_clip(
+    hidden_in,
+    lengths,
+    ln1_gain,
+    ln1_shift,
+    qkv_weight,
+    qv_bias,
+    out_weight,
+    out_bias,
+    ln2_gain,
+    ln2_shift,
+    in_weight,
+    in_bias,
+    down_weight,
+    down_bias,
+    cotangent,
+):
+    row, col = lax.axis_index("row"), lax.axis_index("col")
+    y, c = row // 2, row % 2
+    zh, zl, x = col // 4, col // 2 % 2, col % 2
+    same_zy = y == zh
+    spots = jnp.stack([c, zl == c, zh == c, x, same_zy]).astype(jnp.int32)
+
+    def flip(grid):
+        grid = jnp.where(same_zy, grid, grid[::-1])
+        return jnp.where(x == 0, grid, grid[:, ::-1])
+
+    def fold_cores(parts):
+        keep = parts[0] + swap_core(parts[1])
+        return keep[:, 0], keep[:, 1].astype(BF)
+
+    kept, sent = prepare(
+        spots,
+        jnp.swapaxes(qkv_weight, 1, 2),
+        out_weight,
+        in_weight,
+        jnp.swapaxes(down_weight, 0, 1),
+    )
+    weights_got = swap_core(sent)
+    h_kept, h_sent, c_kept, c_sent = split(spots, hidden_in, cotangent)
+    h_here, h_send = deal(spots, h_kept, swap_core(h_sent))
+    s_qk, s_vo, s_up, s_down = join_lanes(spots, kept, weights_got)
+    h_there = swap_x(h_send)
+    qk_zh, vo_zh = swap_zh(s_qk), swap_zh(s_vo)
+
+    pack = jnp.stack(
+        [ln1_gain, ln1_shift, ln2_gain, ln2_shift, out_bias, qv_bias[0], qv_bias[1]]
+    )
+    pack = jnp.where(c == 0, pack[:, :HEAD_DIM], pack[:, HEAD_DIM:])
+    hidden_shift = jnp.where(c == 0, in_bias[:OWN], in_bias[OWN:])
+    pack = jnp.concatenate([pack, hidden_shift.reshape(4, HEAD_DIM)])
+    pack = jnp.stack([pack, swap_x(pack)])
+    pack = jnp.stack([pack, swap_zh(pack)])
+
+    h_message = jnp.stack([h_here[1], h_there[1]])
+    h_message, qk_zh, vo_zh = lax.optimization_barrier((h_message, qk_zh, vo_zh))
+    h_far = swap_zh(h_message)
+    qk_one = jnp.stack([s_qk, qk_zh])
+    vo_one = jnp.stack([s_vo, vo_zh])
+    qk_two, vo_two = swap_x(qk_one), swap_y(vo_one)
+    h_far, qk_two, vo_two = lax.optimization_barrier((h_far, qk_two, vo_two))
+    w_qk = jnp.stack([qk_one, qk_two])
+    w_vo = jnp.stack([vo_one, vo_two])
+    w_qk = w_qk, swap_y(w_qk)
+    w_vo = w_vo, swap_x(w_vo)
+    s_up = after(s_up, h_far)
+    up_zh = swap_zh(s_up)
+
+    owned = flip(pack)
+    gain_one, shift_one, gain_two, shift_two, out_shift = (
+        owned[:, :, i, :, None] for i in range(5)
+    )
+    by_head = pack.transpose(1, 0, 2, 3)
+    q_shift = by_head[:, :, 5].reshape(4, HEAD_DIM, 1)
+    v_shift = by_head[:, :, 6].reshape(4, HEAD_DIM, 1)
+    in_shift = by_head[:, :, 7:].reshape(UNITS, 1)
+
+    hidden_own, stats = place(spots, h_here, h_there, h_far, True)
+    stats = merge_stats(stats, OWN, swap_core)
+    stats = merge_stats(stats, 2 * OWN, swap_zl)
+    inv_one = lax.rsqrt(stats[1] / D + EPS)
+    own_one = (hidden_own - stats[0]) * inv_one
+    low_one = (own_one * gain_one + shift_one).astype(BF)
+    low_one_z = swap_zl(low_one)
+    s_down = after(s_down, low_one_z)
+    down_zh = swap_zh(s_down)
+    c_here, c_send = deal(spots, c_kept, swap_core(after(c_sent, low_one)))
+    c_there = swap_x(after(c_send, w_vo[1]))
+    wide_one = low_one, swap_core(low_one), low_one_z, swap_core(low_one_z)
+    wide_one = after(wide_one, c_send, s_down)
+
+    qk, values, ln_one = project(wide_one, w_qk, w_vo, q_shift, v_shift)
+    clip_len = lax.dynamic_slice_in_dim(lengths, 4 * y + 2 * zh + x, 1)
+    attended, log_sum = attend_clip(qk, values, clip_len, CLIP)
+    attended, up_zh, down_zh, c_there = lax.optimization_barrier(
+        (attended, up_zh, down_zh, c_there)
+    )
+    up_one = jnp.stack([s_up, up_zh])
+    down_one = jnp.stack([s_down, down_zh])
+    c_message = jnp.stack([c_here[1], c_there[1]])
+    up_two, down_two, c_far = swap_x(up_one), swap_y(down_one), swap_zh(c_message)
+    delta_near, delta_send = fold_cores(
+        fold(fill_out, w_vo, (after(attended, up_one, down_one, c_message),), "fold_out")
+    )
+    delta_got = swap_zl(delta_send)
+    delta_got, up_two, down_two, c_far = lax.optimization_barrier(
+        (delta_got, up_two, down_two, c_far)
+    )
+    delta_mid = delta_near + delta_got + out_shift
+    w_up = jnp.stack([up_one, up_two])
+    w_down = jnp.stack([down_one, down_two])
+    w_up = w_up, swap_y(w_up)
+    w_down = w_down, swap_x(w_down)
+
+    hidden_mid = hidden_own + delta_mid
+    stats = token_stats(hidden_mid.reshape(OWN, CLIP))
+    stats = merge_stats(stats, OWN, swap_core)
+    stats = merge_stats(stats, 2 * OWN, swap_zl)
+    inv_two = lax.rsqrt(stats[1] / D + EPS)
+    own_two = (hidden_mid - stats[0]) * inv_two
+    low_two = (own_two * gain_two + shift_two).astype(BF)
+    low_two_z = swap_zl(low_two)
+    (cot_own,) = place(spots, c_here, c_there, after(c_far, low_two), False)
+    cot_own = after(cot_own, low_two_z)
+    cot_z = swap_zl(cot_own)
+    wide_cot = cot_own, swap_core(cot_own), cot_z, swap_core(cot_z)
+    wide_two = low_two, swap_core(low_two), low_two_z, swap_core(low_two_z)
+    act_low, slope, ln_two = up_project(after(wide_two, cot_own), w_up, in_shift)
+    out_near, out_send = fold_cores(fold(fill_down, w_down, (act_low,), "fold_down"))
+    out_send = after(out_send, cot_z)
+    out_got = swap_zl(out_send)
+
+    grad_pre, cot_all = grad_act(after(wide_cot, out_send), w_down, slope)
+    two_near, two_send = fold_cores(fold(fill_up, w_up, (grad_pre,), "fold_up"))
+    two_send, out_got = lax.optimization_barrier((two_send, out_got))
+    two_got = swap_zl(two_send)
+    by_unit = (2, 2, OWN, CLIP)
+    act_low_after, cot_all_after = after((act_low, cot_all), two_send)
+    part_down = grad_x_first((act_low_after.reshape(by_unit),), (cot_all_after,), "grad_down")
+    down_first = swap_x(part_down[1])
+    part_up = grad_y_first(
+        after(grad_pre, part_down[1]).reshape(4, OWN, CLIP), ln_two, "grad_up"
+    )
+    up_first = swap_y(part_up[1])
+    two_got = after(two_got, part_up[1])
+    grad_two = two_near + two_got
+
+    def norm_back(grad, normed, inv, gain):
+        scaled = grad * gain
+        sums = jnp.stack([jnp.sum(scaled, axis=(0, 1, 2)), jnp.sum(scaled * normed, axis=(0, 1, 2))])
+        sums = sums + swap_core(sums)
+        sums = (sums + swap_zl(sums)) / D
+        return inv * (scaled - sums[0] - normed * sums[1])
+
+    norm_two_grad = norm_back(grad_two, own_two, inv_two, gain_two)
+    mid_own = cot_own.astype(F32) + norm_two_grad
+    mid_low = mid_own.astype(BF)
+    mid_z = swap_zl(mid_low)
+    out_leave, out_leave_far = leave(spots, delta_mid + after(out_near, mid_low) + out_got)
+    out_leave_far, mid_z = lax.optimization_barrier((out_leave_far, mid_z))
+    out_far = swap_zh(out_leave_far)
+    wide_mid = mid_low, swap_core(mid_low), mid_z, swap_core(mid_z)
+    wide_mid = after(wide_mid, out_leave_far)
+
+    def second_step(keep, got):
+        keep = keep.reshape(2, 2, -1, HALF) + got.reshape(2, 2, -1, HALF)
+        return keep[0], keep[1].astype(BF)
+
+    def third_step(keep, got):
+        keep = keep + got
+        return keep[0], keep[1].astype(BF)
+
+    grad_attended, mid_all = grad_attended_of(wide_mid, w_vo)
+    grad_attended, down_first, up_first = lax.optimization_barrier(
+        (grad_attended, down_first, up_first)
+    )
+    down_keep, down_send = second_step(part_down[0], down_first)
+    up_keep, up_send = second_step(part_up[0], up_first)
+    down_second, up_second = swap_y(down_send), swap_x(up_send)
+    grad_attended = after(grad_attended, down_send, up_send)
+    grad_qk, grad_v = attend_clip_back(qk, values, log_sum, grad_attended, clip_len, CLIP)
+    grad_qk, grad_v, down_second, up_second, out_far = lax.optimization_barrier(
+        (grad_qk, grad_v, down_second, up_second, out_far)
+    )
+    down_keep, down_send = third_step(down_keep, down_second)
+    up_keep, up_send = third_step(up_keep, up_second)
+    down_third, up_third = swap_zh(down_send), swap_zh(up_send)
+    out_message = jnp.stack([out_leave[1], out_far[1]])
+    out_there = swap_x(out_message)
+    folded = fold(
+        fill_project,
+        (*w_qk, *w_vo),
+        after((grad_qk, grad_v), down_send, up_send, out_message),
+        "fold_project",
+    )
+    one_near, one_send = fold_cores(folded)
+    one_got = swap_zl(one_send)
+    by_head_dims = (2, 2, HEAD_DIM, CLIP)
+    grad_v, grad_qk = after((grad_v, grad_qk), one_send)
+    part_vo = grad_x_first(
+        (grad_v.reshape(by_head_dims), attended.reshape(by_head_dims)),
+        (ln_one, mid_all),
+        "grad_vo",
+    )
+    vo_first = swap_x(part_vo[1])
+    part_qk = grad_y_first(
+        after(grad_qk, part_vo[1]).reshape(4, 2 * HEAD_DIM, CLIP), ln_one, "grad_qk"
+    )
+    qk_first = swap_y(part_qk[1])
+    out_kept, out_sent = undeal(spots, out_leave, out_far, after(out_there, part_qk[1]))
+    hidden_out = finish(spots, out_kept, swap_core(out_sent), hidden_in, down_bias[:, None])
+
+    one_got = after(one_got, out_sent)
+    grad_one = one_near + one_got
+    norm_one_grad = norm_back(grad_one, own_one, inv_one, gain_one)
+    in_leave, in_leave_far = leave(spots, norm_two_grad + norm_one_grad)
+    in_far = swap_zh(in_leave_far)
+
+    vo_first, qk_first, down_third, up_third = after(
+        (vo_first, qk_first, down_third, up_third), in_leave_far
+    )
+    vo_keep, vo_send = second_step(part_vo[0], vo_first)
+    qk_keep, qk_send = second_step(part_qk[0], qk_first)
+    vo_second, qk_second = swap_y(vo_send), swap_x(qk_send)
+    ff_kept, ff_sent = store_ff(
+        spots, after(up_keep + up_third, vo_send, qk_send), down_keep + down_third
+    )
+    ff_got = swap_core(ff_sent)
+    in_far, vo_second, qk_second = lax.optimization_barrier(
+        after((in_far, vo_second, qk_second), ff_sent)
+    )
+    in_message = jnp.stack([in_leave[1], in_far[1]])
+    in_there = swap_x(in_message)
+    vo_keep, vo_send = third_step(vo_keep, vo_second)
+    qk_keep, qk_send = third_step(qk_keep, qk_second)
+    vo_third, qk_third = swap_zh(vo_send), swap_zh(qk_send)
+    g_up, g_down = join_ff(spots, ff_kept, after(ff_got, vo_send, qk_send, in_message))
+    in_kept, in_sent = undeal(spots, in_leave, in_far, in_there)
+    no_shift = jnp.zeros((2 * HEAD_DIM, 1), F32)
+    hidden_grad = finish(spots, in_kept, swap_core(in_sent), cotangent, no_shift)
+    at_kept, at_sent = store_qkvo(spots, qk_keep + qk_third, vo_keep + vo_third)
+    g_qkv, g_out = join_qkvo(spots, at_kept, swap_core(at_sent))
+
+    def over_tokens(values):
+        return jnp.sum(values, axis=-1, dtype=F32)
+
+    owned = jnp.stack(
+        [
+            over_tokens(v)
+            for v in (
+                grad_one * own_one,
+                grad_one,
+                grad_two * own_two,
+                grad_two,
+                mid_own,
+                cot_own.astype(F32),
+            )
+        ],
+        axis=2,
+    ).reshape(2, 2, -1)
+    heads = jnp.concatenate(
+        [
+            over_tokens(grad_qk[:, 0].astype(F32)),
+            over_tokens(grad_v.astype(F32)),
+            over_tokens(grad_pre.astype(F32)).reshape(4, OWN),
+        ],
+        axis=1,
+    )
+    vectors = jnp.concatenate([flip(owned), heads.reshape(2, 2, -1).transpose(1, 0, 2)], axis=2)
+    total = vectors[0] + swap_zh(vectors[1])
+    total = total[0] + swap_x(total[1])
+    total = total + swap_y(total)
+    other = swap_core(total)
+    both = jnp.where(c == 0, jnp.stack([total, other]), jnp.stack([other, total]))
+    singles = both[:, : 8 * HEAD_DIM].reshape(2, 8, HEAD_DIM).transpose(1, 0, 2).reshape(8, -1)
+
+    return (
+        hidden_out,
+        hidden_grad,
+        singles[0],
+        singles[1],
+        jnp.swapaxes(g_qkv, 1, 2),
+        singles[6:8],
+        g_out,
+        singles[4],
+        singles[2],
+        singles[3],
+        g_up,
+        both[:, 8 * HEAD_DIM :].reshape(-1),
+        jnp.swapaxes(g_down, 0, 1),
+        singles[5],
+    )
+
+
 def solution(mesh):
+    sizes = dict(mesh.shape)
+
+    def program(*arrays):
+        small = sizes == {"row": 4, "col": 8} and arrays[0].shape == (D, 2 * sizes["row"] * CLIP)
+        return mapped(local_clip if small else local, mesh)(*arrays)
+
+    return program
+
+
+def mapped(body, mesh):
     return jax.shard_map(
-        local,
+        body,
         mesh=mesh,
         in_specs=(
             P("col", "row"),

time: 2620 us -> 530 us (0.20)
  waiting for transfers between devices: 1790 us -> 180 us
  blocking collectives: 267 us -> 0 us
  Pallas kernels: 0 us -> 176 us
  matrix products: 156 us -> 0 us
  local copies, waits for them, and re-layouts: 129 us -> 44.5 us
  other arithmetic: 120 us -> 46.5 us
  starting transfers between devices: 139 us -> 73.5 us
    reduce_scatter x12 -> x0, waiting for transfers between devices: 652 us -> none  [the longest x8 556 us: narrow(): return lax.psum_scatter(values, 'col', scatter_dimension=1, tiled=True)]
    all_gather x11 -> x0, waiting for transfers between devices: 513 us -> none  [the longest x8 497 us: widen(): return lax.all_gather(values, 'col', axis=1, tiled=True)]
    ppermute x24 -> x73, waiting for transfers between devices: 494 us -> 180 us  [the longest x14 76.2 us: swap_zh(): return lax.ppermute(values, 'col', [(i, i ^ 4) for i in range(8)])]
    pallas_call x0 -> x31, Pallas kernels: none -> 176 us  [the longest x4 30.8 us: fold(): pl.pallas_call(functools.partial(fold_kernel, fill, (len(sources), len(va...]
    dot_general x34 -> x0, matrix products: 148 us -> none  [the longest x6 41 us: contract_cols(): lax.dot_general(left, right, (((1,), (1,)), ((), ())), preferred_element_...]
    all_to_all x4 -> x0, blocking collectives: 130 us -> none  [the longest x2 82.1 us: to_clips(): lax.all_to_all(stacked, 'col', split_axis=1, concat_axis=2, tiled=True)]
    all_to_all x4 -> x0, waiting for transfers between devices: 122 us -> none  [the longest x2 116 us: to_columns(): lax.all_to_all(stacked, 'col', split_axis=2, concat_axis=1, tiled=True)]
    psum x4 -> x0, blocking collectives: 118 us -> none  [row_totals(): return lax.psum((first_sum, second_sum), 'col')]
  transfers between devices with their start and end apart: 51 -> 73, of which waited for: 37 -> 34; matrix products, arithmetic and copies ran while one was open for 12% -> 9% of each run, Pallas kernels for 0% -> 24%
where the time goes in v1:
time: 530 us; the launch traced here: 523 us
  waiting for transfers between devices  180 us (34%)
  Pallas kernels  176 us (33%)
  starting transfers between devices  73.5 us (14%)
  other arithmetic  46.5 us (9%)
  local copies, waits for them, and re-layouts  44.5 us (8%)
    ppermute x14, waiting for transfers between devices, swap_zh(): return lax.ppermute(values, 'col', [(i, i ^ 4) for i in range(8)])  76.2 us
    ppermute x12, waiting for transfers between devices, swap_zl(): return lax.ppermute(values, 'col', [(i, i ^ 2) for i in range(8)])  66.5 us
    ppermute x24, starting transfers between devices, swap_core(): return lax.ppermute(values, 'row', [(i, i ^ 1) for i in range(4)])  35.8 us
    pallas_call x4, Pallas kernels, fold(): pl.pallas_call(functools.partial(fold_kernel, fill, (len(sources), len(va...  30.8 us
    ppermute x9, waiting for transfers between devices, swap_y(): return lax.ppermute(values, 'row', [(i, i ^ 2) for i in range(4)])  21.5 us
    pallas_call x1, Pallas kernels, attend_clip_back(): pl.pallas_call(attend_back_kernel, grid_spec=pltpu.PrefetchScalarGridSpec...  18.1 us
    pallas_call x2, Pallas kernels, grad_x_first(): pl.pallas_call(functools.partial(pair_x_kernel, len(lefts)), grid=(2,), i...  17.7 us
    unnamed x136, local copies, waits for them, and re-layouts  16.8 us
  transfers between devices with their start and end apart: 73, of which 34 were waited for; matrix products, arithmetic and copies ran while one was open for 9% of the time, Pallas kernels for 24%

profile of v1, /device:TPU:1, one launch (start us, length us, event | category | flops | bytes accessed | tf_op | source)
XLA Modules:
  0.0 522.8 jit_solution(18172666647111393042)
XLA Ops:
  5.4 4.4 prepare_weights.1
  23.8 11.2 %collective-permute-done.4 = bf16[160,640]{1,0:T(8,128)(2,1)S(1)} collective-permute-done((bf16[160,640]{1,0:T(8,128)(2,1)}, bf16[160,640]{1,0:T(8,128)(2,1)S(1)}, u32[]{:S(2)}, u32[]{:S(2)}) %collective-permute-start.4) | collective-permute-done | bytes 204832 | tf_op jit(solution)/shard_map/ppermute | solution.py:387
  35.0 4.4 collective-permute-done.3
  43.6 13.7 %collective-permute-done.12 = f32[2,11,80]{2,1,0:T(8,128)S(1)} collective-permute-done((f32[2,11,80]{2,1,0:T(8,128)S(1)}, f32[2,11,80]{2,1,0:T(8,128)S(1)}, u32[]{:S(2)}, u32[]{:S(2)}) %collective-permute-start.12) | collective-permute-done | bytes 7072 | tf_op jit(solution)/shard_map/ppermute | solution.py:387
  74.0 11.2 %collective-permute-done.14.b2 = bf16[2,2,80,1024]{3,2,1,0:T(8,128)(2,1)} collective-permute-done((bf16[2,2,80,1024]{3,2,1,0:T(8,128)(2,1)}, bf16[2,2,80,1024]{3,2,1,0:T(8,128)(2,1)}, u32[]{:S(2)}, u32[]{:S(2)}) %collective-permute-start.14) | collective-permute-done | bytes 655392 | tf_op jit(solution)/shard_map/ppermute | solution.py:383
  96.6 7.4 %project.1 = (bf16[4,2,80,1024]{3,2,1,0:T(8,128)(2,1)}, bf16[4,80,1024]{2,1,0:T(8,128)(2,1)}, bf16[1280,1024]{1,0:T(8,128)(2,1)}) custom-call(bf16[2,2,80,1024]{3,2,1,0:T(8,128)(2,1)} %add_convert_fusion.1.b0, bf16[2,2,80,1024]{3,2,1,0:T(8,128)(2,1)} %collective-permute-done.13.b1, bf16[2,2,80,1024]{3,2,1,0:T(8,128)(2,1)} %collective-permute-done.14.b2, ...), custom_call_target="tpu_custom_call" | custom-call | flops 1 | bytes 1 | tf_op jit(solution)/shard_map/project/pallas_call | solution.py:938
  104.0 10.3 %attend_clip.1 = (bf16[4,80,1024]{2,1,0:T(8,128)(2,1)}, f32[4,1,1024]{2,1,0:T(1,128)}) custom-call(s32[1]{0:T(128)} %dynamic_slice.3.len_ref, bf16[4,2,80,1024]{3,2,1,0:T(8,128)(2,1)} %get-tuple-element.177.q_ref.k_ref, bf16[4,2,80,1024]{3,2,1,0:T(8,128)(2,1)} %get-tuple-element.177.q_ref.k_ref, bf16[4,80,1024]{2,1,0:T(8,128)(2,1)} %get-tuple-element.178.v_ref), custom_call_target="tpu_custom_call" | custom-call | flops 1 | bytes 1 | tf_op jit(solution)/shard_map/attend_clip/pallas_call | solution.py:443
  117.5 8.8 %collective-permute-done.19 = bf16[320,640]{1,0:T(8,128)(2,1)} collective-permute-done((bf16[320,640]{1,0:T(8,128)(2,1)}, bf16[320,640]{1,0:T(8,128)(2,1)}, u32[]{:S(2)}, u32[]{:S(2)}) %collective-permute-start.19) | collective-permute-done | bytes 409632 | tf_op jit(solution)/shard_map/ppermute | solution.py:387
  130.0 5.7 %fold_out.1 = (f32[2,2,2,80,1024]{4,3,2,1,0:T(8,128)}, bf16[2,2,2,80,1024]{4,3,2,1,0:T(8,128)(2,1)}) custom-call(bf16[2,2,160,640]{3,2,1,0:T(8,128)(2,1)} %copy-done.2, bf16[2,2,160,640]{3,2,1,0:T(8,128)(2,1)} %copy-done.8, bf16[4,80,1024]{2,1,0:T(8,128)(2,1)} %get-tuple-element.188.refs_2_), custom_call_target="tpu_custom_call" | custom-call | flops 1 | bytes 1 | tf_op jit(solution)/shard_map/fold_out/pallas_call | solution.py:1050
  142.8 19.6 %collective-permute-done.25.far_ref = bf16[2,80,1024]{2,1,0:T(8,128)(2,1)S(1)} collective-permute-done((bf16[2,80,1024]{2,1,0:T(8,128)(2,1)S(1)}, bf16[2,80,1024]{2,1,0:T(8,128)(2,1)S(1)}, u32[]{:S(2)}, u32[]{:S(2)}) %collective-permute-start.25) | collective-permute-done | bytes 327712 | tf_op jit(solution)/shard_map/ppermute | solution.py:387
  174.9 11.3 %collective-permute-done.30.b2 = bf16[2,2,80,1024]{3,2,1,0:T(8,128)(2,1)} collective-permute-done((bf16[2,2,80,1024]{3,2,1,0:T(8,128)(2,1)S(1)}, bf16[2,2,80,1024]{3,2,1,0:T(8,128)(2,1)}, u32[]{:S(2)}, u32[]{:S(2)}) %collective-permute-start.30) | collective-permute-done | bytes 655392 | tf_op jit(solution)/shard_map/ppermute | solution.py:383
  194.0 10.8 %collective-permute-done.32.up1.refs_1_ = bf16[2,2,320,640]{3,2,1,0:T(8,128)(2,1)} collective-permute-done((bf16[2,2,320,640]{3,2,1,0:T(8,128)(2,1)}, bf16[2,2,320,640]{3,2,1,0:T(8,128)(2,1)}, u32[]{:S(2)}, u32[]{:S(2)}) %collective-permute-start.32) | collective-permute-done | bytes 1638432 | tf_op jit(solution)/shard_map/ppermute | solution.py:375
  204.7 10.4 %up_project.1 = (bf16[1280,1024]{1,0:T(8,128)(2,1)}, f32[1280,1024]{1,0:T(8,128)}, bf16[1280,1024]{1,0:T(8,128)(2,1)}) custom-call(bf16[2,2,80,1024]{3,2,1,0:T(8,128)(2,1)} %copy-done.33, bf16[2,2,80,1024]{3,2,1,0:T(8,128)(2,1)} %collective-permute-done.29.b1, bf16[2,2,80,1024]{3,2,1,0:T(8,128)(2,1)} %collective-permute-done.30.b2, ...), custom_call_target="tpu_custom_call" | custom-call | flops 1 | bytes 1 | tf_op jit(solution)/shard_map/up_project/pallas_call | solution.py:966
  215.1 8.5 %fold_down.1 = (f32[2,2,2,80,1024]{4,3,2,1,0:T(8,128)}, bf16[2,2,2,80,1024]{4,3,2,1,0:T(8,128)(2,1)}) custom-call(bf16[2,2,320,640]{3,2,1,0:T(8,128)(2,1)} %pad_maximum_fusion.refs_0_.down0, bf16[2,2,320,640]{3,2,1,0:T(8,128)(2,1)} %collective-permute-done.26.refs_1_.down1, bf16[1280,1024]{1,0:T(8,128)(2,1)} %get-tuple-element.215.refs_2_), custom_call_target="tpu_custom_call" | custom-call | flops 1 | bytes 1 | tf_op jit(solution)/shard_map/fold_down/pallas_call | solution.py:1050
  227.5 15.6 %collective-permute-done.35.b2 = bf16[2,2,80,1024]{3,2,1,0:T(8,128)(2,1)S(1)} collective-permute-done((bf16[2,2,80,1024]{3,2,1,0:T(8,128)(2,1)S(1)}, bf16[2,2,80,1024]{3,2,1,0:T(8,128)(2,1)S(1)}, u32[]{:S(2)}, u32[]{:S(2)}) %collective-permute-start.35) | collective-permute-done | bytes 655392 | tf_op jit(solution)/shard_map/ppermute | solution.py:383
  249.4 9.1 %grad_act.1 = (bf16[1280,1024]{1,0:T(8,128)(2,1)}, bf16[1280,1024]{1,0:T(8,128)(2,1)}) custom-call(bf16[2,2,80,1024]{3,2,1,0:T(8,128)(2,1)} %place_in.3.b0, bf16[2,2,80,1024]{3,2,1,0:T(8,128)(2,1)} %copy-done.45, bf16[2,2,80,1024]{3,2,1,0:T(8,128)(2,1)} %copy-done.44, bf16[2,2,80,1024]{3,2,1,0:T(8,128)(2,1)} %copy-done.46, ...), custom_call_target="tpu_custom_call" | custom-call | flops 1 | bytes 1 | tf_op jit(solution)/shard_map/grad_act/pallas_call | solution.py:992
  258.6 8.7 %fold_up.1 = (f32[2,2,2,80,1024]{4,3,2,1,0:T(8,128)}, bf16[2,2,2,80,1024]{4,3,2,1,0:T(8,128)(2,1)}) custom-call(bf16[2,2,320,640]{3,2,1,0:T(8,128)(2,1)} %pad_maximum_fusion.1.up0.refs_0_, bf16[2,2,320,640]{3,2,1,0:T(8,128)(2,1)} %collective-permute-done.32.up1.refs_1_, bf16[1280,1024]{1,0:T(8,128)(2,1)} %get-tuple-element.218.refs_2_), custom_call_target="tpu_custom_call" | custom-call | flops 1 | bytes 1 | tf_op jit(solution)/shard_map/fold_up/pallas_call | solution.py:1050
  275.0 10.3 %collective-permute-done.38 = bf16[2,2,80,1024]{3,2,1,0:T(8,128)(2,1)} collective-permute-done((bf16[2,2,80,1024]{3,2,1,0:T(8,128)(2,1)S(1)}, bf16[2,2,80,1024]{3,2,1,0:T(8,128)(2,1)}, u32[]{:S(2)}, u32[]{:S(2)}) %collective-permute-start.38) | collective-permute-done | bytes 655392 | tf_op jit(solution)/shard_map/ppermute | solution.py:383
  285.6 7.4 %grad_down.1 = (f32[2,2,320,640]{3,2,1,0:T(8,128)}, bf16[2,2,320,640]{3,2,1,0:T(8,128)(2,1)}) custom-call(bf16[2,2,320,1024]{3,2,1,0:T(8,128)(2,1)} %bitcast.179, bf16[1280,1024]{1,0:T(8,128)(2,1)} %get-tuple-element.216.refs_1_), custom_call_target="tpu_custom_call" | custom-call | flops 1 | bytes 1 | tf_op jit(solution)/shard_map/grad_down/pallas_call | solution.py:1119
  292.9 7.2 %grad_up.1 = (f32[4,320,640]{2,1,0:T(8,128)}, bf16[4,320,640]{2,1,0:T(8,128)(2,1)}) custom-call(bf16[4,320,1024]{2,1,0:T(8,128)(2,1)} %bitcast.178, bf16[1280,1024]{1,0:T(8,128)(2,1)} %get-tuple-element.219.right_ref), custom_call_target="tpu_custom_call" | custom-call | flops 1 | bytes 1 | tf_op jit(solution)/shard_map/grad_up/pallas_call | solution.py:1088
  320.0 5.4 %collective-permute-done.43.b2 = bf16[2,2,80,1024]{3,2,1,0:T(8,128)(2,1)S(1)} collective-permute-done((bf16[2,2,80,1024]{3,2,1,0:T(8,128)(2,1)S(1)}, bf16[2,2,80,1024]{3,2,1,0:T(8,128)(2,1)S(1)}, u32[]{:S(2)}, u32[]{:S(2)}) %collective-permute-start.43) | collective-permute-done | bytes 655392 | tf_op jit(solution)/shard_map/ppermute | solution.py:383
  329.5 5.2 grad_attended.1
  334.7 8.5 %collective-permute-done.46 = bf16[4,320,640]{2,1,0:T(8,128)(2,1)} collective-permute-done((bf16[4,320,640]{2,1,0:T(8,128)(2,1)}, bf16[4,320,640]{2,1,0:T(8,128)(2,1)}, u32[]{:S(2)}, u32[]{:S(2)}) %collective-permute-start.46) | collective-permute-done | bytes 1638432 | tf_op jit(solution)/shard_map/ppermute | solution.py:375
  354.1 18.1 %attend_clip_back.1 = (bf16[4,2,80,1024]{3,2,1,0:T(8,128)(2,1)}, bf16[4,80,1024]{2,1,0:T(8,128)(2,1)}) custom-call(s32[1]{0:T(128)} %dynamic_slice.3.len_ref, bf16[4,2,80,1024]{3,2,1,0:T(8,128)(2,1)} %get-tuple-element.177.q_ref.k_ref, bf16[4,2,80,1024]{3,2,1,0:T(8,128)(2,1)} %get-tuple-element.177.q_ref.k_ref, ...), custom_call_target="tpu_custom_call" | custom-call | flops 1 | bytes 1 | tf_op jit(solution)/shard_map/attend_clip_back/pallas_call | solution.py:497
  379.4 7.8 %fold_project.1 = (f32[2,2,2,80,1024]{4,3,2,1,0:T(8,128)}, bf16[2,2,2,80,1024]{4,3,2,1,0:T(8,128)(2,1)}) custom-call(bf16[2,2,160,640]{3,2,1,0:T(8,128)(2,1)} %copy-done.19, bf16[2,2,160,640]{3,2,1,0:T(8,128)(2,1)} %copy-done.25, bf16[2,2,160,640]{3,2,1,0:T(8,128)(2,1)} %copy-done.2, bf16[2,2,160,640]{3,2,1,0:T(8,128)(2,1)} %copy-done.8, ...), custom_call_target="tpu_custom_call" | custom-call | flops 1 | bytes 1 | tf_op jit(solution)/shard_map/fold_project/pallas_call | solution.py:1050
  401.1 10.4 %grad_vo.1 = (f32[2,2,160,640]{3,2,1,0:T(8,128)}, bf16[2,2,160,640]{3,2,1,0:T(8,128)(2,1)}) custom-call(bf16[2,2,80,1024]{3,2,1,0:T(8,128)(2,1)} %bitcast.181, bf16[2,2,80,1024]{3,2,1,0:T(8,128)(2,1)} %bitcast.182, bf16[1280,1024]{1,0:T(8,128)(2,1)} %get-tuple-element.253.refs_2_.right_ref, bf16[1280,1024]{1,0:T(8,128)(2,1)} %get-tuple-element.254.refs_3_), custom_call_target="tpu_custom_call" | custom-call | flops 1 | bytes 1 | tf_op jit(solution)/shard_map/grad_vo/pallas_call | solution.py:1119
  412.6 6.7 %grad_qk.1 = (f32[4,160,640]{2,1,0:T(8,128)}, bf16[4,160,640]{2,1,0:T(8,128)(2,1)}) custom-call(bf16[4,160,1024]{2,1,0:T(8,128)(2,1)} %bitcast.180, bf16[1280,1024]{1,0:T(8,128)(2,1)} %get-tuple-element.253.refs_2_.right_ref), custom_call_target="tpu_custom_call" | custom-call | flops 1 | bytes 1 | tf_op jit(solution)/shard_map/grad_qk/pallas_call | solution.py:1088
  455.2 4.0 store_ff.1
  459.3 4.9 collective-permute-start.72
  470.2 11.8 %collective-permute-done.70 = bf16[160,640]{1,0:T(8,128)(2,1)S(1)} collective-permute-done((bf16[160,640]{1,0:T(8,128)(2,1)S(1)}, bf16[160,640]{1,0:T(8,128)(2,1)S(1)}, u32[]{:S(2)}, u32[]{:S(2)}) %collective-permute-start.70) | collective-permute-done | bytes 204832 | tf_op jit(solution)/shard_map/ppermute | solution.py:387
  502.9 3.9 finish.2
  515.8 3.9 finish.3
  (416 shorter events, 234.5 us)
Async XLA Ops:
  21.5 19.7 %collective-permute-start.11 = (f32[11,80]{1,0:T(8,128)S(1)}, f32[11,80]{1,0:T(8,128)S(1)}, u32[]{:S(2)}, u32[]{:S(2)}) collective-permute-start(f32[11,80]{1,0:T(8,128)S(1)} %get-tuple-element.345), channel_id=1, source_target_pairs={{0,1},{1,0},{2,3},{3,2},{4,5},{5,4},{6,7},{7,6},{8,9},{9,8},{10,11... | collective-permute-start | bytes 10568 | tf_op jit(solution)/shard_map/ppermute | solution.py:379
  70.7 21.5 %collective-permute-start.13 = (bf16[2,2,80,1024]{3,2,1,0:T(8,128)(2,1)}, bf16[2,2,80,1024]{3,2,1,0:T(8,128)(2,1)}, u32[]{:S(2)}, u32[]{:S(2)}) collective-permute-start(bf16[2,2,80,1024]{3,2,1,0:T(8,128)(2,1)} %add_convert_fusion.1.b0), channel_id=1, source_target_pairs={{0,8},{8,0},{16,24},{24,16},{1,9},{9,1},{17,25},{25,17},{2,10},{10... | collective-permute-start | bytes 1966088 | tf_op jit(solution)/shard_map/ppermute | solution.py:371
  72.6 23.1 %collective-permute-start.17 = (bf16[2,2,160,640]{3,2,1,0:T(8,128)(2,1)S(1)}, bf16[2,2,160,640]{3,2,1,0:T(8,128)(2,1)S(1)}, u32[]{:S(2)}, u32[]{:S(2)}) collective-permute-start(bf16[2,2,160,640]{3,2,1,0:T(8,128)(2,1)S(1)} %pad_maximum_fusion.3.qk0.refs_0_), channel_id=1, source_target_pairs={{0,16},{8,24},{16,0},{24,8},{1,17},{9,25},{17,1},{25,9},{2,18},{10... | collective-permute-start | bytes 2457608 | tf_op jit(solution)/shard_map/ppermute | solution.py:375
  87.5 29.9 %collective-permute-start.18 = (bf16[320,640]{1,0:T(8,128)(2,1)}, bf16[320,640]{1,0:T(8,128)(2,1)}, u32[]{:S(2)}, u32[]{:S(2)}) collective-permute-start(bf16[320,640]{1,0:T(8,128)(2,1)} %get-tuple-element.181), channel_id=1, source_target_pairs={{0,4},{1,5},{2,6},{3,7},{4,0},{5,1},{6,2},{7,3},{8,12},{9,13},{10,... | collective-permute-start | bytes 1228808 | tf_op jit(solution)/shard_map/ppermute | solution.py:387
  88.6 37.7 %collective-permute-start.19 = (bf16[320,640]{1,0:T(8,128)(2,1)}, bf16[320,640]{1,0:T(8,128)(2,1)}, u32[]{:S(2)}, u32[]{:S(2)}) collective-permute-start(bf16[320,640]{1,0:T(8,128)(2,1)} %get-tuple-element.171), channel_id=1, source_target_pairs={{0,4},{1,5},{2,6},{3,7},{4,0},{5,1},{6,2},{7,3},{8,12},{9,13},{10,... | collective-permute-start | bytes 1228808 | tf_op jit(solution)/shard_map/ppermute | solution.py:387
  92.1 34.1 %collective-permute-start.20 = (bf16[2,80,1024]{2,1,0:T(8,128)(2,1)}, bf16[2,80,1024]{2,1,0:T(8,128)(2,1)}, u32[]{:S(2)}, u32[]{:S(2)}) collective-permute-start(bf16[2,80,1024]{2,1,0:T(8,128)(2,1)} %get-tuple-element.182), channel_id=1, source_target_pairs={{0,1},{1,0},{2,3},{3,2},{4,5},{5,4},{6,7},{7,6},{8,9},{9,8},{10,11... | collective-permute-start | bytes 983048 | tf_op jit(solution)/shard_map/ppermute | solution.py:379
  137.9 24.5 %collective-permute-start.24 = (bf16[2,320,640]{2,1,0:T(8,128)(2,1)}, bf16[2,320,640]{2,1,0:T(8,128)(2,1)S(1)}, u32[]{:S(2)}, u32[]{:S(2)}) collective-permute-start(bf16[2,320,640]{2,1,0:T(8,128)(2,1)} %get-tuple-element.308), channel_id=1, source_target_pairs={{0,16},{8,24},{16,0},{24,8},{1,17},{9,25},{17,1},{25,9},{2,18},{10... | collective-permute-start | bytes 2457608 | tf_op jit(solution)/shard_map/ppermute | solution.py:375
  139.1 23.3 %collective-permute-start.23 = (bf16[2,320,640]{2,1,0:T(8,128)(2,1)S(1)}, bf16[2,320,640]{2,1,0:T(8,128)(2,1)S(1)}, u32[]{:S(2)}, u32[]{:S(2)}) collective-permute-start(bf16[2,320,640]{2,1,0:T(8,128)(2,1)S(1)} %get-tuple-element.346), channel_id=1, source_target_pairs={{0,1},{1,0},{2,3},{3,2},{4,5},{5,4},{6,7},{7,6},{8,9},{9,8},{10,11... | collective-permute-start | bytes 2457608 | tf_op jit(solution)/shard_map/ppermute | solution.py:379
  141.3 23.0 %collective-permute-start.22 = (bf16[2,2,80,1024]{3,2,1,0:T(8,128)(2,1)S(1)}, bf16[2,2,80,1024]{3,2,1,0:T(8,128)(2,1)S(1)}, u32[]{:S(2)}, u32[]{:S(2)}) collective-permute-start(bf16[2,2,80,1024]{3,2,1,0:T(8,128)(2,1)S(1)} %fusion.12), channel_id=1, source_target_pairs={{0,2},{1,3},{2,0},{3,1},{4,6},{5,7},{6,4},{7,5},{8,10},{9,11},{10,... | collective-permute-start | bytes 1966088 | tf_op jit(solution)/shard_map/ppermute | solution.py:383
  141.4 21.0 %collective-permute-start.25 = (bf16[2,80,1024]{2,1,0:T(8,128)(2,1)S(1)}, bf16[2,80,1024]{2,1,0:T(8,128)(2,1)S(1)}, u32[]{:S(2)}, u32[]{:S(2)}) collective-permute-start(bf16[2,80,1024]{2,1,0:T(8,128)(2,1)S(1)} %pad_maximum_fusion.9), channel_id=1, source_target_pairs={{0,4},{1,5},{2,6},{3,7},{4,0},{5,1},{6,2},{7,3},{8,12},{9,13},{10,... | collective-permute-start | bytes 983048 | tf_op jit(solution)/shard_map/ppermute | solution.py:387
  167.9 36.8 %collective-permute-start.32 = (bf16[2,2,320,640]{3,2,1,0:T(8,128)(2,1)}, bf16[2,2,320,640]{3,2,1,0:T(8,128)(2,1)}, u32[]{:S(2)}, u32[]{:S(2)}) collective-permute-start(bf16[2,2,320,640]{3,2,1,0:T(8,128)(2,1)} %pad_maximum_fusion.1.up0.refs_0_), channel_id=1, source_target_pairs={{0,16},{8,24},{16,0},{24,8},{1,17},{9,25},{17,1},{25,9},{2,18},{10... | collective-permute-start | bytes 4915208 | tf_op jit(solution)/shard_map/ppermute | solution.py:375
  170.9 44.2 %collective-permute-start.26 = (bf16[2,2,320,640]{3,2,1,0:T(8,128)(2,1)}, bf16[2,2,320,640]{3,2,1,0:T(8,128)(2,1)}, u32[]{:S(2)}, u32[]{:S(2)}) collective-permute-start(bf16[2,2,320,640]{3,2,1,0:T(8,128)(2,1)} %pad_maximum_fusion.refs_0_.down0), channel_id=1, source_target_pairs={{0,1},{1,0},{2,3},{3,2},{4,5},{5,4},{6,7},{7,6},{8,9},{9,8},{10,11... | collective-permute-start | bytes 4915208 | tf_op jit(solution)/shard_map/ppermute | solution.py:379
  172.7 21.3 %collective-permute-start.29 = (bf16[2,2,80,1024]{3,2,1,0:T(8,128)(2,1)S(1)}, bf16[2,2,80,1024]{3,2,1,0:T(8,128)(2,1)}, u32[]{:S(2)}, u32[]{:S(2)}) collective-permute-start(bf16[2,2,80,1024]{3,2,1,0:T(8,128)(2,1)S(1)} %add_convert_fusion.b0), channel_id=1, source_target_pairs={{0,8},{8,0},{16,24},{24,16},{1,9},{9,1},{17,25},{25,17},{2,10},{10... | collective-permute-start | bytes 1966088 | tf_op jit(solution)/shard_map/ppermute | solution.py:371
  227.2 19.2 %collective-permute-start.34 = (bf16[2,2,80,1024]{3,2,1,0:T(8,128)(2,1)S(1)}, bf16[2,2,80,1024]{3,2,1,0:T(8,128)(2,1)S(1)}, u32[]{:S(2)}, u32[]{:S(2)}) collective-permute-start(bf16[2,2,80,1024]{3,2,1,0:T(8,128)(2,1)S(1)} %copy-done.11), channel_id=1, source_target_pairs={{0,8},{8,0},{16,24},{24,16},{1,9},{9,1},{17,25},{25,17},{2,10},{10... | collective-permute-start | bytes 1966088 | tf_op jit(solution)/shard_map/ppermute | solution.py:371
  306.1 37.0 %collective-permute-start.46 = (bf16[4,320,640]{2,1,0:T(8,128)(2,1)}, bf16[4,320,640]{2,1,0:T(8,128)(2,1)}, u32[]{:S(2)}, u32[]{:S(2)}) collective-permute-start(bf16[4,320,640]{2,1,0:T(8,128)(2,1)} %get-tuple-element.220), channel_id=1, source_target_pairs={{0,16},{8,24},{16,0},{24,8},{1,17},{9,25},{17,1},{25,9},{2,18},{10... | collective-permute-start | bytes 4915208 | tf_op jit(solution)/shard_map/ppermute | solution.py:375
  307.3 36.8 %collective-permute-start.45 = (bf16[2,2,320,640]{3,2,1,0:T(8,128)(2,1)}, bf16[2,2,320,640]{3,2,1,0:T(8,128)(2,1)}, u32[]{:S(2)}, u32[]{:S(2)}) collective-permute-start(bf16[2,2,320,640]{3,2,1,0:T(8,128)(2,1)} %get-tuple-element.217), channel_id=1, source_target_pairs={{0,1},{1,0},{2,3},{3,2},{4,5},{5,4},{6,7},{7,6},{8,9},{9,8},{10,11... | collective-permute-start | bytes 4915208 | tf_op jit(solution)/shard_map/ppermute | solution.py:379
  351.5 20.7 %collective-permute-start.48 = (bf16[2,320,640]{2,1,0:T(8,128)(2,1)S(1)}, bf16[2,320,640]{2,1,0:T(8,128)(2,1)}, u32[]{:S(2)}, u32[]{:S(2)}) collective-permute-start(bf16[2,320,640]{2,1,0:T(8,128)(2,1)S(1)} %slice.525), channel_id=1, source_target_pairs={{0,1},{1,0},{2,3},{3,2},{4,5},{5,4},{6,7},{7,6},{8,9},{9,8},{10,11... | collective-permute-start | bytes 2457608 | tf_op jit(solution)/shard_map/ppermute | solution.py:379
  351.8 20.5 %collective-permute-start.47 = (bf16[2,320,640]{2,1,0:T(8,128)(2,1)S(1)}, bf16[2,320,640]{2,1,0:T(8,128)(2,1)}, u32[]{:S(2)}, u32[]{:S(2)}) collective-permute-start(bf16[2,320,640]{2,1,0:T(8,128)(2,1)S(1)} %fusion.7), channel_id=1, source_target_pairs={{0,16},{8,24},{16,0},{24,8},{1,17},{9,25},{17,1},{25,9},{2,18},{10... | collective-permute-start | bytes 2457608 | tf_op jit(solution)/shard_map/ppermute | solution.py:375
  352.1 20.1 %collective-permute-start.49 = (bf16[2,80,1024]{2,1,0:T(8,128)(2,1)}, bf16[2,80,1024]{2,1,0:T(8,128)(2,1)S(1)}, u32[]{:S(2)}, u32[]{:S(2)}) collective-permute-start(bf16[2,80,1024]{2,1,0:T(8,128)(2,1)} %get-tuple-element.228), channel_id=1, source_target_pairs={{0,4},{1,5},{2,6},{3,7},{4,0},{5,1},{6,2},{7,3},{8,12},{9,13},{10,... | collective-permute-start | bytes 983048 | tf_op jit(solution)/shard_map/ppermute | solution.py:387
  391.4 27.8 %collective-permute-start.50 = (bf16[2,80,1024]{2,1,0:T(8,128)(2,1)}, bf16[2,80,1024]{2,1,0:T(8,128)(2,1)}, u32[]{:S(2)}, u32[]{:S(2)}) collective-permute-start(bf16[2,80,1024]{2,1,0:T(8,128)(2,1)} %pad_maximum_fusion.10), channel_id=1, source_target_pairs={{0,1},{1,0},{2,3},{3,2},{4,5},{5,4},{6,7},{7,6},{8,9},{9,8},{10,11... | collective-permute-start | bytes 983048 | tf_op jit(solution)/shard_map/ppermute | solution.py:379
  397.1 28.6 %collective-permute-start.53 = (bf16[2,2,80,1024]{3,2,1,0:T(8,128)(2,1)}, bf16[2,2,80,1024]{3,2,1,0:T(8,128)(2,1)}, u32[]{:S(2)}, u32[]{:S(2)}) collective-permute-start(bf16[2,2,80,1024]{3,2,1,0:T(8,128)(2,1)} %fusion.15), channel_id=1, source_target_pairs={{0,2},{1,3},{2,0},{3,1},{4,6},{5,7},{6,4},{7,5},{8,10},{9,11},{10,... | collective-permute-start | bytes 1966088 | tf_op jit(solution)/shard_map/ppermute | solution.py:383
  398.7 44.2 %collective-permute-start.60 = (bf16[320,640]{1,0:T(8,128)(2,1)}, bf16[320,640]{1,0:T(8,128)(2,1)}, u32[]{:S(2)}, u32[]{:S(2)}) collective-permute-start(bf16[320,640]{1,0:T(8,128)(2,1)} %fusion.17), channel_id=1, source_target_pairs={{0,4},{1,5},{2,6},{3,7},{4,0},{5,1},{6,2},{7,3},{8,12},{9,13},{10,... | collective-permute-start | bytes 1228808 | tf_op jit(solution)/shard_map/ppermute | solution.py:387
  400.0 44.4 %collective-permute-start.59 = (bf16[320,640]{1,0:T(8,128)(2,1)}, bf16[320,640]{1,0:T(8,128)(2,1)}, u32[]{:S(2)}, u32[]{:S(2)}) collective-permute-start(bf16[320,640]{1,0:T(8,128)(2,1)} %fusion.16), channel_id=1, source_target_pairs={{0,4},{1,5},{2,6},{3,7},{4,0},{5,1},{6,2},{7,3},{8,12},{9,13},{10,... | collective-permute-start | bytes 1228808 | tf_op jit(solution)/shard_map/ppermute | solution.py:387
  411.5 33.0 %collective-permute-start.57 = (bf16[2,2,160,640]{3,2,1,0:T(8,128)(2,1)}, bf16[2,2,160,640]{3,2,1,0:T(8,128)(2,1)}, u32[]{:S(2)}, u32[]{:S(2)}) collective-permute-start(bf16[2,2,160,640]{3,2,1,0:T(8,128)(2,1)} %get-tuple-element.255), channel_id=1, source_target_pairs={{0,1},{1,0},{2,3},{3,2},{4,5},{5,4},{6,7},{7,6},{8,9},{9,8},{10,11... | collective-permute-start | bytes 2457608 | tf_op jit(solution)/shard_map/ppermute | solution.py:379
  419.3 25.2 %collective-permute-start.58 = (bf16[4,160,640]{2,1,0:T(8,128)(2,1)}, bf16[4,160,640]{2,1,0:T(8,128)(2,1)}, u32[]{:S(2)}, u32[]{:S(2)}) collective-permute-start(bf16[4,160,640]{2,1,0:T(8,128)(2,1)} %get-tuple-element.257), channel_id=1, source_target_pairs={{0,16},{8,24},{16,0},{24,8},{1,17},{9,25},{17,1},{25,9},{2,18},{10... | collective-permute-start | bytes 2457608 | tf_op jit(solution)/shard_map/ppermute | solution.py:375
  437.6 53.1 %collective-permute-start.65 = (f32[2,960]{1,0:T(2,128)S(1)}, f32[2,960]{1,0:T(2,128)S(1)}, u32[]{:S(2)}, u32[]{:S(2)}) collective-permute-start(f32[2,960]{1,0:T(2,128)S(1)} %fusion.26), channel_id=1, source_target_pairs={{0,4},{1,5},{2,6},{3,7},{4,0},{5,1},{6,2},{7,3},{8,12},{9,13},{10,... | collective-permute-start | bytes 23048 | tf_op jit(solution)/shard_map/ppermute | solution.py:387
  442.9 21.3 %collective-permute-start.56 = (bf16[2,80,1024]{2,1,0:T(8,128)(2,1)}, bf16[2,80,1024]{2,1,0:T(8,128)(2,1)}, u32[]{:S(2)}, u32[]{:S(2)}) collective-permute-start(bf16[2,80,1024]{2,1,0:T(8,128)(2,1)} %get-tuple-element.263), channel_id=1, source_target_pairs={{0,4},{1,5},{2,6},{3,7},{4,0},{5,1},{6,2},{7,3},{8,12},{9,13},{10,... | collective-permute-start | bytes 983048 | tf_op jit(solution)/shard_map/ppermute | solution.py:387
  459.3 52.9 %collective-permute-start.72 = (f32[320,640]{1,0:T(8,128)}, f32[320,640]{1,0:T(8,128)}, u32[]{:S(2)}, u32[]{:S(2)}) collective-permute-start(f32[320,640]{1,0:T(8,128)} %get-tuple-element.271), channel_id=1, source_target_pairs={{0,8},{8,0},{16,24},{24,16},{1,9},{9,1},{17,25},{25,17},{2,10},{10... | collective-permute-start | bytes 2457608 | tf_op jit(solution)/shard_map/ppermute | solution.py:371
  467.4 19.0 %collective-permute-start.69 = (bf16[160,640]{1,0:T(8,128)(2,1)S(1)}, bf16[160,640]{1,0:T(8,128)(2,1)S(1)}, u32[]{:S(2)}, u32[]{:S(2)}) collective-permute-start(bf16[160,640]{1,0:T(8,128)(2,1)S(1)} %fusion.21), channel_id=1, source_target_pairs={{0,4},{1,5},{2,6},{3,7},{4,0},{5,1},{6,2},{7,3},{8,12},{9,13},{10,... | collective-permute-start | bytes 614408 | tf_op jit(solution)/shard_map/ppermute | solution.py:387
  469.9 21.0 %collective-permute-start.63 = (bf16[2,80,1024]{2,1,0:T(8,128)(2,1)S(1)}, bf16[2,80,1024]{2,1,0:T(8,128)(2,1)S(1)}, u32[]{:S(2)}, u32[]{:S(2)}) collective-permute-start(bf16[2,80,1024]{2,1,0:T(8,128)(2,1)S(1)} %pad_maximum_fusion.11), channel_id=1, source_target_pairs={{0,1},{1,0},{2,3},{3,2},{4,5},{5,4},{6,7},{7,6},{8,9},{9,8},{10,11... | collective-permute-start | bytes 983048 | tf_op jit(solution)/shard_map/ppermute | solution.py:379
  490.7 29.0 %collective-permute-start.71 = (f32[320,384]{1,0:T(8,128)}, f32[320,384]{1,0:T(8,128)S(1)}, u32[]{:S(2)}, u32[]{:S(2)}) collective-permute-start(f32[320,384]{1,0:T(8,128)} %get-tuple-element.281), channel_id=1, source_target_pairs={{0,8},{8,0},{16,24},{24,16},{1,9},{9,1},{17,25},{25,17},{2,10},{10... | collective-permute-start | bytes 1474568 | tf_op jit(solution)/shard_map/ppermute | solution.py:371
  493.7 21.4 %collective-permute-start.64 = (bf16[80,2048]{1,0:T(8,128)(2,1)}, bf16[80,2048]{1,0:T(8,128)(2,1)S(1)}, u32[]{:S(2)}, u32[]{:S(2)}) collective-permute-start(bf16[80,2048]{1,0:T(8,128)(2,1)} %get-tuple-element.277), channel_id=1, source_target_pairs={{0,8},{8,0},{16,24},{24,16},{1,9},{9,1},{17,25},{25,17},{2,10},{10... | collective-permute-start | bytes 983048 | tf_op jit(solution)/shard_map/ppermute | solution.py:371
  (110 other events, 896.4 us)

commit v2 on v1

--- a/solution.py
+++ b/solution.py
@@ -458,12 +458,11 @@
 
 
 def attend_back_kernel(
-    len_ref, q_ref, k_ref, v_ref, lse_ref, grad_ref, gqk_ref, gv_ref, ksum_ref, vsum_ref
+    len_ref, q_ref, k_ref, v_ref, lse_ref, grad_ref, *refs
 ):
-    step = pl.program_id(1)
+    gqk_ref, gv_ref = refs[-2:]
     scale = HEAD_DIM**-0.5
     queries, keys, values, grad = q_ref[...], k_ref[...], v_ref[...], grad_ref[...]
-    block = queries.shape[1]
     scores = mm(keys, queries, 0, 0) * scale
     live = lax.broadcasted_iota(jnp.int32, scores.shape, 0) < len_ref[0]
     scores = jnp.where(live, scores, -1e30)
@@ -474,46 +473,41 @@
     grad_query = mm(keys, score_low, 1, 0) * scale
     grad_key = mm(queries, score_low, 1, 1)
     grad_value = mm(grad, probs.astype(BF), 1, 1)
-    start = pl.multiple_of(step * block, block)
-    gqk_ref[0, :, pl.ds(start, block)] = grad_query.astype(BF)
-
-    @pl.when(step == 0)
-    def _():
-        ksum_ref[...] = grad_key
-        vsum_ref[...] = grad_value
-
-    @pl.when(step > 0)
-    def _():
-        ksum_ref[...] += grad_key
-        vsum_ref[...] += grad_value
-
-    @pl.when(step == pl.num_programs(1) - 1)
-    def _():
-        gqk_ref[1] = (ksum_ref[...] * scale).astype(BF)
-        gv_ref[...] = vsum_ref[...].astype(BF)
-
-
-def attend_clip_back(qk, values, log_sum, grad_attended, clip_len, block):
+    gqk_ref[0] = grad_query.astype(BF)
+    gqk_ref[1] = (grad_key * scale).astype(BF)
+    gv_ref[...] = grad_value.astype(BF)
+
+
+def attend_clip_back(qk, values, log_sum, grad_attended, clip_len, first, earlier=()):
+    def heads(*dims):
+        return pl.BlockSpec(
+            (None,) + dims, lambda h, n: (h + first,) + (0,) * len(dims)
+        )
+
+    def part(i):
+        return pl.BlockSpec((None, None, HEAD_DIM, CLIP), lambda h, n: (h + first, i, 0, 0))
+
+    operands = (qk, qk, values, log_sum, grad_attended)
     return pl.pallas_call(
         attend_back_kernel,
         grid_spec=pltpu.PrefetchScalarGridSpec(
             num_scalar_prefetch=1,
-            grid=(4, CLIP // block),
-            in_specs=head_specs(block)
-            + [
-                pl.BlockSpec((None, 1, block), lambda h, i, n: (h, 0, i)),
-                pl.BlockSpec((None, HEAD_DIM, block), lambda h, i, n: (h, 0, i)),
-            ],
-            out_specs=[
-                pl.BlockSpec((None, 2, HEAD_DIM, CLIP), lambda h, i, n: (h, 0, 0, 0)),
-                pl.BlockSpec((None, HEAD_DIM, CLIP), lambda h, i, n: (h, 0, 0)),
-            ],
-            scratch_shapes=[pltpu.VMEM((HEAD_DIM, CLIP), F32)] * 2,
+            grid=(2,),
+            in_specs=[
+                part(0),
+                part(1),
+                heads(HEAD_DIM, CLIP),
+                heads(1, CLIP),
+                heads(HEAD_DIM, CLIP),
+            ]
+            + [pl.BlockSpec(memory_space=pl.ANY)] * len(earlier),
+            out_specs=[heads(2, HEAD_DIM, CLIP), heads(HEAD_DIM, CLIP)],
         ),
         out_shape=[shaped((4, 2, HEAD_DIM, CLIP)), shaped((4, HEAD_DIM, CLIP))],
-        cost_estimate=cost(40 * CLIP * CLIP * HEAD_DIM, 32 * HEAD_DIM * CLIP * 2),
+        input_output_aliases={6: 0, 7: 1} if earlier else {},
+        cost_estimate=cost(20 * CLIP * CLIP * HEAD_DIM, 16 * HEAD_DIM * CLIP * 2),
         name="attend_clip_back",
-    )(clip_len, qk, qk, values, log_sum, grad_attended)
+    )(clip_len, *operands, *earlier)
 
 
 WIDE = 384
@@ -802,14 +796,12 @@
 
 def place(spots, here, there, far, with_stats):
     rows = here.shape[1]
-    spec = pl.BlockSpec((2, rows, BLOCK), lambda i: (0, 0, i))
     own = (2, 2, HEAD_DIM, CLIP)
     outs = [(own, F32), ((2, CLIP), F32)] if with_stats else [(own, BF)]
     return pl.pallas_call(
         place_kernel,
-        grid=(STEPS,),
-        in_specs=[spots_spec()] + [spec] * 3,
-        out_specs=[tokens_spec(dims) for dims, _ in outs],
+        in_specs=[spots_spec()] + [whole()] * 3,
+        out_specs=[whole()] * len(outs),
         out_shape=[shaped(dims, kind) for dims, kind in outs],
         cost_estimate=cost(0, 8 * rows * CLIP * 6),
         name="place_in",
@@ -832,9 +824,8 @@
     dims = (2, HEAD_DIM, CLIP)
     return pl.pallas_call(
         leave_kernel,
-        grid=(STEPS,),
-        in_specs=[spots_spec(), tokens_spec(own.shape)],
-        out_specs=[tokens_spec(dims)] * 2,
+        in_specs=[spots_spec(), whole()],
+        out_specs=[whole()] * 2,
         out_shape=[shaped(dims)] * 2,
         cost_estimate=cost(0, 4 * HEAD_DIM * CLIP * 6),
         name="leave",
@@ -1039,9 +1030,9 @@
             part = result[spot * HEAD_DIM : (spot + 1) * HEAD_DIM]
             zlr, xr, cr = spot >> 2, spot >> 1 & 1, spot & 1
             if cr == 0:
-                keep_ref[yr, zlr, xr] = part
+                keep_ref[zlr, yr, xr] = part
             else:
-                send_ref[yr, zlr, xr] = part.astype(BF)
+                send_ref[zlr, yr, xr] = part.astype(BF)
 
 
 def fold(fill, sources, values, name):
@@ -1134,12 +1125,20 @@
     return jnp.stack([mean, jnp.sum(off * off, axis=0)])
 
 
-def merge_stats(stats, count, swap):
-    other = swap(stats)
-    apart = other[0] - stats[0]
-    return jnp.stack(
-        [0.5 * (stats[0] + other[0]), stats[1] + other[1] + apart * apart * (0.5 * count)]
-    )
+def swap_both(values):
+    route = [(8 * r + q, 8 * (r ^ 1) + (q ^ 2)) for r in range(4) for q in range(8)]
+    return lax.ppermute(values, ("row", "col"), route)
+
+
+def group_round(values):
+    return values, swap_core(values), swap_zl(values), swap_both(values)
+
+
+def merge_stats(stats, count):
+    stats = group_round(stats)
+    mean = sum(s[0] for s in stats) * 0.25
+    total = sum(s[1] + count * jnp.square(s[0] - mean) for s in stats)
+    return mean, total / (4 * count)
 
 
 def after(values, *others):
@@ -1174,8 +1173,8 @@
         return jnp.where(x == 0, grid, grid[:, ::-1])
 
     def fold_cores(parts):
-        keep = parts[0] + swap_core(parts[1])
-        return keep[:, 0], keep[:, 1].astype(BF)
+        got = swap_core(parts[1])
+        return parts[0][0] + got[0], (parts[0][1] + got[1]).astype(BF)
 
     kept, sent = prepare(
         spots,
@@ -1189,6 +1188,8 @@
     h_here, h_send = deal(spots, h_kept, swap_core(h_sent))
     s_qk, s_vo, s_up, s_down = join_lanes(spots, kept, weights_got)
     h_there = swap_x(h_send)
+    c_here, c_send = deal(spots, c_kept, swap_core(after(c_sent, h_send)))
+    c_there = swap_x(after(c_send, h_there))
     qk_zh, vo_zh = swap_zh(s_qk), swap_zh(s_vo)
 
     pack = jnp.stack(
@@ -1201,86 +1202,81 @@
     pack = jnp.stack([pack, swap_zh(pack)])
 
     h_message = jnp.stack([h_here[1], h_there[1]])
-    h_message, qk_zh, vo_zh = lax.optimization_barrier((h_message, qk_zh, vo_zh))
-    h_far = swap_zh(h_message)
+    h_far = swap_zh(after(h_message, c_send))
     qk_one = jnp.stack([s_qk, qk_zh])
     vo_one = jnp.stack([s_vo, vo_zh])
     qk_two, vo_two = swap_x(qk_one), swap_y(vo_one)
-    h_far, qk_two, vo_two = lax.optimization_barrier((h_far, qk_two, vo_two))
+    h_far = after(h_far, qk_one, vo_one)
+    s_up, s_down = after((s_up, s_down), h_far)
+
+    owned = flip(pack)
+    gain_one, shift_one, gain_two, shift_two, out_shift = (
+        owned[:, :, i, :, None] for i in range(5)
+    )
+    by_head = pack.transpose(1, 0, 2, 3)
+    q_shift = by_head[:, :, 5].reshape(4, HEAD_DIM, 1)
+    v_shift = by_head[:, :, 6].reshape(4, HEAD_DIM, 1)
+    in_shift = by_head[:, :, 7:].reshape(UNITS, 1)
+
+    hidden_own, stats = place(spots, h_here, h_there, h_far, True)
+    mean, variance = merge_stats(stats, OWN)
+    inv_one = lax.rsqrt(variance + EPS)
+    inv_one, qk_two, vo_two, c_there = lax.optimization_barrier(
+        (inv_one, qk_two, vo_two, c_there)
+    )
+    own_one = (hidden_own - mean) * inv_one
     w_qk = jnp.stack([qk_one, qk_two])
     w_vo = jnp.stack([vo_one, vo_two])
     w_qk = w_qk, swap_y(w_qk)
     w_vo = w_vo, swap_x(w_vo)
-    s_up = after(s_up, h_far)
     up_zh = swap_zh(s_up)
-
-    owned = flip(pack)
-    gain_one, shift_one, gain_two, shift_two, out_shift = (
-        owned[:, :, i, :, None] for i in range(5)
-    )
-    by_head = pack.transpose(1, 0, 2, 3)
-    q_shift = by_head[:, :, 5].reshape(4, HEAD_DIM, 1)
-    v_shift = by_head[:, :, 6].reshape(4, HEAD_DIM, 1)
-    in_shift = by_head[:, :, 7:].reshape(UNITS, 1)
-
-    hidden_own, stats = place(spots, h_here, h_there, h_far, True)
-    stats = merge_stats(stats, OWN, swap_core)
-    stats = merge_stats(stats, 2 * OWN, swap_zl)
-    inv_one = lax.rsqrt(stats[1] / D + EPS)
-    own_one = (hidden_own - stats[0]) * inv_one
     low_one = (own_one * gain_one + shift_one).astype(BF)
     low_one_z = swap_zl(low_one)
-    s_down = after(s_down, low_one_z)
+    low_one_z, up_zh = lax.optimization_barrier((low_one_z, up_zh))
+    s_down = after(s_down, up_zh)
     down_zh = swap_zh(s_down)
-    c_here, c_send = deal(spots, c_kept, swap_core(after(c_sent, low_one)))
-    c_there = swap_x(after(c_send, w_vo[1]))
+    up_one = jnp.stack([s_up, up_zh])
+    up_two = swap_x(after(up_one, w_vo[1]))
     wide_one = low_one, swap_core(low_one), low_one_z, swap_core(low_one_z)
-    wide_one = after(wide_one, c_send, s_down)
+    wide_one = after(wide_one, up_one, s_down)
 
     qk, values, ln_one = project(wide_one, w_qk, w_vo, q_shift, v_shift)
     clip_len = lax.dynamic_slice_in_dim(lengths, 4 * y + 2 * zh + x, 1)
-    attended, log_sum = attend_clip(qk, values, clip_len, CLIP)
-    attended, up_zh, down_zh, c_there = lax.optimization_barrier(
-        (attended, up_zh, down_zh, c_there)
-    )
-    up_one = jnp.stack([s_up, up_zh])
+    qk, down_zh = lax.optimization_barrier((qk, down_zh))
     down_one = jnp.stack([s_down, down_zh])
-    c_message = jnp.stack([c_here[1], c_there[1]])
-    up_two, down_two, c_far = swap_x(up_one), swap_y(down_one), swap_zh(c_message)
-    delta_near, delta_send = fold_cores(
-        fold(fill_out, w_vo, (after(attended, up_one, down_one, c_message),), "fold_out")
-    )
-    delta_got = swap_zl(delta_send)
-    delta_got, up_two, down_two, c_far = lax.optimization_barrier(
-        (delta_got, up_two, down_two, c_far)
-    )
-    delta_mid = delta_near + delta_got + out_shift
+    c_message = after(jnp.stack([c_here[1], c_there[1]]), down_zh)
+    down_two, c_far = swap_y(down_one), swap_zh(c_message)
+    attended, log_sum = attend_clip(after(qk, down_one, c_message), values, clip_len, CLIP)
+    delta = fold(fill_out, w_vo, (attended,), "fold_out")
+    *delta, up_two, down_two, c_far = lax.optimization_barrier(
+        (*delta, up_two, down_two, c_far)
+    )
     w_up = jnp.stack([up_one, up_two])
     w_down = jnp.stack([down_one, down_two])
     w_up = w_up, swap_y(w_up)
     w_down = w_down, swap_x(w_down)
+    delta_near, delta_send = fold_cores(delta)
+    delta_mid = delta_near + swap_zl(delta_send) + out_shift
 
     hidden_mid = hidden_own + delta_mid
-    stats = token_stats(hidden_mid.reshape(OWN, CLIP))
-    stats = merge_stats(stats, OWN, swap_core)
-    stats = merge_stats(stats, 2 * OWN, swap_zl)
-    inv_two = lax.rsqrt(stats[1] / D + EPS)
-    own_two = (hidden_mid - stats[0]) * inv_two
+    mean, variance = merge_stats(token_stats(hidden_mid.reshape(OWN, CLIP)), OWN)
+    inv_two = lax.rsqrt(variance + EPS)
+    own_two = (hidden_mid - mean) * inv_two
     low_two = (own_two * gain_two + shift_two).astype(BF)
     low_two_z = swap_zl(low_two)
     (cot_own,) = place(spots, c_here, c_there, after(c_far, low_two), False)
     cot_own = after(cot_own, low_two_z)
     cot_z = swap_zl(cot_own)
-    wide_cot = cot_own, swap_core(cot_own), cot_z, swap_core(cot_z)
     wide_two = low_two, swap_core(low_two), low_two_z, swap_core(low_two_z)
     act_low, slope, ln_two = up_project(after(wide_two, cot_own), w_up, in_shift)
+    act_low, slope, cot_z = lax.optimization_barrier((act_low, slope, cot_z))
+    wide_cot = cot_own, swap_core(cot_own), cot_z, swap_core(cot_z)
     out_near, out_send = fold_cores(fold(fill_down, w_down, (act_low,), "fold_down"))
-    out_send = after(out_send, cot_z)
     out_got = swap_zl(out_send)
 
     grad_pre, cot_all = grad_act(after(wide_cot, out_send), w_down, slope)
-    two_near, two_send = fold_cores(fold(fill_up, w_up, (grad_pre,), "fold_up"))
-    two_send, out_got = lax.optimization_barrier((two_send, out_got))
+    grad_pre_fold, out_got = lax.optimization_barrier((grad_pre, out_got))
+    two_near, two_send = fold_cores(fold(fill_up, w_up, (grad_pre_fold,), "fold_up"))
     two_got = swap_zl(two_send)
     by_unit = (2, 2, OWN, CLIP)
     act_low_after, cot_all_after = after((act_low, cot_all), two_send)
@@ -1293,14 +1289,13 @@
     two_got = after(two_got, part_up[1])
     grad_two = two_near + two_got
 
-    def norm_back(grad, normed, inv, gain):
+    def norm_back(grad, normed, inv, gain, meanwhile=()):
         scaled = grad * gain
         sums = jnp.stack([jnp.sum(scaled, axis=(0, 1, 2)), jnp.sum(scaled * normed, axis=(0, 1, 2))])
-        sums = sums + swap_core(sums)
-        sums = (sums + swap_zl(sums)) / D
-        return inv * (scaled - sums[0] - normed * sums[1])
-
-    norm_two_grad = norm_back(grad_two, own_two, inv_two, gain_two)
+        sums, meanwhile = lax.optimization_barrier((sum(group_round(sums)) / D, meanwhile))
+        return inv * (scaled - sums[0] - normed * sums[1]), meanwhile
+
+    norm_two_grad, _ = norm_back(grad_two, own_two, inv_two, gain_two)
     mid_own = cot_own.astype(F32) + norm_two_grad
     mid_low = mid_own.astype(BF)
     mid_z = swap_zl(mid_low)
@@ -1319,75 +1314,70 @@
         return keep[0], keep[1].astype(BF)
 
     grad_attended, mid_all = grad_attended_of(wide_mid, w_vo)
-    grad_attended, down_first, up_first = lax.optimization_barrier(
-        (grad_attended, down_first, up_first)
-    )
+    early = attend_clip_back(qk, values, log_sum, grad_attended, clip_len, 0)
+    *early, down_first, up_first = lax.optimization_barrier((*early, down_first, up_first))
     down_keep, down_send = second_step(part_down[0], down_first)
     up_keep, up_send = second_step(part_up[0], up_first)
     down_second, up_second = swap_y(down_send), swap_x(up_send)
     grad_attended = after(grad_attended, down_send, up_send)
-    grad_qk, grad_v = attend_clip_back(qk, values, log_sum, grad_attended, clip_len, CLIP)
-    grad_qk, grad_v, down_second, up_second, out_far = lax.optimization_barrier(
-        (grad_qk, grad_v, down_second, up_second, out_far)
+    grad_qk, grad_v = attend_clip_back(
+        qk, values, log_sum, grad_attended, clip_len, 2, tuple(early)
+    )
+    grad_qk, grad_v, out_far = lax.optimization_barrier((grad_qk, grad_v, out_far))
+    out_message = jnp.stack([out_leave[1], out_far[1]])
+    out_there = swap_x(out_message)
+    folded = fold(
+        fill_project, (*w_qk, *w_vo), after((grad_qk, grad_v), out_message), "fold_project"
+    )
+    *folded, down_second, up_second = lax.optimization_barrier(
+        (*folded, down_second, up_second)
     )
     down_keep, down_send = third_step(down_keep, down_second)
     up_keep, up_send = third_step(up_keep, up_second)
     down_third, up_third = swap_zh(down_send), swap_zh(up_send)
-    out_message = jnp.stack([out_leave[1], out_far[1]])
-    out_there = swap_x(out_message)
-    folded = fold(
-        fill_project,
-        (*w_qk, *w_vo),
-        after((grad_qk, grad_v), down_send, up_send, out_message),
-        "fold_project",
-    )
     one_near, one_send = fold_cores(folded)
     one_got = swap_zl(one_send)
     by_head_dims = (2, 2, HEAD_DIM, CLIP)
-    grad_v, grad_qk = after((grad_v, grad_qk), one_send)
+    grad_v, grad_qk = after((grad_v, grad_qk), one_send, down_send, up_send)
     part_vo = grad_x_first(
         (grad_v.reshape(by_head_dims), attended.reshape(by_head_dims)),
         (ln_one, mid_all),
         "grad_vo",
     )
+    *part_vo, one_got = lax.optimization_barrier((*part_vo, one_got))
     vo_first = swap_x(part_vo[1])
     part_qk = grad_y_first(
         after(grad_qk, part_vo[1]).reshape(4, 2 * HEAD_DIM, CLIP), ln_one, "grad_qk"
     )
+    *part_qk, down_third = lax.optimization_barrier((*part_qk, down_third))
     qk_first = swap_y(part_qk[1])
     out_kept, out_sent = undeal(spots, out_leave, out_far, after(out_there, part_qk[1]))
     hidden_out = finish(spots, out_kept, swap_core(out_sent), hidden_in, down_bias[:, None])
 
-    one_got = after(one_got, out_sent)
     grad_one = one_near + one_got
-    norm_one_grad = norm_back(grad_one, own_one, inv_one, gain_one)
+    norm_one_grad, (vo_first, qk_first) = norm_back(
+        grad_one, own_one, inv_one, gain_one, (vo_first, qk_first)
+    )
+    vo_keep, vo_send = second_step(part_vo[0], vo_first)
+    vo_second = swap_y(vo_send)
+    qk_keep, qk_send = second_step(part_qk[0], qk_first)
+    qk_second = swap_x(qk_send)
+    norm_one_grad = after(norm_one_grad, qk_send, vo_send)
     in_leave, in_leave_far = leave(spots, norm_two_grad + norm_one_grad)
     in_far = swap_zh(in_leave_far)
 
-    vo_first, qk_first, down_third, up_third = after(
-        (vo_first, qk_first, down_third, up_third), in_leave_far
-    )
-    vo_keep, vo_send = second_step(part_vo[0], vo_first)
-    qk_keep, qk_send = second_step(part_qk[0], qk_first)
-    vo_second, qk_second = swap_y(vo_send), swap_x(qk_send)
-    ff_kept, ff_sent = store_ff(
-        spots, after(up_keep + up_third, vo_send, qk_send), down_keep + down_third
-    )
+    up_third, vo_second = after((up_third, vo_second), in_leave_far)
+    vo_keep, vo_send = third_step(vo_keep, vo_second)
+    vo_third = swap_zh(vo_send)
+    up_third = after(up_third, vo_send)
+    ff_kept, ff_sent = store_ff(spots, up_keep + up_third, down_keep + down_third)
     ff_got = swap_core(ff_sent)
-    in_far, vo_second, qk_second = lax.optimization_barrier(
-        after((in_far, vo_second, qk_second), ff_sent)
-    )
+    in_far, qk_second = lax.optimization_barrier(after((in_far, qk_second), ff_sent))
     in_message = jnp.stack([in_leave[1], in_far[1]])
     in_there = swap_x(in_message)
-    vo_keep, vo_send = third_step(vo_keep, vo_second)
     qk_keep, qk_send = third_step(qk_keep, qk_second)
-    vo_third, qk_third = swap_zh(vo_send), swap_zh(qk_send)
-    g_up, g_down = join_ff(spots, ff_kept, after(ff_got, vo_send, qk_send, in_message))
-    in_kept, in_sent = undeal(spots, in_leave, in_far, in_there)
-    no_shift = jnp.zeros((2 * HEAD_DIM, 1), F32)
-    hidden_grad = finish(spots, in_kept, swap_core(in_sent), cotangent, no_shift)
-    at_kept, at_sent = store_qkvo(spots, qk_keep + qk_third, vo_keep + vo_third)
-    g_qkv, g_out = join_qkvo(spots, at_kept, swap_core(at_sent))
+    qk_third = swap_zh(qk_send)
+    g_up, g_down = join_ff(spots, ff_kept, after(ff_got, qk_send, in_message))
 
     def over_tokens(values):
         return jnp.sum(values, axis=-1, dtype=F32)
@@ -1421,6 +1411,13 @@
     other = swap_core(total)
     both = jnp.where(c == 0, jnp.stack([total, other]), jnp.stack([other, total]))
     singles = both[:, : 8 * HEAD_DIM].reshape(2, 8, HEAD_DIM).transpose(1, 0, 2).reshape(8, -1)
+
+    in_kept, in_sent = undeal(spots, in_leave, in_far, in_there)
+    no_shift = jnp.zeros((2 * HEAD_DIM, 1), F32)
+    hidden_grad = finish(spots, in_kept, swap_core(in_sent), cotangent, no_shift)
+    qk_third, vo_third = after((qk_third, vo_third), other, g_up, g_down, hidden_out)
+    at_kept, at_sent = store_qkvo(spots, qk_keep + qk_third, vo_keep + vo_third)
+    g_qkv, g_out = join_qkvo(spots, at_kept, swap_core(at_sent))
 
     return (
         hidden_out,

time: 530 us -> 504 us (0.951)
  waiting for transfers between devices: 180 us -> 148 us
  starting transfers between devices: 73.5 us -> 85 us
  local copies, waits for them, and re-layouts: 44.5 us -> 33.5 us
  other arithmetic: 46.5 us -> 53.9 us
    ppermute x14, waiting for transfers between devices: 76.2 us -> 60.7 us  [swap_zh(): return lax.ppermute(values, 'col', [(i, i ^ 4) for i in range(8)])]
    ppermute x12, waiting for transfers between devices: 66.5 us -> 52.8 us  [swap_zl(): return lax.ppermute(values, 'col', [(i, i ^ 2) for i in range(8)])]
    ppermute x12, starting transfers between devices: 3.71 us -> 15.5 us  [swap_zl(): return lax.ppermute(values, 'col', [(i, i ^ 2) for i in range(8)])]
    ppermute x9, waiting for transfers between devices: 21.5 us -> 13.6 us  [swap_y(): return lax.ppermute(values, 'row', [(i, i ^ 2) for i in range(4)])]
    ppermute x24, starting transfers between devices: 35.8 us -> 28.9 us  [swap_core(): return lax.ppermute(values, 'row', [(i, i ^ 1) for i in range(4)])]
    pallas_call x4 -> x0, local copies, waits for them, and re-layouts: 6.23 us -> none  [fold(): pl.pallas_call(functools.partial(fold_kernel, fill, (len(sources), len(va...]
    ppermute x0 -> x4, waiting for transfers between devices: none -> 5.93 us  [swap_both(): return lax.ppermute(values, ('row', 'col'), route)]
    convert_element_type x0 -> x3, other arithmetic: none -> 5.37 us  [fold_cores(): return (parts[0][0] + got[0], (parts[0][1] + got[1]).astype(BF))]
  transfers between devices with their start and end apart: 73 -> 77, of which waited for: 34 -> 34; matrix products, arithmetic and copies ran while one was open for 9% -> 11% of each run, Pallas kernels for 24% -> 30%
where the time goes in v2:
time: 504 us; the launch traced here: 497 us
  Pallas kernels  175 us (35%)
  waiting for transfers between devices  148 us (29%)
  starting transfers between devices  85 us (17%)
  other arithmetic  53.9 us (11%)
  local copies, waits for them, and re-layouts  33.5 us (7%)
    ppermute x14, waiting for transfers between devices, swap_zh(): return lax.ppermute(values, 'col', [(i, i ^ 4) for i in range(8)])  60.7 us
    ppermute x12, waiting for transfers between devices, swap_zl(): return lax.ppermute(values, 'col', [(i, i ^ 2) for i in range(8)])  52.8 us
    pallas_call x4, Pallas kernels, fold(): pl.pallas_call(functools.partial(fold_kernel, fill, (len(sources), len(va...  30.9 us
    ppermute x24, starting transfers between devices, swap_core(): return lax.ppermute(values, 'row', [(i, i ^ 1) for i in range(4)])  28.9 us
    pallas_call x2, Pallas kernels, attend_clip_back(): pl.pallas_call(attend_back_kernel, grid_spec=pltpu.PrefetchScalarGridSpec...  20.6 us
    ppermute x14, starting transfers between devices, swap_zh(): return lax.ppermute(values, 'col', [(i, i ^ 4) for i in range(8)])  19.8 us
    pallas_call x2, Pallas kernels, grad_x_first(): pl.pallas_call(functools.partial(pair_x_kernel, len(lefts)), grid=(2,), i...  18.1 us
    unnamed x144, local copies, waits for them, and re-layouts  17.4 us
  transfers between devices with their start and end apart: 77, of which 34 were waited for; matrix products, arithmetic and copies ran while one was open for 11% of the time, Pallas kernels for 30%

profile of v2, /device:TPU:1, one launch (start us, length us, event | category | flops | bytes accessed | tf_op | source)
XLA Modules:
  0.0 497.1 jit_solution(16515797136121286021)
XLA Ops:
  1.4 3.9 split_in.1
  8.4 4.4 prepare_weights.1
  37.8 22.7 %collective-permute-done.1 = bf16[160,640]{1,0:T(8,128)(2,1)S(1)} collective-permute-done((bf16[160,640]{1,0:T(8,128)(2,1)}, bf16[160,640]{1,0:T(8,128)(2,1)S(1)}, u32[]{:S(2)}, u32[]{:S(2)}) %collective-permute-start.1) | collective-permute-done | bytes 204832 | tf_op jit(solution)/shard_map/ppermute | solution.py:387
  88.0 13.4 %collective-permute-done.18 = bf16[320,640]{1,0:T(8,128)(2,1)S(1)} collective-permute-done((bf16[320,640]{1,0:T(8,128)(2,1)S(1)}, bf16[320,640]{1,0:T(8,128)(2,1)S(1)}, u32[]{:S(2)}, u32[]{:S(2)}) %collective-permute-start.18) | collective-permute-done | bytes 409632 | tf_op jit(solution)/shard_map/ppermute | solution.py:387
  113.4 7.4 %project.1 = (bf16[4,2,80,1024]{3,2,1,0:T(8,128)(2,1)}, bf16[4,80,1024]{2,1,0:T(8,128)(2,1)}, bf16[1280,1024]{1,0:T(8,128)(2,1)}) custom-call(bf16[2,2,80,1024]{3,2,1,0:T(8,128)(2,1)} %add_convert_fusion.5.b0, bf16[2,2,80,1024]{3,2,1,0:T(8,128)(2,1)} %collective-permute-done.16.b1, bf16[2,2,80,1024]{3,2,1,0:T(8,128)(2,1)} %collective-permute-done.17.b2, ...), custom_call_target="tpu_custom_call" | custom-call | flops 1 | bytes 1 | tf_op jit(solution)/shard_map/project/pallas_call | solution.py:929
  120.8 5.6 %collective-permute-done.21 = bf16[320,640]{1,0:T(8,128)(2,1)} collective-permute-done((bf16[320,640]{1,0:T(8,128)(2,1)}, bf16[320,640]{1,0:T(8,128)(2,1)}, u32[]{:S(2)}, u32[]{:S(2)}) %collective-permute-start.21) | collective-permute-done | bytes 409632 | tf_op jit(solution)/shard_map/ppermute | solution.py:387
  130.4 10.3 %attend_clip.1 = (bf16[4,80,1024]{2,1,0:T(8,128)(2,1)}, f32[4,1,1024]{2,1,0:T(1,128)}) custom-call(s32[1]{0:T(128)} %dynamic_slice.3.len_ref, bf16[4,2,80,1024]{3,2,1,0:T(8,128)(2,1)} %get-tuple-element.206.q_ref.k_ref, bf16[4,2,80,1024]{3,2,1,0:T(8,128)(2,1)} %get-tuple-element.206.q_ref.k_ref, bf16[4,80,1024]{2,1,0:T(8,128)(2,1)} %get-tuple-element.207.v_ref), custom_call_target="tpu_custom_call" | custom-call | flops 1 | bytes 1 | tf_op jit(solution)/shard_map/attend_clip/pallas_call | solution.py:443
  140.7 5.8 %fold_out.1 = (f32[2,2,2,80,1024]{4,3,2,1,0:T(8,128)}, bf16[2,2,2,80,1024]{4,3,2,1,0:T(8,128)(2,1)}) custom-call(bf16[2,2,160,640]{3,2,1,0:T(8,128)(2,1)} %copy-done.3, bf16[2,2,160,640]{3,2,1,0:T(8,128)(2,1)} %copy-done.6, bf16[4,80,1024]{2,1,0:T(8,128)(2,1)} %get-tuple-element.208.refs_2_), custom_call_target="tpu_custom_call" | custom-call | flops 1 | bytes 1 | tf_op jit(solution)/shard_map/fold_out/pallas_call | solution.py:1041
  157.9 13.2 %collective-permute-done.26 = bf16[2,2,80,1024]{3,2,1,0:T(8,128)(2,1)S(1)} collective-permute-done((bf16[2,2,80,1024]{3,2,1,0:T(8,128)(2,1)S(1)}, bf16[2,2,80,1024]{3,2,1,0:T(8,128)(2,1)S(1)}, u32[]{:S(2)}, u32[]{:S(2)}) %collective-permute-start.26) | collective-permute-done | bytes 655392 | tf_op jit(solution)/shard_map/ppermute | solution.py:383
  181.3 13.8 %collective-permute-done.32.b2 = bf16[2,2,80,1024]{3,2,1,0:T(8,128)(2,1)} collective-permute-done((bf16[2,2,80,1024]{3,2,1,0:T(8,128)(2,1)}, bf16[2,2,80,1024]{3,2,1,0:T(8,128)(2,1)}, u32[]{:S(2)}, u32[]{:S(2)}) %collective-permute-start.32) | collective-permute-done | bytes 655392 | tf_op jit(solution)/shard_map/ppermute | solution.py:383
  201.9 8.2 %collective-permute-done.34.up1.refs_1_ = bf16[2,2,320,640]{3,2,1,0:T(8,128)(2,1)} collective-permute-done((bf16[2,2,320,640]{3,2,1,0:T(8,128)(2,1)S(1)}, bf16[2,2,320,640]{3,2,1,0:T(8,128)(2,1)}, u32[]{:S(2)}, u32[]{:S(2)}) %collective-permute-start.34) | collective-permute-done | bytes 1638432 | tf_op jit(solution)/shard_map/ppermute | solution.py:375
  210.1 10.3 %up_project.1 = (bf16[1280,1024]{1,0:T(8,128)(2,1)}, f32[1280,1024]{1,0:T(8,128)}, bf16[1280,1024]{1,0:T(8,128)(2,1)}) custom-call(bf16[2,2,80,1024]{3,2,1,0:T(8,128)(2,1)} %add_convert_fusion.3.b0, bf16[2,2,80,1024]{3,2,1,0:T(8,128)(2,1)} %collective-permute-done.31.b1, bf16[2,2,80,1024]{3,2,1,0:T(8,128)(2,1)} %collective-permute-done.32.b2, ...), custom_call_target="tpu_custom_call" | custom-call | flops 1 | bytes 1 | tf_op jit(solution)/shard_map/up_project/pallas_call | solution.py:957
  220.4 8.6 %fold_down.1 = (f32[2,2,2,80,1024]{4,3,2,1,0:T(8,128)}, bf16[2,2,2,80,1024]{4,3,2,1,0:T(8,128)(2,1)}) custom-call(bf16[2,2,320,640]{3,2,1,0:T(8,128)(2,1)} %pad_maximum_fusion.refs_0_.down0, bf16[2,2,320,640]{3,2,1,0:T(8,128)(2,1)} %collective-permute-done.27.refs_1_.down1, bf16[1280,1024]{1,0:T(8,128)(2,1)} %get-tuple-element.239.refs_2_), custom_call_target="tpu_custom_call" | custom-call | flops 1 | bytes 1 | tf_op jit(solution)/shard_map/fold_down/pallas_call | solution.py:1041
  238.8 9.2 %grad_act.1 = (bf16[1280,1024]{1,0:T(8,128)(2,1)}, bf16[1280,1024]{1,0:T(8,128)(2,1)}) custom-call(bf16[2,2,80,1024]{3,2,1,0:T(8,128)(2,1)} %place_in.3.b0, bf16[2,2,80,1024]{3,2,1,0:T(8,128)(2,1)} %copy-done.49, bf16[2,2,80,1024]{3,2,1,0:T(8,128)(2,1)} %collective-permute-done.35.b2, bf16[2,2,80,1024]{3,2,1,0:T(8,128)(2,1)} %collective-permute-done.38.b3, ...), custom_call_target="tpu_custom_call" | custom-call | flops 1 | bytes 1 | tf_op jit(solution)/shard_map/grad_act/pallas_call | solution.py:983
  248.0 4.9 collective-permute-done.39
  252.8 8.6 %fold_up.1 = (f32[2,2,2,80,1024]{4,3,2,1,0:T(8,128)}, bf16[2,2,2,80,1024]{4,3,2,1,0:T(8,128)(2,1)}) custom-call(bf16[2,2,320,640]{3,2,1,0:T(8,128)(2,1)} %copy-done.5, bf16[2,2,320,640]{3,2,1,0:T(8,128)(2,1)} %collective-permute-done.34.up1.refs_1_, bf16[1280,1024]{1,0:T(8,128)(2,1)} %get-tuple-element.242.refs_2_), custom_call_target="tpu_custom_call" | custom-call | flops 1 | bytes 1 | tf_op jit(solution)/shard_map/fold_up/pallas_call | solution.py:1041
  269.0 7.4 %grad_down.1 = (f32[2,2,320,640]{3,2,1,0:T(8,128)}, bf16[2,2,320,640]{3,2,1,0:T(8,128)(2,1)}) custom-call(bf16[2,2,320,1024]{3,2,1,0:T(8,128)(2,1)} %bitcast.164, bf16[1280,1024]{1,0:T(8,128)(2,1)} %get-tuple-element.240.refs_1_), custom_call_target="tpu_custom_call" | custom-call | flops 1 | bytes 1 | tf_op jit(solution)/shard_map/grad_down/pallas_call | solution.py:1110
  276.4 7.2 %grad_up.1 = (f32[4,320,640]{2,1,0:T(8,128)}, bf16[4,320,640]{2,1,0:T(8,128)(2,1)}) custom-call(bf16[4,320,1024]{2,1,0:T(8,128)(2,1)} %bitcast.161, bf16[1280,1024]{1,0:T(8,128)(2,1)} %get-tuple-element.243.right_ref), custom_call_target="tpu_custom_call" | custom-call | flops 1 | bytes 1 | tf_op jit(solution)/shard_map/grad_up/pallas_call | solution.py:1079
  300.5 9.4 %collective-permute-done.46.b2 = bf16[2,2,80,1024]{3,2,1,0:T(8,128)(2,1)S(1)} collective-permute-done((bf16[2,2,80,1024]{3,2,1,0:T(8,128)(2,1)S(1)}, bf16[2,2,80,1024]{3,2,1,0:T(8,128)(2,1)S(1)}, u32[]{:S(2)}, u32[]{:S(2)}) %collective-permute-start.46) | collective-permute-done | bytes 655392 | tf_op jit(solution)/shard_map/ppermute | solution.py:383
  313.6 5.4 %grad_attended.1 = (bf16[4,80,1024]{2,1,0:T(8,128)(2,1)}, bf16[1280,1024]{1,0:T(8,128)(2,1)}) custom-call(bf16[2,2,80,1024]{3,2,1,0:T(8,128)(2,1)} %copy-done.32, bf16[2,2,80,1024]{3,2,1,0:T(8,128)(2,1)} %copy-done.50, bf16[2,2,80,1024]{3,2,1,0:T(8,128)(2,1)} %copy-done.48, bf16[2,2,80,1024]{3,2,1,0:T(8,128)(2,1)} %copy-done.51, ...), custom_call_target="tpu_custom_call" | custom-call | flops 1 | bytes 1 | tf_op jit(solution)/shard_map/grad_attended/pallas_call | solution.py:1006
  319.0 10.4 %attend_clip_back.2 = (bf16[4,2,80,1024]{3,2,1,0:T(8,128)(2,1)}, bf16[4,80,1024]{2,1,0:T(8,128)(2,1)}) custom-call(s32[1]{0:T(128)} %dynamic_slice.3.len_ref, bf16[4,2,80,1024]{3,2,1,0:T(8,128)(2,1)} %get-tuple-element.206.q_ref.k_ref, bf16[4,2,80,1024]{3,2,1,0:T(8,128)(2,1)} %get-tuple-element.206.q_ref.k_ref, ...), custom_call_target="tpu_custom_call" | custom-call | flops 1 | bytes 1 | tf_op jit(solution)/shard_map/attend_clip_back/pallas_call | solution.py:491
  338.5 10.1 %attend_clip_back.3 = (bf16[4,2,80,1024]{3,2,1,0:T(8,128)(2,1)}, bf16[4,80,1024]{2,1,0:T(8,128)(2,1)}) custom-call(s32[1]{0:T(128)} %dynamic_slice.3.len_ref, bf16[4,2,80,1024]{3,2,1,0:T(8,128)(2,1)} %get-tuple-element.206.q_ref.k_ref, bf16[4,2,80,1024]{3,2,1,0:T(8,128)(2,1)} %get-tuple-element.206.q_ref.k_ref, ...), custom_call_target="tpu_custom_call", output_to_operand_aliasing={{0}: (6, {}), {1}: (7, {})} | custom-call | flops 1 | bytes 1 | tf_op jit(solution)/shard_map/attend_clip_back/pallas_call | solution.py:491
  348.6 4.7 collective-permute-done.50.far_ref
  354.8 7.9 %fold_project.1 = (f32[2,2,2,80,1024]{4,3,2,1,0:T(8,128)}, bf16[2,2,2,80,1024]{4,3,2,1,0:T(8,128)(2,1)}) custom-call(bf16[2,2,160,640]{3,2,1,0:T(8,128)(2,1)} %copy-done.15, bf16[2,2,160,640]{3,2,1,0:T(8,128)(2,1)} %copy-done.25, bf16[2,2,160,640]{3,2,1,0:T(8,128)(2,1)} %copy-done.3, bf16[2,2,160,640]{3,2,1,0:T(8,128)(2,1)} %copy-done.6, ...), custom_call_target="tpu_custom_call" | custom-call | flops 1 | bytes 1 | tf_op jit(solution)/shard_map/fold_project/pallas_call | solution.py:1041
  374.8 10.7 %grad_vo.1 = (f32[2,2,160,640]{3,2,1,0:T(8,128)}, bf16[2,2,160,640]{3,2,1,0:T(8,128)(2,1)}) custom-call(bf16[2,2,80,1024]{3,2,1,0:T(8,128)(2,1)} %bitcast.163, bf16[2,2,80,1024]{3,2,1,0:T(8,128)(2,1)} %bitcast.165, bf16[1280,1024]{1,0:T(8,128)(2,1)} %get-tuple-element.282.refs_2_.right_ref, bf16[1280,1024]{1,0:T(8,128)(2,1)} %get-tuple-element.283.refs_3_), custom_call_target="tpu_custom_call" | custom-call | flops 1 | bytes 1 | tf_op jit(solution)/shard_map/grad_vo/pallas_call | solution.py:1110
  386.0 10.4 %collective-permute-done.55 = bf16[2,2,80,1024]{3,2,1,0:T(8,128)(2,1)S(1)} collective-permute-done((bf16[2,2,80,1024]{3,2,1,0:T(8,128)(2,1)S(1)}, bf16[2,2,80,1024]{3,2,1,0:T(8,128)(2,1)S(1)}, u32[]{:S(2)}, u32[]{:S(2)}) %collective-permute-start.55) | collective-permute-done | bytes 655392 | tf_op jit(solution)/shard_map/ppermute | solution.py:383
  398.3 6.7 %grad_qk.1 = (f32[4,160,640]{2,1,0:T(8,128)}, bf16[4,160,640]{2,1,0:T(8,128)(2,1)}) custom-call(bf16[4,160,1024]{2,1,0:T(8,128)(2,1)} %bitcast.162, bf16[1280,1024]{1,0:T(8,128)(2,1)} %get-tuple-element.282.refs_2_.right_ref), custom_call_target="tpu_custom_call" | custom-call | flops 1 | bytes 1 | tf_op jit(solution)/shard_map/grad_qk/pallas_call | solution.py:1079
  420.2 3.7 collective-permute-done.62
  441.1 4.1 store_ff.1
  448.6 8.5 %collective-permute-done.63.far_ref = bf16[2,80,1024]{2,1,0:T(8,128)(2,1)S(1)} collective-permute-done((bf16[2,80,1024]{2,1,0:T(8,128)(2,1)}, bf16[2,80,1024]{2,1,0:T(8,128)(2,1)S(1)}, u32[]{:S(2)}, u32[]{:S(2)}) %collective-permute-start.63) | collective-permute-done | bytes 327712 | tf_op jit(solution)/shard_map/ppermute | solution.py:387
  466.9 3.9 finish.2
  490.0 3.9 finish.3
  (426 shorter events, 230.5 us)
Async XLA Ops:
  12.8 18.7 %collective-permute-start = (bf16[960,384]{1,0:T(8,128)(2,1)}, bf16[960,384]{1,0:T(8,128)(2,1)S(1)}, u32[]{:S(2)}, u32[]{:S(2)}) collective-permute-start(bf16[960,384]{1,0:T(8,128)(2,1)} %get-tuple-element.170), channel_id=1, source_target_pairs={{0,8},{8,0},{16,24},{24,16},{1,9},{9,1},{17,25},{25,17},{2,10},{10... | collective-permute-start | bytes 2211848 | tf_op jit(solution)/shard_map/ppermute | solution.py:371
  29.2 36.4 %collective-permute-start.5 = (bf16[2,88,1024]{2,1,0:T(8,128)(2,1)}, bf16[2,88,1024]{2,1,0:T(8,128)(2,1)}, u32[]{:S(2)}, u32[]{:S(2)}) collective-permute-start(bf16[2,88,1024]{2,1,0:T(8,128)(2,1)} %pad_maximum_fusion.8), channel_id=1, source_target_pairs={{0,4},{1,5},{2,6},{3,7},{4,0},{5,1},{6,2},{7,3},{8,12},{9,13},{10,... | collective-permute-start | bytes 1081352 | tf_op jit(solution)/shard_map/ppermute | solution.py:387
  35.1 25.4 %collective-permute-start.1 = (bf16[160,640]{1,0:T(8,128)(2,1)}, bf16[160,640]{1,0:T(8,128)(2,1)S(1)}, u32[]{:S(2)}, u32[]{:S(2)}) collective-permute-start(bf16[160,640]{1,0:T(8,128)(2,1)} %get-tuple-element.171), channel_id=1, source_target_pairs={{0,4},{1,5},{2,6},{3,7},{4,0},{5,1},{6,2},{7,3},{8,12},{9,13},{10,... | collective-permute-start | bytes 614408 | tf_op jit(solution)/shard_map/ppermute | solution.py:387
  35.2 29.8 %collective-permute-start.6 = (bf16[160,640]{1,0:T(8,128)(2,1)}, bf16[160,640]{1,0:T(8,128)(2,1)S(1)}, u32[]{:S(2)}, u32[]{:S(2)}) collective-permute-start(bf16[160,640]{1,0:T(8,128)(2,1)} %get-tuple-element.181), channel_id=1, source_target_pairs={{0,4},{1,5},{2,6},{3,7},{4,0},{5,1},{6,2},{7,3},{8,12},{9,13},{10,... | collective-permute-start | bytes 614408 | tf_op jit(solution)/shard_map/ppermute | solution.py:387
  37.5 37.2 %collective-permute-start.12 = (bf16[2,80,1024]{2,1,0:T(8,128)(2,1)}, bf16[2,80,1024]{2,1,0:T(8,128)(2,1)S(1)}, u32[]{:S(2)}, u32[]{:S(2)}) collective-permute-start(bf16[2,80,1024]{2,1,0:T(8,128)(2,1)} %get-tuple-element.184), channel_id=1, source_target_pairs={{0,1},{1,0},{2,3},{3,2},{4,5},{5,4},{6,7},{7,6},{8,9},{9,8},{10,11... | collective-permute-start | bytes 983048 | tf_op jit(solution)/shard_map/ppermute | solution.py:379
  77.4 24.9 %collective-permute-start.17 = (bf16[2,2,80,1024]{3,2,1,0:T(8,128)(2,1)}, bf16[2,2,80,1024]{3,2,1,0:T(8,128)(2,1)}, u32[]{:S(2)}, u32[]{:S(2)}) collective-permute-start(bf16[2,2,80,1024]{3,2,1,0:T(8,128)(2,1)} %add_convert_fusion.5.b0), channel_id=1, source_target_pairs={{0,2},{1,3},{2,0},{3,1},{4,6},{5,7},{6,4},{7,5},{8,10},{9,11},{10,... | collective-permute-start | bytes 1966088 | tf_op jit(solution)/shard_map/ppermute | solution.py:383
  79.7 21.7 %collective-permute-start.18 = (bf16[320,640]{1,0:T(8,128)(2,1)S(1)}, bf16[320,640]{1,0:T(8,128)(2,1)S(1)}, u32[]{:S(2)}, u32[]{:S(2)}) collective-permute-start(bf16[320,640]{1,0:T(8,128)(2,1)S(1)} %copy-done.53), channel_id=1, source_target_pairs={{0,4},{1,5},{2,6},{3,7},{4,0},{5,1},{6,2},{7,3},{8,12},{9,13},{10,... | collective-permute-start | bytes 1228808 | tf_op jit(solution)/shard_map/ppermute | solution.py:387
  82.8 28.8 %collective-permute-start.13 = (bf16[2,2,160,640]{3,2,1,0:T(8,128)(2,1)S(1)}, bf16[2,2,160,640]{3,2,1,0:T(8,128)(2,1)S(1)}, u32[]{:S(2)}, u32[]{:S(2)}) collective-permute-start(bf16[2,2,160,640]{3,2,1,0:T(8,128)(2,1)S(1)} %pad_maximum_fusion.2.vo0.refs_0_.refs_2_), channel_id=1, source_target_pairs={{0,1},{1,0},{2,3},{3,2},{4,5},{5,4},{6,7},{7,6},{8,9},{9,8},{10,11... | collective-permute-start | bytes 2457608 | tf_op jit(solution)/shard_map/ppermute | solution.py:379
  84.2 27.7 %collective-permute-start.20 = (bf16[2,2,160,640]{3,2,1,0:T(8,128)(2,1)S(1)}, bf16[2,2,160,640]{3,2,1,0:T(8,128)(2,1)S(1)}, u32[]{:S(2)}, u32[]{:S(2)}) collective-permute-start(bf16[2,2,160,640]{3,2,1,0:T(8,128)(2,1)S(1)} %pad_maximum_fusion.4.qk0.refs_0_), channel_id=1, source_target_pairs={{0,16},{8,24},{16,0},{24,8},{1,17},{9,25},{17,1},{25,9},{2,18},{10... | collective-permute-start | bytes 2457608 | tf_op jit(solution)/shard_map/ppermute | solution.py:375
  85.5 26.4 %collective-permute-start.16 = (bf16[2,2,80,1024]{3,2,1,0:T(8,128)(2,1)}, bf16[2,2,80,1024]{3,2,1,0:T(8,128)(2,1)}, u32[]{:S(2)}, u32[]{:S(2)}) collective-permute-start(bf16[2,2,80,1024]{3,2,1,0:T(8,128)(2,1)} %add_convert_fusion.5.b0), channel_id=1, source_target_pairs={{0,8},{8,0},{16,24},{24,16},{1,9},{9,1},{17,25},{25,17},{2,10},{10... | collective-permute-start | bytes 1966088 | tf_op jit(solution)/shard_map/ppermute | solution.py:371
  104.4 21.9 %collective-permute-start.21 = (bf16[320,640]{1,0:T(8,128)(2,1)}, bf16[320,640]{1,0:T(8,128)(2,1)}, u32[]{:S(2)}, u32[]{:S(2)}) collective-permute-start(bf16[320,640]{1,0:T(8,128)(2,1)} %get-tuple-element.194), channel_id=1, source_target_pairs={{0,4},{1,5},{2,6},{3,7},{4,0},{5,1},{6,2},{7,3},{8,12},{9,13},{10,... | collective-permute-start | bytes 1228808 | tf_op jit(solution)/shard_map/ppermute | solution.py:387
  111.6 35.0 %collective-permute-start.22 = (bf16[2,320,640]{2,1,0:T(8,128)(2,1)}, bf16[2,320,640]{2,1,0:T(8,128)(2,1)S(1)}, u32[]{:S(2)}, u32[]{:S(2)}) collective-permute-start(bf16[2,320,640]{2,1,0:T(8,128)(2,1)} %get-tuple-element.211), channel_id=1, source_target_pairs={{0,1},{1,0},{2,3},{3,2},{4,5},{5,4},{6,7},{7,6},{8,9},{9,8},{10,11... | collective-permute-start | bytes 2457608 | tf_op jit(solution)/shard_map/ppermute | solution.py:379
  127.7 19.4 %collective-permute-start.23 = (bf16[2,320,640]{2,1,0:T(8,128)(2,1)S(1)}, bf16[2,320,640]{2,1,0:T(8,128)(2,1)S(1)}, u32[]{:S(2)}, u32[]{:S(2)}) collective-permute-start(bf16[2,320,640]{2,1,0:T(8,128)(2,1)S(1)} %get-tuple-element.348), channel_id=1, source_target_pairs={{0,16},{8,24},{16,0},{24,8},{1,17},{9,25},{17,1},{25,9},{2,18},{10... | collective-permute-start | bytes 2457608 | tf_op jit(solution)/shard_map/ppermute | solution.py:375
  157.7 62.7 %collective-permute-start.27 = (bf16[2,2,320,640]{3,2,1,0:T(8,128)(2,1)}, bf16[2,2,320,640]{3,2,1,0:T(8,128)(2,1)}, u32[]{:S(2)}, u32[]{:S(2)}) collective-permute-start(bf16[2,2,320,640]{3,2,1,0:T(8,128)(2,1)} %pad_maximum_fusion.refs_0_.down0), channel_id=1, source_target_pairs={{0,1},{1,0},{2,3},{3,2},{4,5},{5,4},{6,7},{7,6},{8,9},{9,8},{10,11... | collective-permute-start | bytes 4915208 | tf_op jit(solution)/shard_map/ppermute | solution.py:379
  173.4 36.7 %collective-permute-start.34 = (bf16[2,2,320,640]{3,2,1,0:T(8,128)(2,1)S(1)}, bf16[2,2,320,640]{3,2,1,0:T(8,128)(2,1)}, u32[]{:S(2)}, u32[]{:S(2)}) collective-permute-start(bf16[2,2,320,640]{3,2,1,0:T(8,128)(2,1)S(1)} %pad_maximum_fusion.1.up0.refs_0_), channel_id=1, source_target_pairs={{0,16},{8,24},{16,0},{24,8},{1,17},{9,25},{17,1},{25,9},{2,18},{10... | collective-permute-start | bytes 4915208 | tf_op jit(solution)/shard_map/ppermute | solution.py:375
  180.8 21.1 %collective-permute-start.31 = (bf16[2,2,80,1024]{3,2,1,0:T(8,128)(2,1)}, bf16[2,2,80,1024]{3,2,1,0:T(8,128)(2,1)}, u32[]{:S(2)}, u32[]{:S(2)}) collective-permute-start(bf16[2,2,80,1024]{3,2,1,0:T(8,128)(2,1)} %add_convert_fusion.3.b0), channel_id=1, source_target_pairs={{0,8},{8,0},{16,24},{24,16},{1,9},{9,1},{17,25},{25,17},{2,10},{10... | collective-permute-start | bytes 1966088 | tf_op jit(solution)/shard_map/ppermute | solution.py:371
  199.6 20.8 %collective-permute-start.35 = (bf16[2,2,80,1024]{3,2,1,0:T(8,128)(2,1)}, bf16[2,2,80,1024]{3,2,1,0:T(8,128)(2,1)}, u32[]{:S(2)}, u32[]{:S(2)}) collective-permute-start(bf16[2,2,80,1024]{3,2,1,0:T(8,128)(2,1)} %place_in.3.b0), channel_id=1, source_target_pairs={{0,2},{1,3},{2,0},{3,1},{4,6},{5,7},{6,4},{7,5},{8,10},{9,11},{10,... | collective-permute-start | bytes 1966088 | tf_op jit(solution)/shard_map/ppermute | solution.py:383
  289.2 40.2 %collective-permute-start.49 = (bf16[4,320,640]{2,1,0:T(8,128)(2,1)}, bf16[4,320,640]{2,1,0:T(8,128)(2,1)}, u32[]{:S(2)}, u32[]{:S(2)}) collective-permute-start(bf16[4,320,640]{2,1,0:T(8,128)(2,1)} %get-tuple-element.244), channel_id=1, source_target_pairs={{0,16},{8,24},{16,0},{24,8},{1,17},{9,25},{17,1},{25,9},{2,18},{10... | collective-permute-start | bytes 4915208 | tf_op jit(solution)/shard_map/ppermute | solution.py:375
  289.4 40.0 %collective-permute-start.48 = (bf16[2,2,320,640]{3,2,1,0:T(8,128)(2,1)}, bf16[2,2,320,640]{3,2,1,0:T(8,128)(2,1)}, u32[]{:S(2)}, u32[]{:S(2)}) collective-permute-start(bf16[2,2,320,640]{3,2,1,0:T(8,128)(2,1)} %get-tuple-element.241), channel_id=1, source_target_pairs={{0,1},{1,0},{2,3},{3,2},{4,5},{5,4},{6,7},{7,6},{8,9},{9,8},{10,11... | collective-permute-start | bytes 4915208 | tf_op jit(solution)/shard_map/ppermute | solution.py:379
  336.1 26.6 %collective-permute-start.53 = (bf16[2,320,640]{2,1,0:T(8,128)(2,1)S(1)}, bf16[2,320,640]{2,1,0:T(8,128)(2,1)}, u32[]{:S(2)}, u32[]{:S(2)}) collective-permute-start(bf16[2,320,640]{2,1,0:T(8,128)(2,1)S(1)} %slice.539), channel_id=1, source_target_pairs={{0,1},{1,0},{2,3},{3,2},{4,5},{5,4},{6,7},{7,6},{8,9},{9,8},{10,11... | collective-permute-start | bytes 2457608 | tf_op jit(solution)/shard_map/ppermute | solution.py:379
  336.4 26.4 %collective-permute-start.52 = (bf16[2,320,640]{2,1,0:T(8,128)(2,1)}, bf16[2,320,640]{2,1,0:T(8,128)(2,1)}, u32[]{:S(2)}, u32[]{:S(2)}) collective-permute-start(bf16[2,320,640]{2,1,0:T(8,128)(2,1)} %fusion.4), channel_id=1, source_target_pairs={{0,16},{8,24},{16,0},{24,8},{1,17},{9,25},{17,1},{25,9},{2,18},{10... | collective-permute-start | bytes 2457608 | tf_op jit(solution)/shard_map/ppermute | solution.py:375
  364.7 48.3 %collective-permute-start.51 = (bf16[2,80,1024]{2,1,0:T(8,128)(2,1)}, bf16[2,80,1024]{2,1,0:T(8,128)(2,1)}, u32[]{:S(2)}, u32[]{:S(2)}) collective-permute-start(bf16[2,80,1024]{2,1,0:T(8,128)(2,1)} %pad_maximum_fusion.10), channel_id=1, source_target_pairs={{0,1},{1,0},{2,3},{3,2},{4,5},{5,4},{6,7},{7,6},{8,9},{9,8},{10,11... | collective-permute-start | bytes 983048 | tf_op jit(solution)/shard_map/ppermute | solution.py:379
  371.6 24.8 %collective-permute-start.55 = (bf16[2,2,80,1024]{3,2,1,0:T(8,128)(2,1)S(1)}, bf16[2,2,80,1024]{3,2,1,0:T(8,128)(2,1)S(1)}, u32[]{:S(2)}, u32[]{:S(2)}) collective-permute-start(bf16[2,2,80,1024]{3,2,1,0:T(8,128)(2,1)S(1)} %fusion.11), channel_id=1, source_target_pairs={{0,2},{1,3},{2,0},{3,1},{4,6},{5,7},{6,4},{7,5},{8,10},{9,11},{10,... | collective-permute-start | bytes 1966088 | tf_op jit(solution)/shard_map/ppermute | solution.py:383
  372.7 32.3 %collective-permute-start.56 = (bf16[320,640]{1,0:T(8,128)(2,1)}, bf16[320,640]{1,0:T(8,128)(2,1)}, u32[]{:S(2)}, u32[]{:S(2)}) collective-permute-start(bf16[320,640]{1,0:T(8,128)(2,1)} %get-tuple-element.392), channel_id=1, source_target_pairs={{0,4},{1,5},{2,6},{3,7},{4,0},{5,1},{6,2},{7,3},{8,12},{9,13},{10,... | collective-permute-start | bytes 1228808 | tf_op jit(solution)/shard_map/ppermute | solution.py:387
  397.3 26.6 %collective-permute-start.61 = (bf16[2,2,160,640]{3,2,1,0:T(8,128)(2,1)}, bf16[2,2,160,640]{3,2,1,0:T(8,128)(2,1)S(1)}, u32[]{:S(2)}, u32[]{:S(2)}) collective-permute-start(bf16[2,2,160,640]{3,2,1,0:T(8,128)(2,1)} %get-tuple-element.286), channel_id=1, source_target_pairs={{0,1},{1,0},{2,3},{3,2},{4,5},{5,4},{6,7},{7,6},{8,9},{9,8},{10,11... | collective-permute-start | bytes 2457608 | tf_op jit(solution)/shard_map/ppermute | solution.py:379
  405.0 18.9 %collective-permute-start.62 = (bf16[4,160,640]{2,1,0:T(8,128)(2,1)}, bf16[4,160,640]{2,1,0:T(8,128)(2,1)}, u32[]{:S(2)}, u32[]{:S(2)}) collective-permute-start(bf16[4,160,640]{2,1,0:T(8,128)(2,1)} %get-tuple-element.290), channel_id=1, source_target_pairs={{0,16},{8,24},{16,0},{24,8},{1,17},{9,25},{17,1},{25,9},{2,18},{10... | collective-permute-start | bytes 2457608 | tf_op jit(solution)/shard_map/ppermute | solution.py:375
  416.8 21.2 %collective-permute-start.65 = (bf16[320,640]{1,0:T(8,128)(2,1)}, bf16[320,640]{1,0:T(8,128)(2,1)}, u32[]{:S(2)}, u32[]{:S(2)}) collective-permute-start(bf16[320,640]{1,0:T(8,128)(2,1)} %get-tuple-element.393), channel_id=1, source_target_pairs={{0,4},{1,5},{2,6},{3,7},{4,0},{5,1},{6,2},{7,3},{8,12},{9,13},{10,... | collective-permute-start | bytes 1228808 | tf_op jit(solution)/shard_map/ppermute | solution.py:387
  419.5 47.4 %collective-permute-start.57 = (bf16[80,2048]{1,0:T(8,128)(2,1)}, bf16[80,2048]{1,0:T(8,128)(2,1)}, u32[]{:S(2)}, u32[]{:S(2)}) collective-permute-start(bf16[80,2048]{1,0:T(8,128)(2,1)} %get-tuple-element.293), channel_id=1, source_target_pairs={{0,8},{8,0},{16,24},{24,16},{1,9},{9,1},{17,25},{25,17},{2,10},{10... | collective-permute-start | bytes 983048 | tf_op jit(solution)/shard_map/ppermute | solution.py:371
  433.3 24.5 %collective-permute-start.64 = (bf16[2,160,640]{2,1,0:T(8,128)(2,1)S(1)}, bf16[2,160,640]{2,1,0:T(8,128)(2,1)}, u32[]{:S(2)}, u32[]{:S(2)}) collective-permute-start(bf16[2,160,640]{2,1,0:T(8,128)(2,1)S(1)} %slice.540), channel_id=1, source_target_pairs={{0,1},{1,0},{2,3},{3,2},{4,5},{5,4},{6,7},{7,6},{8,9},{9,8},{10,11... | collective-permute-start | bytes 1228808 | tf_op jit(solution)/shard_map/ppermute | solution.py:379
  435.7 21.4 %collective-permute-start.63 = (bf16[2,80,1024]{2,1,0:T(8,128)(2,1)}, bf16[2,80,1024]{2,1,0:T(8,128)(2,1)S(1)}, u32[]{:S(2)}, u32[]{:S(2)}) collective-permute-start(bf16[2,80,1024]{2,1,0:T(8,128)(2,1)} %get-tuple-element.302), channel_id=1, source_target_pairs={{0,4},{1,5},{2,6},{3,7},{4,0},{5,1},{6,2},{7,3},{8,12},{9,13},{10,... | collective-permute-start | bytes 983048 | tf_op jit(solution)/shard_map/ppermute | solution.py:387
  441.1 33.8 %collective-permute-start.74 = (bf16[160,640]{1,0:T(8,128)(2,1)S(1)}, bf16[160,640]{1,0:T(8,128)(2,1)}, u32[]{:S(2)}, u32[]{:S(2)}) collective-permute-start(bf16[160,640]{1,0:T(8,128)(2,1)S(1)} %fusion.18), channel_id=1, source_target_pairs={{0,4},{1,5},{2,6},{3,7},{4,0},{5,1},{6,2},{7,3},{8,12},{9,13},{10,... | collective-permute-start | bytes 614408 | tf_op jit(solution)/shard_map/ppermute | solution.py:387
  445.3 26.7 %collective-permute-start.75 = (f32[320,640]{1,0:T(8,128)}, f32[320,640]{1,0:T(8,128)}, u32[]{:S(2)}, u32[]{:S(2)}) collective-permute-start(f32[320,640]{1,0:T(8,128)} %get-tuple-element.307), channel_id=1, source_target_pairs={{0,8},{8,0},{16,24},{24,16},{1,9},{9,1},{17,25},{25,17},{2,10},{10... | collective-permute-start | bytes 2457608 | tf_op jit(solution)/shard_map/ppermute | solution.py:371
  (119 other events, 840.8 us)

commit v3 on v2

--- a/solution.py
+++ b/solution.py
@@ -579,8 +579,8 @@
     return pl.pallas_call(
         lanes_kernel,
         in_specs=[spots_spec(), whole(), whole()],
-        out_specs=[whole()] * 4,
-        out_shape=[shaped((n, HALF)) for n in (OWN // 2, OWN // 2, OWN, OWN)],
+        out_specs=[whole()] * 3,
+        out_shape=[shaped((OWN, HALF))] * 3,
         cost_estimate=cost(0, 4 * 3 * OWN * OWN * 2),
         name="join_lanes",
     )(spots, kept, got)
@@ -701,7 +701,7 @@
 TAIL = 8
 
 
-def split_kernel(spots_ref, hid_ref, cot_ref, hk_ref, hs_ref, ck_ref, cs_ref):
+def split_kernel(spots_ref, hid_ref, cot_ref, pack_ref, hk_ref, hs_ref, ck_ref, cs_ref):
     c = spots_ref[0]
     data, tails, cots = [], [], []
     for half in (0, 1):
@@ -709,15 +709,14 @@
         value = hid_ref[rows]
         mean = jnp.mean(value, axis=0, keepdims=True)
         data.append(value - mean)
-        high = mean.astype(BF).astype(F32)
-        middle = (mean - high).astype(BF).astype(F32)
-        low = mean - high - middle
         spot = lax.broadcasted_iota(jnp.int32, (TAIL, value.shape[1]), 0)
-        tails.append(
-            jnp.where(
-                spot == 0, high, jnp.where(spot == 1, middle, jnp.where(spot == 2, low, 0.0))
-            )
-        )
+        tail = jnp.zeros(spot.shape, F32)
+        for first, exact in ((0, mean), (3, pack_ref[half : half + 1])):
+            high = exact.astype(BF).astype(F32)
+            middle = (exact - high).astype(BF).astype(F32)
+            for i, term in enumerate((high, middle, exact - high - middle)):
+                tail = jnp.where(spot == first + i, term, tail)
+        tails.append(tail)
         cots.append(cot_ref[rows])
     for ref, cot, first in ((hk_ref, ck_ref, c == 0), (hs_ref, cs_ref, c == 1)):
         ref[:HEAD_DIM] = jnp.where(first, data[0], data[1]).astype(BF)
@@ -725,7 +724,7 @@
         cot[...] = jnp.where(first, cots[0], cots[1]).astype(BF)
 
 
-def split(spots, hidden_in, cotangent):
+def split(spots, hidden_in, cotangent, pack):
     block = pl.BlockSpec((2 * HEAD_DIM, CLIP // 2), lambda i: (0, i))
     specs = [
         pl.BlockSpec((n, CLIP // 2), lambda i: (0, i))
@@ -734,14 +733,19 @@
     return pl.pallas_call(
         split_kernel,
         grid=(4,),
-        in_specs=[spots_spec(), block, block],
+        in_specs=[
+            spots_spec(),
+            block,
+            block,
+            pl.BlockSpec((2, CLIP // 2), lambda i: (0, i % 2)),
+        ],
         out_specs=specs,
         out_shape=[
             shaped((n, 2 * CLIP)) for n in (HEAD_DIM + TAIL, HEAD_DIM + TAIL, HEAD_DIM, HEAD_DIM)
         ],
         cost_estimate=cost(0, 8 * HEAD_DIM * 2 * CLIP * 4),
         name="split_in",
-    )(spots, hidden_in, cotangent)
+    )(spots, hidden_in, cotangent, pack)
 
 
 def deal_kernel(spots_ref, kept_ref, got_ref, here_ref, send_ref):
@@ -783,6 +787,8 @@
                             tail = ref[k, HEAD_DIM:].astype(F32)
                             mean = tail[0:1] + tail[1:2] + tail[2:3]
                             own_ref[i, j] = ref[k, :HEAD_DIM].astype(F32) + mean
+                            spot = 2 * i + j
+                            stats_ref[1][spot : spot + 1] = tail[3:4] + tail[4:5] + tail[5:6]
                         else:
                             own_ref[i, j] = ref[k]
 
@@ -797,7 +803,7 @@
 def place(spots, here, there, far, with_stats):
     rows = here.shape[1]
     own = (2, 2, HEAD_DIM, CLIP)
-    outs = [(own, F32), ((2, CLIP), F32)] if with_stats else [(own, BF)]
+    outs = [(own, F32), ((2, CLIP), F32), ((4, CLIP), F32)] if with_stats else [(own, BF)]
     return pl.pallas_call(
         place_kernel,
         in_specs=[spots_spec()] + [whole()] * 3,
@@ -881,16 +887,23 @@
     )(spots, kept, got, base, shift)
 
 
-def y_last(pair, yr, rows=slice(None)):
-    return jnp.concatenate([pair[yr][xr, zhr, rows] for xr in (0, 1) for zhr in (0, 1)])
-
-
-def x_last(pair, yr, rows=slice(None)):
-    return jnp.concatenate([pair[xr][yr, zhr, rows] for xr in (0, 1) for zhr in (0, 1)])
-
-
-def wide_rows(half, pair, rows=slice(None)):
-    return jnp.concatenate([half(pair, 0, rows), half(pair, 1, rows)], axis=1)
+def rows_of(array, zhr, first, count, base):
+    start = first + (base if array.shape[1] == OWN else 0)
+    return array[zhr, start : start + count]
+
+
+def pieces(weight, yr, first=0, count=OWN, base=0):
+    return jnp.concatenate(
+        [
+            rows_of(weight[2 * yr + xr], zhr, first, count, base)
+            for xr in (0, 1)
+            for zhr in (0, 1)
+        ]
+    )
+
+
+def wide_rows(weight, *rows):
+    return jnp.concatenate([pieces(weight, 0, *rows), pieces(weight, 1, *rows)], axis=1)
 
 
 def join_blocks(refs):
@@ -905,26 +918,29 @@
     )
 
 
-HEAD_ROWS = slice(0, HEAD_DIM)
-OUT_ROWS = slice(HEAD_DIM, 2 * HEAD_DIM)
-
-
-def project_kernel(b0, b1, b2, b3, qk0, qk1, vo0, vo1, qs_ref, vs_ref, qk_ref, v_ref, wide_ref):
-    wide = join_blocks((b0, b1, b2, b3))
+QK_ROWS = (0, 2 * HEAD_DIM, 0)
+HEAD_ROWS = (0, HEAD_DIM, OWN // 2)
+OUT_ROWS = (HEAD_DIM, HEAD_DIM, OWN // 2)
+
+
+def project_kernel(*refs):
+    blocks, w_qk, w_vo = refs[:4], refs[4:8], (*refs[4:7], refs[8])
+    qs_ref, vs_ref, qk_ref, v_ref, wide_ref = refs[9:]
+    wide = join_blocks(blocks)
     wide_ref[...] = wide
-    result = mm(wide_rows(y_last, (qk0, qk1)), wide, 1, 0)
+    result = mm(wide_rows(w_qk, *QK_ROWS), wide, 1, 0)
     for t in range(4):
         first = t * 2 * HEAD_DIM
         queries = result[first : first + HEAD_DIM] + qs_ref[t]
         qk_ref[t, 0] = queries.astype(BF)
         qk_ref[t, 1] = result[first + HEAD_DIM : first + 2 * HEAD_DIM].astype(BF)
-    result = mm(wide_rows(x_last, (vo0, vo1), HEAD_ROWS), wide, 1, 0)
+    result = mm(wide_rows(w_vo, *HEAD_ROWS), wide, 1, 0)
     for t in range(4):
         v_ref[t] = (result[t * HEAD_DIM : (t + 1) * HEAD_DIM] + vs_ref[t]).astype(BF)
 
 
-def project(blocks, qk, vo, q_shift, v_shift):
-    operands = (*blocks, *qk, *vo, q_shift, v_shift)
+def project(blocks, weights, q_shift, v_shift):
+    operands = (*blocks, *weights, q_shift, v_shift)
     outs = ((4, 2, HEAD_DIM, CLIP), (4, HEAD_DIM, CLIP), (D, CLIP))
     return pl.pallas_call(
         project_kernel,
@@ -937,14 +953,16 @@
     )(*operands)
 
 
-def up_kernel(b0, b1, b2, b3, up0, up1, shift_ref, act_ref, slope_ref, wide_ref):
-    wide = join_blocks((b0, b1, b2, b3))
+def up_kernel(*refs):
+    blocks, up = refs[:4], refs[4:8]
+    shift_ref, act_ref, slope_ref, wide_ref = refs[8:]
+    wide = join_blocks(blocks)
     wide_ref[...] = wide
     for xr in (0, 1):
         for zhr in (0, 1):
             first = (2 * xr + zhr) * OWN
             rows = slice(first, first + OWN)
-            weight = jnp.concatenate([up0[xr, zhr], up1[xr, zhr]], axis=1)
+            weight = jnp.concatenate([up[xr][zhr], up[2 + xr][zhr]], axis=1)
             pre = mm(weight, wide, 1, 0) + shift_ref[rows]
             cdf = 0.5 * (1.0 + lax.erf(pre * (0.5**0.5)))
             act_ref[rows] = (pre * cdf).astype(BF)
@@ -965,15 +983,16 @@
     )(*operands)
 
 
-def grad_act_kernel(b0, b1, b2, b3, down0, down1, slope_ref, out_ref, wide_ref):
-    wide = join_blocks((b0, b1, b2, b3))
+def grad_act_kernel(*refs):
+    blocks, down = refs[:4], refs[4:8]
+    slope_ref, out_ref, wide_ref = refs[8:]
+    wide = join_blocks(blocks)
     wide_ref[...] = wide
     for xr in (0, 1):
         for zhr in (0, 1):
             first = (2 * xr + zhr) * OWN
             rows = slice(first, first + OWN)
-            pair = (down0, down1)[xr]
-            weight = jnp.concatenate([pair[0, zhr], pair[1, zhr]], axis=1)
+            weight = jnp.concatenate([down[xr][zhr], down[2 + xr][zhr]], axis=1)
             out_ref[rows] = (mm(weight, wide, 1, 0) * slope_ref[rows]).astype(BF)
 
 
@@ -993,10 +1012,12 @@
     )(*operands)
 
 
-def grad_attended_kernel(b0, b1, b2, b3, vo0, vo1, out_ref, wide_ref):
-    wide = join_blocks((b0, b1, b2, b3))
+def grad_attended_kernel(*refs):
+    blocks, w_vo = refs[:4], refs[4:8]
+    out_ref, wide_ref = refs[8:]
+    wide = join_blocks(blocks)
     wide_ref[...] = wide
-    result = mm(wide_rows(x_last, (vo0, vo1), OUT_ROWS), wide, 1, 0)
+    result = mm(wide_rows(w_vo, *OUT_ROWS), wide, 1, 0)
     for t in range(4):
         out_ref[t] = result[t * HEAD_DIM : (t + 1) * HEAD_DIM].astype(BF)
 
@@ -1051,44 +1072,55 @@
 
 
 def fill_out(sources, yr):
-    return x_last(sources, yr, OUT_ROWS)
-
-
-def fill_up(sources, yr):
-    return y_last(sources, yr)
-
-
-def fill_down(sources, yr):
-    return x_last(sources, yr)
+    return pieces(sources, yr, *OUT_ROWS)
+
+
+def fill_all(sources, yr):
+    return pieces(sources, yr)
 
 
 def fill_project(sources, yr):
-    return jnp.concatenate([y_last(sources[:2], yr), x_last(sources[2:], yr, HEAD_ROWS)])
-
-
-def pair_y_kernel(left_ref, right_ref, keep_ref, send_ref):
+    return jnp.concatenate(
+        [
+            pieces(sources[:4], yr, *QK_ROWS),
+            pieces((*sources[:3], sources[4]), yr, *HEAD_ROWS),
+        ]
+    )
+
+
+def pair_y_kernel(left_ref, right_ref, keep_ref, first_ref, later_ref):
     result = mm(left_ref[0], right_ref[...], 1, 1)
     keep_ref[0] = result[:, :HALF]
-    send_ref[0] = result[:, HALF:].astype(BF)
+    far = result[:, HALF:].astype(BF)
+
+    @pl.when(pl.program_id(0) < 2)
+    def _():
+        first_ref[0] = far
+
+    @pl.when(pl.program_id(0) >= 2)
+    def _():
+        later_ref[0] = far
 
 
 def grad_y_first(left, right, name):
     rows = left.shape[1]
-    dims = (4, rows, HALF)
-    spec = pl.BlockSpec((1, rows, HALF), lambda i: (i, 0, 0))
     return pl.pallas_call(
         pair_y_kernel,
         grid=(4,),
-        in_specs=[pl.BlockSpec((1, rows, CLIP), lambda i: (i, 0, 0)), fixed(right)],
-        out_specs=[spec] * 2,
-        out_shape=[shaped(dims, F32), shaped(dims)],
+        in_specs=[pl.BlockSpec((1, rows, CLIP), lambda i: (i ^ 2, 0, 0)), fixed(right)],
+        out_specs=[
+            pl.BlockSpec((1, rows, HALF), lambda i: (i ^ 2, 0, 0)),
+            pl.BlockSpec((1, rows, HALF), lambda i: (jnp.minimum(i, 1), 0, 0)),
+            pl.BlockSpec((1, rows, HALF), lambda i: (jnp.maximum(i - 2, 0), 0, 0)),
+        ],
+        out_shape=[shaped((4, rows, HALF), F32)] + [shaped((2, rows, HALF))] * 2,
         cost_estimate=cost(2 * 4 * rows * D * CLIP, 4 * rows * D * 6),
         name=name,
     )(left, right)
 
 
 def pair_x_kernel(count, *refs):
-    keep_ref, send_ref = refs[2 * count :]
+    keep_ref, *send_refs = refs[2 * count :]
     start = 0
     for left_ref, right_ref in zip(refs[:count], refs[count : 2 * count]):
         rows = slice(start, start + left_ref.shape[2])
@@ -1100,20 +1132,19 @@
                 if xr == 0:
                     keep_ref[yr, 0, rows] = part
                 else:
-                    send_ref[yr, 0, rows] = part.astype(BF)
+                    send_refs[1 - yr][0, rows] = part.astype(BF)
 
 
 def grad_x_first(lefts, rights, name):
     rows = sum(v.shape[2] for v in lefts)
-    dims = (2, 2, rows, HALF)
-    spec = pl.BlockSpec((2, 1, rows, HALF), lambda i: (0, i, 0, 0))
+    send = pl.BlockSpec((1, rows, HALF), lambda i: (i, 0, 0))
     return pl.pallas_call(
         functools.partial(pair_x_kernel, len(lefts)),
         grid=(2,),
         in_specs=[pl.BlockSpec((2, 1) + v.shape[2:], lambda i: (0, i, 0, 0)) for v in lefts]
         + [fixed(v) for v in rights],
-        out_specs=[spec] * 2,
-        out_shape=[shaped(dims, F32), shaped(dims)],
+        out_specs=[pl.BlockSpec((2, 1, rows, HALF), lambda i: (0, i, 0, 0)), send, send],
+        out_shape=[shaped((2, 2, rows, HALF), F32)] + [shaped((2, rows, HALF))] * 2,
         cost_estimate=cost(2 * 4 * rows * D * CLIP, 4 * rows * D * 6),
         name=name,
     )(*lefts, *rights)
@@ -1132,6 +1163,16 @@
 
 def group_round(values):
     return values, swap_core(values), swap_zl(values), swap_both(values)
+
+
+def merge_in_turn(stats, count):
+    for swap in (swap_core, swap_zl):
+        other = swap(stats)
+        apart = other[0] - stats[0]
+        total = stats[1] + other[1] + apart * apart * (0.5 * count)
+        stats = jnp.stack([0.5 * (stats[0] + other[0]), total])
+        count = 2 * count
+    return stats[0], stats[1] / count
 
 
 def merge_stats(stats, count):
@@ -1176,6 +1217,19 @@
         got = swap_core(parts[1])
         return parts[0][0] + got[0], (parts[0][1] + got[1]).astype(BF)
 
+    pack = jnp.concatenate(
+        [
+            jnp.stack(
+                [ln1_gain, ln1_shift, ln2_gain, ln2_shift, out_bias, qv_bias[0], qv_bias[1]]
+            )
+            .reshape(7, 2, HEAD_DIM)
+            .transpose(1, 0, 2)
+            .reshape(2, 7 * HEAD_DIM),
+            in_bias.reshape(2, OWN),
+            jnp.zeros((2, CLIP - 11 * HEAD_DIM), F32),
+        ],
+        axis=1,
+    )
     kept, sent = prepare(
         spots,
         jnp.swapaxes(qkv_weight, 1, 2),
@@ -1184,79 +1238,66 @@
         jnp.swapaxes(down_weight, 0, 1),
     )
     weights_got = swap_core(sent)
-    h_kept, h_sent, c_kept, c_sent = split(spots, hidden_in, cotangent)
-    h_here, h_send = deal(spots, h_kept, swap_core(h_sent))
-    s_qk, s_vo, s_up, s_down = join_lanes(spots, kept, weights_got)
+    h_kept, h_sent, c_kept, c_sent = split(spots, after(hidden_in, sent), cotangent, pack)
+    s_at, s_up, s_down = join_lanes(spots, kept, weights_got)
+    at_zh = swap_zh(s_at)
+    h_here, h_send = deal(spots, after(h_kept, s_at), swap_core(h_sent))
     h_there = swap_x(h_send)
-    c_here, c_send = deal(spots, c_kept, swap_core(after(c_sent, h_send)))
-    c_there = swap_x(after(c_send, h_there))
-    qk_zh, vo_zh = swap_zh(s_qk), swap_zh(s_vo)
-
-    pack = jnp.stack(
-        [ln1_gain, ln1_shift, ln2_gain, ln2_shift, out_bias, qv_bias[0], qv_bias[1]]
-    )
-    pack = jnp.where(c == 0, pack[:, :HEAD_DIM], pack[:, HEAD_DIM:])
-    hidden_shift = jnp.where(c == 0, in_bias[:OWN], in_bias[OWN:])
-    pack = jnp.concatenate([pack, hidden_shift.reshape(4, HEAD_DIM)])
-    pack = jnp.stack([pack, swap_x(pack)])
-    pack = jnp.stack([pack, swap_zh(pack)])
-
+    c_got = swap_core(after(c_sent, h_send))
+
+    h_there, at_zh = lax.optimization_barrier((h_there, at_zh))
     h_message = jnp.stack([h_here[1], h_there[1]])
-    h_far = swap_zh(after(h_message, c_send))
-    qk_one = jnp.stack([s_qk, qk_zh])
-    vo_one = jnp.stack([s_vo, vo_zh])
-    qk_two, vo_two = swap_x(qk_one), swap_y(vo_one)
-    h_far = after(h_far, qk_one, vo_one)
-    s_up, s_down = after((s_up, s_down), h_far)
-
-    owned = flip(pack)
+    h_far = swap_zh(h_message)
+    at_one = jnp.stack([s_at, at_zh])
+    at_x, at_y = swap_x(at_one), swap_y(at_one)
+    c_here, c_send = deal(spots, after(c_kept, at_one, h_message), c_got)
+    c_there = swap_x(c_send)
+    h_far, c_there = lax.optimization_barrier(after((h_far, c_there), at_one))
+
+    hidden_own, stats, owned = place(spots, h_here, h_there, h_far, True)
+    owned = owned[:, : 11 * HEAD_DIM].reshape(2, 2, 11, HEAD_DIM)
     gain_one, shift_one, gain_two, shift_two, out_shift = (
         owned[:, :, i, :, None] for i in range(5)
     )
-    by_head = pack.transpose(1, 0, 2, 3)
+    by_head = flip(owned).transpose(1, 0, 2, 3)
     q_shift = by_head[:, :, 5].reshape(4, HEAD_DIM, 1)
     v_shift = by_head[:, :, 6].reshape(4, HEAD_DIM, 1)
     in_shift = by_head[:, :, 7:].reshape(UNITS, 1)
 
-    hidden_own, stats = place(spots, h_here, h_there, h_far, True)
     mean, variance = merge_stats(stats, OWN)
     inv_one = lax.rsqrt(variance + EPS)
-    inv_one, qk_two, vo_two, c_there = lax.optimization_barrier(
-        (inv_one, qk_two, vo_two, c_there)
-    )
+    s_up = after(s_up, h_far)
+    up_zh = swap_zh(s_up)
+    inv_one, at_x, at_y = lax.optimization_barrier((inv_one, at_x, at_y))
     own_one = (hidden_own - mean) * inv_one
-    w_qk = jnp.stack([qk_one, qk_two])
-    w_vo = jnp.stack([vo_one, vo_two])
-    w_qk = w_qk, swap_y(w_qk)
-    w_vo = w_vo, swap_x(w_vo)
-    up_zh = swap_zh(s_up)
+    qk_xy, vo_xy = swap_y(at_x[:, : OWN // 2]), swap_x(at_y[:, OWN // 2 :])
     low_one = (own_one * gain_one + shift_one).astype(BF)
     low_one_z = swap_zl(low_one)
-    low_one_z, up_zh = lax.optimization_barrier((low_one_z, up_zh))
-    s_down = after(s_down, up_zh)
+    low_one_z, qk_xy, vo_xy, up_zh = lax.optimization_barrier((low_one_z, qk_xy, vo_xy, up_zh))
+    w_qk = at_one, at_x, at_y, qk_xy
+    w_vo = at_one, at_x, at_y, vo_xy
+    s_down, c_message = after((s_down, jnp.stack([c_here[1], c_there[1]])), low_one_z)
     down_zh = swap_zh(s_down)
     up_one = jnp.stack([s_up, up_zh])
-    up_two = swap_x(after(up_one, w_vo[1]))
+    up_x, up_y = swap_x(after(up_one, vo_xy)), swap_y(after(up_one, qk_xy))
     wide_one = low_one, swap_core(low_one), low_one_z, swap_core(low_one_z)
-    wide_one = after(wide_one, up_one, s_down)
-
-    qk, values, ln_one = project(wide_one, w_qk, w_vo, q_shift, v_shift)
+    wide_one = after(wide_one, s_down, up_one, c_message)
+
+    qk, values, ln_one = project(wide_one, (*w_qk, vo_xy), q_shift, v_shift)
     clip_len = lax.dynamic_slice_in_dim(lengths, 4 * y + 2 * zh + x, 1)
-    qk, down_zh = lax.optimization_barrier((qk, down_zh))
+    c_message = after(c_message, qk)
+    c_far = swap_zh(c_message)
+    attended, log_sum = attend_clip(after(qk, c_message), values, clip_len, CLIP)
+    attended, up_x, up_y = lax.optimization_barrier((attended, up_x, up_y))
+    w_up = up_one, up_x, up_y, swap_y(up_x)
+    delta = fold(fill_out, w_vo, (attended,), "fold_out")
+    *delta, c_far, down_zh = lax.optimization_barrier((*delta, c_far, down_zh))
     down_one = jnp.stack([s_down, down_zh])
-    c_message = after(jnp.stack([c_here[1], c_there[1]]), down_zh)
-    down_two, c_far = swap_y(down_one), swap_zh(c_message)
-    attended, log_sum = attend_clip(after(qk, down_one, c_message), values, clip_len, CLIP)
-    delta = fold(fill_out, w_vo, (attended,), "fold_out")
-    *delta, up_two, down_two, c_far = lax.optimization_barrier(
-        (*delta, up_two, down_two, c_far)
-    )
-    w_up = jnp.stack([up_one, up_two])
-    w_down = jnp.stack([down_one, down_two])
-    w_up = w_up, swap_y(w_up)
-    w_down = w_down, swap_x(w_down)
+    down_x, down_y = swap_x(down_one), swap_y(down_one)
     delta_near, delta_send = fold_cores(delta)
-    delta_mid = delta_near + swap_zl(delta_send) + out_shift
+    delta_got, down_x, down_y = lax.optimization_barrier((swap_zl(delta_send), down_x, down_y))
+    w_down = down_one, down_x, down_y, swap_x(down_y)
+    delta_mid = delta_near + delta_got + out_shift
 
     hidden_mid = hidden_own + delta_mid
     mean, variance = merge_stats(token_stats(hidden_mid.reshape(OWN, CLIP)), OWN)
@@ -1265,27 +1306,32 @@
     low_two = (own_two * gain_two + shift_two).astype(BF)
     low_two_z = swap_zl(low_two)
     (cot_own,) = place(spots, c_here, c_there, after(c_far, low_two), False)
-    cot_own = after(cot_own, low_two_z)
+    low_two_z, cot_own, in_shift = lax.optimization_barrier((low_two_z, cot_own, in_shift))
     cot_z = swap_zl(cot_own)
     wide_two = low_two, swap_core(low_two), low_two_z, swap_core(low_two_z)
     act_low, slope, ln_two = up_project(after(wide_two, cot_own), w_up, in_shift)
-    act_low, slope, cot_z = lax.optimization_barrier((act_low, slope, cot_z))
+    out_parts = fold(fill_all, w_down, (act_low,), "fold_down")
+    *out_parts, cot_z = lax.optimization_barrier((*out_parts, cot_z))
     wide_cot = cot_own, swap_core(cot_own), cot_z, swap_core(cot_z)
-    out_near, out_send = fold_cores(fold(fill_down, w_down, (act_low,), "fold_down"))
+    out_near, out_send = fold_cores(out_parts)
     out_got = swap_zl(out_send)
 
     grad_pre, cot_all = grad_act(after(wide_cot, out_send), w_down, slope)
-    grad_pre_fold, out_got = lax.optimization_barrier((grad_pre, out_got))
-    two_near, two_send = fold_cores(fold(fill_up, w_up, (grad_pre_fold,), "fold_up"))
+    two_parts = fold(fill_all, w_up, (grad_pre,), "fold_up")
+    *two_parts, out_got = lax.optimization_barrier((*two_parts, out_got))
+    two_near, two_send = fold_cores(two_parts)
     two_got = swap_zl(two_send)
     by_unit = (2, 2, OWN, CLIP)
     act_low_after, cot_all_after = after((act_low, cot_all), two_send)
     part_down = grad_x_first((act_low_after.reshape(by_unit),), (cot_all_after,), "grad_down")
-    down_first = swap_x(part_down[1])
+    down_keep, down_first, down_later = part_down
+    down_first = swap_x(down_first)
     part_up = grad_y_first(
         after(grad_pre, part_down[1]).reshape(4, OWN, CLIP), ln_two, "grad_up"
     )
-    up_first = swap_y(part_up[1])
+    up_keep, up_first, up_later = part_up
+    up_keep = up_keep.reshape(2, 2, OWN, HALF)
+    up_first = swap_y(up_first)
     two_got = after(two_got, part_up[1])
     grad_two = two_near + two_got
 
@@ -1295,89 +1341,67 @@
         sums, meanwhile = lax.optimization_barrier((sum(group_round(sums)) / D, meanwhile))
         return inv * (scaled - sums[0] - normed * sums[1]), meanwhile
 
-    norm_two_grad, _ = norm_back(grad_two, own_two, inv_two, gain_two)
+    norm_two_grad, down_first = norm_back(grad_two, own_two, inv_two, gain_two, down_first)
     mid_own = cot_own.astype(F32) + norm_two_grad
     mid_low = mid_own.astype(BF)
     mid_z = swap_zl(mid_low)
     out_leave, out_leave_far = leave(spots, delta_mid + after(out_near, mid_low) + out_got)
-    out_leave_far, mid_z = lax.optimization_barrier((out_leave_far, mid_z))
+    down_first, down_later = after((down_first, down_later), mid_low)
+    down_later = swap_x(down_later)
+    down_send = (down_keep[1] + down_first).astype(BF)
+    down_second = swap_y(down_send)
+    out_leave_far, mid_z, up_first = lax.optimization_barrier(
+        after((out_leave_far, mid_z, up_first), down_send)
+    )
+    up_later = swap_y(after(up_later, up_first))
+    up_send = (up_keep[1] + up_first).astype(BF)
+    up_second = swap_x(up_send)
     out_far = swap_zh(out_leave_far)
     wide_mid = mid_low, swap_core(mid_low), mid_z, swap_core(mid_z)
-    wide_mid = after(wide_mid, out_leave_far)
-
-    def second_step(keep, got):
-        keep = keep.reshape(2, 2, -1, HALF) + got.reshape(2, 2, -1, HALF)
-        return keep[0], keep[1].astype(BF)
-
-    def third_step(keep, got):
-        keep = keep + got
-        return keep[0], keep[1].astype(BF)
+    wide_mid = after(wide_mid, out_leave_far, up_send)
+
+    def last_step(keep, later, second):
+        total = keep[0] + later + second
+        return total[0], total[1].astype(BF)
 
     grad_attended, mid_all = grad_attended_of(wide_mid, w_vo)
     early = attend_clip_back(qk, values, log_sum, grad_attended, clip_len, 0)
-    *early, down_first, up_first = lax.optimization_barrier((*early, down_first, up_first))
-    down_keep, down_send = second_step(part_down[0], down_first)
-    up_keep, up_send = second_step(part_up[0], up_first)
-    down_second, up_second = swap_y(down_send), swap_x(up_send)
-    grad_attended = after(grad_attended, down_send, up_send)
+    *early, down_later, down_second, out_far = lax.optimization_barrier(
+        (*early, down_later, down_second, out_far)
+    )
+    down_keep, down_send = last_step(down_keep, down_later, down_second)
+    down_third = swap_zh(down_send)
+    out_message = jnp.stack([out_leave[1], out_far[1]])
+    out_there = swap_x(out_message)
+    grad_attended = after(grad_attended, down_send, out_message)
     grad_qk, grad_v = attend_clip_back(
         qk, values, log_sum, grad_attended, clip_len, 2, tuple(early)
     )
-    grad_qk, grad_v, out_far = lax.optimization_barrier((grad_qk, grad_v, out_far))
-    out_message = jnp.stack([out_leave[1], out_far[1]])
-    out_there = swap_x(out_message)
-    folded = fold(
-        fill_project, (*w_qk, *w_vo), after((grad_qk, grad_v), out_message), "fold_project"
-    )
-    *folded, down_second, up_second = lax.optimization_barrier(
-        (*folded, down_second, up_second)
-    )
-    down_keep, down_send = third_step(down_keep, down_second)
-    up_keep, up_send = third_step(up_keep, up_second)
-    down_third, up_third = swap_zh(down_send), swap_zh(up_send)
+    grad_qk, grad_v, up_later, up_second = lax.optimization_barrier(
+        (grad_qk, grad_v, up_later, up_second)
+    )
+    up_keep, up_send = last_step(up_keep, up_later, up_second)
+    folded = fold(fill_project, (*w_qk, vo_xy), after((grad_qk, grad_v), up_send), "fold_project")
+    *folded, down_third = lax.optimization_barrier((*folded, down_third))
     one_near, one_send = fold_cores(folded)
     one_got = swap_zl(one_send)
     by_head_dims = (2, 2, HEAD_DIM, CLIP)
-    grad_v, grad_qk = after((grad_v, grad_qk), one_send, down_send, up_send)
+    grad_v, grad_qk = after((grad_v, grad_qk), one_send)
     part_vo = grad_x_first(
         (grad_v.reshape(by_head_dims), attended.reshape(by_head_dims)),
         (ln_one, mid_all),
         "grad_vo",
     )
     *part_vo, one_got = lax.optimization_barrier((*part_vo, one_got))
-    vo_first = swap_x(part_vo[1])
+    vo_keep, vo_first, vo_later = part_vo
+    vo_first = swap_x(vo_first)
     part_qk = grad_y_first(
         after(grad_qk, part_vo[1]).reshape(4, 2 * HEAD_DIM, CLIP), ln_one, "grad_qk"
     )
-    *part_qk, down_third = lax.optimization_barrier((*part_qk, down_third))
-    qk_first = swap_y(part_qk[1])
-    out_kept, out_sent = undeal(spots, out_leave, out_far, after(out_there, part_qk[1]))
-    hidden_out = finish(spots, out_kept, swap_core(out_sent), hidden_in, down_bias[:, None])
-
+    qk_keep, qk_first, qk_later = part_qk
+    qk_keep = qk_keep.reshape(2, 2, 2 * HEAD_DIM, HALF)
+    qk_first = swap_y(qk_first)
     grad_one = one_near + one_got
-    norm_one_grad, (vo_first, qk_first) = norm_back(
-        grad_one, own_one, inv_one, gain_one, (vo_first, qk_first)
-    )
-    vo_keep, vo_send = second_step(part_vo[0], vo_first)
-    vo_second = swap_y(vo_send)
-    qk_keep, qk_send = second_step(part_qk[0], qk_first)
-    qk_second = swap_x(qk_send)
-    norm_one_grad = after(norm_one_grad, qk_send, vo_send)
-    in_leave, in_leave_far = leave(spots, norm_two_grad + norm_one_grad)
-    in_far = swap_zh(in_leave_far)
-
-    up_third, vo_second = after((up_third, vo_second), in_leave_far)
-    vo_keep, vo_send = third_step(vo_keep, vo_second)
-    vo_third = swap_zh(vo_send)
-    up_third = after(up_third, vo_send)
-    ff_kept, ff_sent = store_ff(spots, up_keep + up_third, down_keep + down_third)
-    ff_got = swap_core(ff_sent)
-    in_far, qk_second = lax.optimization_barrier(after((in_far, qk_second), ff_sent))
-    in_message = jnp.stack([in_leave[1], in_far[1]])
-    in_there = swap_x(in_message)
-    qk_keep, qk_send = third_step(qk_keep, qk_second)
-    qk_third = swap_zh(qk_send)
-    g_up, g_down = join_ff(spots, ff_kept, after(ff_got, qk_send, in_message))
 
     def over_tokens(values):
         return jnp.sum(values, axis=-1, dtype=F32)
@@ -1405,7 +1429,43 @@
         axis=1,
     )
     vectors = jnp.concatenate([flip(owned), heads.reshape(2, 2, -1).transpose(1, 0, 2)], axis=2)
-    total = vectors[0] + swap_zh(vectors[1])
+    vectors_got = swap_zh(vectors[1])
+
+    up_third = swap_zh(after(up_send, one_got, vectors[1]))
+    norm_one_grad, (qk_first, vo_first, up_third) = norm_back(
+        grad_one, own_one, inv_one, gain_one, (qk_first, vo_first, up_third)
+    )
+    qk_first, vo_first = after((qk_first, vo_first), norm_one_grad)
+    vo_later = swap_x(after(vo_later, vo_first))
+    vo_send = (vo_keep[1] + vo_first).astype(BF)
+    vo_second = swap_y(vo_send)
+    qk_later = swap_y(after(qk_later, qk_first))
+    qk_send = (qk_keep[1] + qk_first).astype(BF)
+    qk_second = swap_x(qk_send)
+    in_leave, in_leave_far = leave(spots, norm_two_grad + norm_one_grad)
+    in_far = swap_zh(in_leave_far)
+    out_kept, out_sent = undeal(spots, out_leave, out_far, after(out_there, in_leave_far))
+    hidden_out = finish(spots, out_kept, swap_core(out_sent), hidden_in, down_bias[:, None])
+
+    vo_later, vo_second = after((vo_later, vo_second), in_leave_far, qk_send)
+    vo_keep, vo_send = last_step(vo_keep, vo_later, vo_second)
+    vo_third = swap_zh(vo_send)
+    ff_kept, ff_sent = store_ff(
+        spots, after(up_keep, vo_send) + up_third, down_keep + down_third
+    )
+    ff_got = swap_core(ff_sent)
+    in_far, qk_later, qk_second = lax.optimization_barrier(
+        after((in_far, qk_later, qk_second), ff_sent)
+    )
+    in_message = jnp.stack([in_leave[1], in_far[1]])
+    in_there = after(swap_x(in_message), hidden_out)
+    qk_later, qk_second = after((qk_later, qk_second), in_message)
+    qk_keep, qk_send = last_step(qk_keep, qk_later, qk_second)
+    qk_third = swap_zh(qk_send)
+    g_up, g_down = join_ff(spots, ff_kept, after(ff_got, qk_send, in_message))
+
+    total = vectors[0] + after(vectors_got, in_leave_far)
+    total = after(total, in_there)
     total = total[0] + swap_x(total[1])
     total = total + swap_y(total)
     other = swap_core(total)

time: 504 us -> 463 us (0.919)
  waiting for transfers between devices: 148 us -> 116 us
  other arithmetic: 53.9 us -> 47.4 us
    ppermute x14 -> x16, waiting for transfers between devices: 4.77 us -> 43 us  [swap_x(): return lax.ppermute(values, 'col', [(i, i ^ 1) for i in range(8)])]
    ppermute x12, waiting for transfers between devices: 52.8 us -> 18.1 us  [swap_zl(): return lax.ppermute(values, 'col', [(i, i ^ 2) for i in range(8)])]
    ppermute x14 -> x12, waiting for transfers between devices: 60.7 us -> 40.9 us  [swap_zh(): return lax.ppermute(values, 'col', [(i, i ^ 4) for i in range(8)])]
    ppermute x9 -> x12, waiting for transfers between devices: 13.6 us -> 3.69 us  [swap_y(): return lax.ppermute(values, 'row', [(i, i ^ 2) for i in range(4)])]
    add x10 -> x6, other arithmetic: 15.2 us -> 6.6 us  [the longest x4 4.56 us: last_step(): total = keep[0] + later + second]
    convert_element_type x0 -> x4, other arithmetic: none -> 6.61 us  [the longest x1 2.52 us: local_clip(): up_send = (up_keep[1] + up_first).astype(BF)]
    ppermute x14 -> x12, starting transfers between devices: 19.8 us -> 13.5 us  [swap_zh(): return lax.ppermute(values, 'col', [(i, i ^ 4) for i in range(8)])]
    ppermute x12, starting transfers between devices: 15.5 us -> 9.34 us  [swap_zl(): return lax.ppermute(values, 'col', [(i, i ^ 2) for i in range(8)])]
  transfers between devices with their start and end apart: 77 -> 80, of which waited for: 34 -> 28; matrix products, arithmetic and copies ran while one was open for 11% -> 12% of each run, Pallas kernels for 30% -> 37%
where the time goes in v3:
time: 463 us; the launch traced here: 457 us
  Pallas kernels  178 us (38%)
  waiting for transfers between devices  116 us (25%)
  starting transfers between devices  80.7 us (17%)
  other arithmetic  47.4 us (10%)
  local copies, waits for them, and re-layouts  33.7 us (7%)
    ppermute x16, waiting for transfers between devices, swap_x(): return lax.ppermute(values, 'col', [(i, i ^ 1) for i in range(8)])  43 us
    ppermute x12, waiting for transfers between devices, swap_zh(): return lax.ppermute(values, 'col', [(i, i ^ 4) for i in range(8)])  40.9 us
    pallas_call x4, Pallas kernels, fold(): pl.pallas_call(functools.partial(fold_kernel, fill, (len(sources), len(va...  31.7 us
    ppermute x24, starting transfers between devices, swap_core(): return lax.ppermute(values, 'row', [(i, i ^ 1) for i in range(4)])  27.7 us
    pallas_call x2, Pallas kernels, attend_clip_back(): pl.pallas_call(attend_back_kernel, grid_spec=pltpu.PrefetchScalarGridSpec...  20.9 us
    ppermute x12, waiting for transfers between devices, swap_zl(): return lax.ppermute(values, 'col', [(i, i ^ 2) for i in range(8)])  18.1 us
    pallas_call x2, Pallas kernels, grad_x_first(): pl.pallas_call(functools.partial(pair_x_kernel, len(lefts)), grid=(2,), i...  18.1 us
    ppermute x16, starting transfers between devices, swap_x(): return lax.ppermute(values, 'col', [(i, i ^ 1) for i in range(8)])  15.2 us
  transfers between devices with their start and end apart: 80, of which 28 were waited for; matrix products, arithmetic and copies ran while one was open for 12% of the time, Pallas kernels for 37%

profile of v3, /device:TPU:1, one launch (start us, length us, event | category | flops | bytes accessed | tf_op | source)
XLA Modules:
  0.0 456.9 jit_solution(3170646063277220772)
XLA Ops:
  1.5 4.4 prepare_weights.1
  7.3 3.9 split_in.1
  24.6 6.2 %collective-permute-done.2.there_ref = bf16[2,88,1024]{2,1,0:T(8,128)(2,1)S(1)} collective-permute-done((bf16[2,88,1024]{2,1,0:T(8,128)(2,1)}, bf16[2,88,1024]{2,1,0:T(8,128)(2,1)S(1)}, u32[]{:S(2)}, u32[]{:S(2)}) %collective-permute-start.2) | collective-permute-done | bytes 360480 | tf_op jit(solution)/shard_map/ppermute | solution.py:379
  30.8 6.2 %collective-permute-done.3 = bf16[320,640]{1,0:T(8,128)(2,1)S(1)} collective-permute-done((bf16[320,640]{1,0:T(8,128)(2,1)}, bf16[320,640]{1,0:T(8,128)(2,1)S(1)}, u32[]{:S(2)}, u32[]{:S(2)}) %collective-permute-start.3) | collective-permute-done | bytes 409632 | tf_op jit(solution)/shard_map/ppermute | solution.py:387
  42.6 6.1 %collective-permute-done.6.there_ref = bf16[2,80,1024]{2,1,0:T(8,128)(2,1)} collective-permute-done((bf16[2,80,1024]{2,1,0:T(8,128)(2,1)}, bf16[2,80,1024]{2,1,0:T(8,128)(2,1)}, u32[]{:S(2)}, u32[]{:S(2)}) %collective-permute-start.6) | collective-permute-done | bytes 327712 | tf_op jit(solution)/shard_map/ppermute | solution.py:379
  48.6 6.1 %collective-permute-done.4.far_ref = bf16[2,88,1024]{2,1,0:T(8,128)(2,1)S(1)} collective-permute-done((bf16[2,88,1024]{2,1,0:T(8,128)(2,1)S(1)}, bf16[2,88,1024]{2,1,0:T(8,128)(2,1)S(1)}, u32[]{:S(2)}, u32[]{:S(2)}) %collective-permute-start.4) | collective-permute-done | bytes 360480 | tf_op jit(solution)/shard_map/ppermute | solution.py:387
  69.1 4.3 collective-permute-start.12
  79.9 15.1 %collective-permute-done.15 = bf16[320,640]{1,0:T(8,128)(2,1)S(1)} collective-permute-done((bf16[320,640]{1,0:T(8,128)(2,1)}, bf16[320,640]{1,0:T(8,128)(2,1)S(1)}, u32[]{:S(2)}, u32[]{:S(2)}) %collective-permute-start.15) | collective-permute-done | bytes 409632 | tf_op jit(solution)/shard_map/ppermute | solution.py:387
  106.5 7.5 %project.1 = (bf16[4,2,80,1024]{3,2,1,0:T(8,128)(2,1)}, bf16[4,80,1024]{2,1,0:T(8,128)(2,1)}, bf16[1280,1024]{1,0:T(8,128)(2,1)}) custom-call(bf16[2,2,80,1024]{3,2,1,0:T(8,128)(2,1)} %add_convert_fusion.6.refs_0_, bf16[2,2,80,1024]{3,2,1,0:T(8,128)(2,1)} %collective-permute-done.16.refs_1_, bf16[2,2,80,1024]{3,2,1,0:T(8,128)(2,1)} %collective-permute-done.12.refs_2_, ...), custom_call_target="tpu_custom_call" | custom-call | flops 1 | bytes 1 | tf_op jit(solution)/shard_map/project/pallas_call | solution.py:945
  114.7 10.3 %attend_clip.1 = (bf16[4,80,1024]{2,1,0:T(8,128)(2,1)}, f32[4,1,1024]{2,1,0:T(1,128)}) custom-call(s32[1]{0:T(128)} %dynamic_slice.3.len_ref, bf16[4,2,80,1024]{3,2,1,0:T(8,128)(2,1)} %get-tuple-element.249.q_ref.k_ref, bf16[4,2,80,1024]{3,2,1,0:T(8,128)(2,1)} %get-tuple-element.249.q_ref.k_ref, bf16[4,80,1024]{2,1,0:T(8,128)(2,1)} %get-tuple-element.250.v_ref), custom_call_target="tpu_custom_call" | custom-call | flops 1 | bytes 1 | tf_op jit(solution)/shard_map/attend_clip/pallas_call | solution.py:443
  125.1 6.6 %fold_out.1 = (f32[2,2,2,80,1024]{4,3,2,1,0:T(8,128)}, bf16[2,2,2,80,1024]{4,3,2,1,0:T(8,128)(2,1)}) custom-call(bf16[2,320,640]{2,1,0:T(8,128)(2,1)} %copy-done.3, bf16[2,320,640]{2,1,0:T(8,128)(2,1)} %copy-done.4, bf16[2,320,640]{2,1,0:T(8,128)(2,1)} %copy-done.5, bf16[2,160,640]{2,1,0:T(8,128)(2,1)} %copy-done.14, ...), custom_call_target="tpu_custom_call" | custom-call | flops 1 | bytes 1 | tf_op jit(solution)/shard_map/fold_out/pallas_call | solution.py:1062
  131.7 6.1 %collective-permute-done.20.far_ref = bf16[2,80,1024]{2,1,0:T(8,128)(2,1)S(1)} collective-permute-done((bf16[2,80,1024]{2,1,0:T(8,128)(2,1)S(1)}, bf16[2,80,1024]{2,1,0:T(8,128)(2,1)S(1)}, u32[]{:S(2)}, u32[]{:S(2)}) %collective-permute-start.20) | collective-permute-done | bytes 327712 | tf_op jit(solution)/shard_map/ppermute | solution.py:387
  143.3 16.4 %collective-permute-done.24.refs_1_.refs_5_ = bf16[2,320,640]{2,1,0:T(8,128)(2,1)S(1)} collective-permute-done((bf16[2,320,640]{2,1,0:T(8,128)(2,1)S(1)}, bf16[2,320,640]{2,1,0:T(8,128)(2,1)S(1)}, u32[]{:S(2)}, u32[]{:S(2)}) %collective-permute-start.24) | collective-permute-done | bytes 819232 | tf_op jit(solution)/shard_map/ppermute | solution.py:379
  172.9 9.7 %collective-permute-done.31.refs_2_ = bf16[2,2,80,1024]{3,2,1,0:T(8,128)(2,1)} collective-permute-done((bf16[2,2,80,1024]{3,2,1,0:T(8,128)(2,1)}, bf16[2,2,80,1024]{3,2,1,0:T(8,128)(2,1)}, u32[]{:S(2)}, u32[]{:S(2)}) %collective-permute-start.31) | collective-permute-done | bytes 655392 | tf_op jit(solution)/shard_map/ppermute | solution.py:383
  187.8 10.3 %up_project.1 = (bf16[1280,1024]{1,0:T(8,128)(2,1)}, f32[1280,1024]{1,0:T(8,128)}, bf16[1280,1024]{1,0:T(8,128)(2,1)}) custom-call(bf16[2,2,80,1024]{3,2,1,0:T(8,128)(2,1)} %add_convert_fusion.4.refs_0_, bf16[2,2,80,1024]{3,2,1,0:T(8,128)(2,1)} %collective-permute-done.30.refs_1_, bf16[2,2,80,1024]{3,2,1,0:T(8,128)(2,1)} %collective-permute-done.31.refs_2_, ...), custom_call_target="tpu_custom_call" | custom-call | flops 1 | bytes 1 | tf_op jit(solution)/shard_map/up_project/pallas_call | solution.py:975
  198.1 8.6 %fold_down.1 = (f32[2,2,2,80,1024]{4,3,2,1,0:T(8,128)}, bf16[2,2,2,80,1024]{4,3,2,1,0:T(8,128)(2,1)}) custom-call(bf16[2,320,640]{2,1,0:T(8,128)(2,1)} %copy-done.13, bf16[2,320,640]{2,1,0:T(8,128)(2,1)} %copy-done.27, bf16[2,320,640]{2,1,0:T(8,128)(2,1)} %collective-permute-done.25.refs_2_.refs_6_, ...), custom_call_target="tpu_custom_call" | custom-call | flops 1 | bytes 1 | tf_op jit(solution)/shard_map/fold_down/pallas_call | solution.py:1062
  216.1 9.1 %grad_act.1 = (bf16[1280,1024]{1,0:T(8,128)(2,1)}, bf16[1280,1024]{1,0:T(8,128)(2,1)}) custom-call(bf16[2,2,80,1024]{3,2,1,0:T(8,128)(2,1)} %place_in.3.refs_0_, bf16[2,2,80,1024]{3,2,1,0:T(8,128)(2,1)} %copy-done.45, bf16[2,2,80,1024]{3,2,1,0:T(8,128)(2,1)} %collective-permute-done.34.refs_2_, bf16[2,2,80,1024]{3,2,1,0:T(8,128)(2,1)} %copy-done.46, ...), custom_call_target="tpu_custom_call" | custom-call | flops 1 | bytes 1 | tf_op jit(solution)/shard_map/grad_act/pallas_call | solution.py:1002
  225.2 8.6 %fold_up.1 = (f32[2,2,2,80,1024]{4,3,2,1,0:T(8,128)}, bf16[2,2,2,80,1024]{4,3,2,1,0:T(8,128)(2,1)}) custom-call(bf16[2,320,640]{2,1,0:T(8,128)(2,1)} %copy-done.12, bf16[2,320,640]{2,1,0:T(8,128)(2,1)} %copy-done.24, bf16[2,320,640]{2,1,0:T(8,128)(2,1)} %copy-done.23, bf16[2,320,640]{2,1,0:T(8,128)(2,1)} %copy-done.25, ...), custom_call_target="tpu_custom_call" | custom-call | flops 1 | bytes 1 | tf_op jit(solution)/shard_map/fold_up/pallas_call | solution.py:1062
  240.6 7.4 %grad_down.1 = (f32[2,2,320,640]{3,2,1,0:T(8,128)}, bf16[2,320,640]{2,1,0:T(8,128)(2,1)}, bf16[2,320,640]{2,1,0:T(8,128)(2,1)}) custom-call(bf16[2,2,320,1024]{3,2,1,0:T(8,128)(2,1)} %bitcast.142, bf16[1280,1024]{1,0:T(8,128)(2,1)} %get-tuple-element.292.refs_1_), custom_call_target="tpu_custom_call" | custom-call | flops 1 | bytes 1 | tf_op jit(solution)/shard_map/grad_down/pallas_call | solution.py:1141
  249.2 8.0 %grad_up.1 = (f32[4,320,640]{2,1,0:T(8,128)}, bf16[2,320,640]{2,1,0:T(8,128)(2,1)}, bf16[2,320,640]{2,1,0:T(8,128)(2,1)}) custom-call(bf16[4,320,1024]{2,1,0:T(8,128)(2,1)} %bitcast.139, bf16[1280,1024]{1,0:T(8,128)(2,1)} %get-tuple-element.295.right_ref), custom_call_target="tpu_custom_call" | custom-call | flops 1 | bytes 1 | tf_op jit(solution)/shard_map/grad_up/pallas_call | solution.py:1107
  291.1 5.6 %grad_attended.1 = (bf16[4,80,1024]{2,1,0:T(8,128)(2,1)}, bf16[1280,1024]{1,0:T(8,128)(2,1)}) custom-call(bf16[2,2,80,1024]{3,2,1,0:T(8,128)(2,1)} %copy-done.30, bf16[2,2,80,1024]{3,2,1,0:T(8,128)(2,1)} %copy-done.44, bf16[2,2,80,1024]{3,2,1,0:T(8,128)(2,1)} %collective-permute-done.46.refs_2_, bf16[2,2,80,1024]{3,2,1,0:T(8,128)(2,1)} %copy-done.47, ...), custom_call_target="tpu_custom_call" | custom-call | flops 1 | bytes 1 | tf_op jit(solution)/shard_map/grad_attended/pallas_call | solution.py:1027
  296.7 10.5 %attend_clip_back.2 = (bf16[4,2,80,1024]{3,2,1,0:T(8,128)(2,1)}, bf16[4,80,1024]{2,1,0:T(8,128)(2,1)}) custom-call(s32[1]{0:T(128)} %dynamic_slice.3.len_ref, bf16[4,2,80,1024]{3,2,1,0:T(8,128)(2,1)} %get-tuple-element.249.q_ref.k_ref, bf16[4,2,80,1024]{3,2,1,0:T(8,128)(2,1)} %get-tuple-element.249.q_ref.k_ref, ...), custom_call_target="tpu_custom_call" | custom-call | flops 1 | bytes 1 | tf_op jit(solution)/shard_map/attend_clip_back/pallas_call | solution.py:491
  314.3 10.5 %attend_clip_back.3 = (bf16[4,2,80,1024]{3,2,1,0:T(8,128)(2,1)}, bf16[4,80,1024]{2,1,0:T(8,128)(2,1)}) custom-call(s32[1]{0:T(128)} %dynamic_slice.3.len_ref, bf16[4,2,80,1024]{3,2,1,0:T(8,128)(2,1)} %get-tuple-element.249.q_ref.k_ref, bf16[4,2,80,1024]{3,2,1,0:T(8,128)(2,1)} %get-tuple-element.249.q_ref.k_ref, ...), custom_call_target="tpu_custom_call", output_to_operand_aliasing={{0}: (6, {}), {1}: (7, {})} | custom-call | flops 1 | bytes 1 | tf_op jit(solution)/shard_map/attend_clip_back/pallas_call | solution.py:491
  328.4 7.9 %fold_project.1 = (f32[2,2,2,80,1024]{4,3,2,1,0:T(8,128)}, bf16[2,2,2,80,1024]{4,3,2,1,0:T(8,128)(2,1)}) custom-call(bf16[2,320,640]{2,1,0:T(8,128)(2,1)} %copy-done.3, bf16[2,320,640]{2,1,0:T(8,128)(2,1)} %copy-done.4, bf16[2,320,640]{2,1,0:T(8,128)(2,1)} %copy-done.5, bf16[2,160,640]{2,1,0:T(8,128)(2,1)} %copy-done.33, bf16[2,160,640]{2,1,0:T(8,128)(2,1)} %copy-done.14, ...), custom_call_target="tpu_custom_call" | custom-call | flops 1 | bytes 1 | tf_op jit(solution)/shard_map/fold_project/pallas_call | solution.py:1062
  344.3 10.7 %grad_vo.1 = (f32[2,2,160,640]{3,2,1,0:T(8,128)}, bf16[2,160,640]{2,1,0:T(8,128)(2,1)}, bf16[2,160,640]{2,1,0:T(8,128)(2,1)}) custom-call(bf16[2,2,80,1024]{3,2,1,0:T(8,128)(2,1)} %bitcast.141, bf16[2,2,80,1024]{3,2,1,0:T(8,128)(2,1)} %bitcast.143, bf16[1280,1024]{1,0:T(8,128)(2,1)} %get-tuple-element.344.refs_2_.right_ref, ...), custom_call_target="tpu_custom_call" | custom-call | flops 1 | bytes 1 | tf_op jit(solution)/shard_map/grad_vo/pallas_call | solution.py:1141
  355.4 3.9 collective-permute-done.57
  366.3 7.1 %grad_qk.1 = (f32[4,160,640]{2,1,0:T(8,128)}, bf16[2,160,640]{2,1,0:T(8,128)(2,1)}, bf16[2,160,640]{2,1,0:T(8,128)(2,1)}) custom-call(bf16[4,160,1024]{2,1,0:T(8,128)(2,1)} %bitcast.140, bf16[1280,1024]{1,0:T(8,128)(2,1)} %get-tuple-element.344.refs_2_.right_ref), custom_call_target="tpu_custom_call" | custom-call | flops 1 | bytes 1 | tf_op jit(solution)/shard_map/grad_qk/pallas_call | solution.py:1107
  379.7 7.4 %collective-permute-done.63 = bf16[320,640]{1,0:T(8,128)(2,1)} collective-permute-done((bf16[320,640]{1,0:T(8,128)(2,1)S(1)}, bf16[320,640]{1,0:T(8,128)(2,1)}, u32[]{:S(2)}, u32[]{:S(2)}) %collective-permute-start.63) | collective-permute-done | bytes 409632 | tf_op jit(solution)/shard_map/ppermute | solution.py:387
  400.3 4.0 finish.2
  410.0 4.0 store_ff.1
  418.0 7.1 %collective-permute-done.70.there_ref = bf16[2,80,1024]{2,1,0:T(8,128)(2,1)} collective-permute-done((bf16[2,80,1024]{2,1,0:T(8,128)(2,1)S(1)}, bf16[2,80,1024]{2,1,0:T(8,128)(2,1)}, u32[]{:S(2)}, u32[]{:S(2)}) %collective-permute-start.70) | collective-permute-done | bytes 327712 | tf_op jit(solution)/shard_map/ppermute | solution.py:379
  449.8 3.9 finish.3
  (428 shorter events, 211.9 us)
Async XLA Ops:
  15.3 21.7 %collective-permute-start.3 = (bf16[320,640]{1,0:T(8,128)(2,1)}, bf16[320,640]{1,0:T(8,128)(2,1)S(1)}, u32[]{:S(2)}, u32[]{:S(2)}) collective-permute-start(bf16[320,640]{1,0:T(8,128)(2,1)} %get-tuple-element.209), channel_id=1, source_target_pairs={{0,4},{1,5},{2,6},{3,7},{4,0},{5,1},{6,2},{7,3},{8,12},{9,13},{10,... | collective-permute-start | bytes 1228808 | tf_op jit(solution)/shard_map/ppermute | solution.py:387
  41.1 25.0 %collective-permute-start.10 = (bf16[2,320,640]{2,1,0:T(8,128)(2,1)S(1)}, bf16[2,320,640]{2,1,0:T(8,128)(2,1)S(1)}, u32[]{:S(2)}, u32[]{:S(2)}) collective-permute-start(bf16[2,320,640]{2,1,0:T(8,128)(2,1)S(1)} %pad_maximum_fusion.refs_4_.refs_0_), channel_id=1, source_target_pairs={{0,1},{1,0},{2,3},{3,2},{4,5},{5,4},{6,7},{7,6},{8,9},{9,8},{10,11... | collective-permute-start | bytes 2457608 | tf_op jit(solution)/shard_map/ppermute | solution.py:379
  41.6 24.5 %collective-permute-start.11 = (bf16[2,320,640]{2,1,0:T(8,128)(2,1)S(1)}, bf16[2,320,640]{2,1,0:T(8,128)(2,1)S(1)}, u32[]{:S(2)}, u32[]{:S(2)}) collective-permute-start(bf16[2,320,640]{2,1,0:T(8,128)(2,1)S(1)} %pad_maximum_fusion.refs_4_.refs_0_), channel_id=1, source_target_pairs={{0,16},{8,24},{16,0},{24,8},{1,17},{9,25},{17,1},{25,9},{2,18},{10... | collective-permute-start | bytes 2457608 | tf_op jit(solution)/shard_map/ppermute | solution.py:375
  69.1 26.9 %collective-permute-start.12 = (bf16[2,2,80,1024]{3,2,1,0:T(8,128)(2,1)}, bf16[2,2,80,1024]{3,2,1,0:T(8,128)(2,1)}, u32[]{:S(2)}, u32[]{:S(2)}) collective-permute-start(bf16[2,2,80,1024]{3,2,1,0:T(8,128)(2,1)} %add_convert_fusion.6.refs_0_), channel_id=1, source_target_pairs={{0,2},{1,3},{2,0},{3,1},{4,6},{5,7},{6,4},{7,5},{8,10},{9,11},{10,... | collective-permute-start | bytes 1966088 | tf_op jit(solution)/shard_map/ppermute | solution.py:383
  73.4 21.6 %collective-permute-start.15 = (bf16[320,640]{1,0:T(8,128)(2,1)}, bf16[320,640]{1,0:T(8,128)(2,1)S(1)}, u32[]{:S(2)}, u32[]{:S(2)}) collective-permute-start(bf16[320,640]{1,0:T(8,128)(2,1)} %get-tuple-element.233), channel_id=1, source_target_pairs={{0,4},{1,5},{2,6},{3,7},{4,0},{5,1},{6,2},{7,3},{8,12},{9,13},{10,... | collective-permute-start | bytes 1228808 | tf_op jit(solution)/shard_map/ppermute | solution.py:387
  73.7 21.2 %collective-permute-start.13 = (bf16[2,160,640]{2,1,0:T(8,128)(2,1)S(1)}, bf16[2,160,640]{2,1,0:T(8,128)(2,1)S(1)}, u32[]{:S(2)}, u32[]{:S(2)}) collective-permute-start(bf16[2,160,640]{2,1,0:T(8,128)(2,1)S(1)} %slice.290), channel_id=1, source_target_pairs={{0,16},{8,24},{16,0},{24,8},{1,17},{9,25},{17,1},{25,9},{2,18},{10... | collective-permute-start | bytes 1228808 | tf_op jit(solution)/shard_map/ppermute | solution.py:375
  75.1 19.9 %collective-permute-start.14 = (bf16[2,160,640]{2,1,0:T(8,128)(2,1)S(1)}, bf16[2,160,640]{2,1,0:T(8,128)(2,1)S(1)}, u32[]{:S(2)}, u32[]{:S(2)}) collective-permute-start(bf16[2,160,640]{2,1,0:T(8,128)(2,1)S(1)} %slice.291), channel_id=1, source_target_pairs={{0,1},{1,0},{2,3},{3,2},{4,5},{5,4},{6,7},{7,6},{8,9},{9,8},{10,11... | collective-permute-start | bytes 1228808 | tf_op jit(solution)/shard_map/ppermute | solution.py:379
  77.3 29.2 %collective-permute-start.16 = (bf16[2,2,80,1024]{3,2,1,0:T(8,128)(2,1)}, bf16[2,2,80,1024]{3,2,1,0:T(8,128)(2,1)}, u32[]{:S(2)}, u32[]{:S(2)}) collective-permute-start(bf16[2,2,80,1024]{3,2,1,0:T(8,128)(2,1)} %add_convert_fusion.6.refs_0_), channel_id=1, source_target_pairs={{0,8},{8,0},{16,24},{24,16},{1,9},{9,1},{17,25},{25,17},{2,10},{10... | collective-permute-start | bytes 1966088 | tf_op jit(solution)/shard_map/ppermute | solution.py:371
  99.3 25.8 %collective-permute-start.19 = (bf16[2,320,640]{2,1,0:T(8,128)(2,1)S(1)}, bf16[2,320,640]{2,1,0:T(8,128)(2,1)S(1)}, u32[]{:S(2)}, u32[]{:S(2)}) collective-permute-start(bf16[2,320,640]{2,1,0:T(8,128)(2,1)S(1)} %pad_maximum_fusion.1.refs_4_.refs_0_), channel_id=1, source_target_pairs={{0,16},{8,24},{16,0},{24,8},{1,17},{9,25},{17,1},{25,9},{2,18},{10... | collective-permute-start | bytes 2457608 | tf_op jit(solution)/shard_map/ppermute | solution.py:375
  100.6 24.5 %collective-permute-start.18 = (bf16[2,320,640]{2,1,0:T(8,128)(2,1)S(1)}, bf16[2,320,640]{2,1,0:T(8,128)(2,1)S(1)}, u32[]{:S(2)}, u32[]{:S(2)}) collective-permute-start(bf16[2,320,640]{2,1,0:T(8,128)(2,1)S(1)} %pad_maximum_fusion.1.refs_4_.refs_0_), channel_id=1, source_target_pairs={{0,1},{1,0},{2,3},{3,2},{4,5},{5,4},{6,7},{7,6},{8,9},{9,8},{10,11... | collective-permute-start | bytes 2457608 | tf_op jit(solution)/shard_map/ppermute | solution.py:379
  102.5 29.2 %collective-permute-start.21 = (bf16[320,640]{1,0:T(8,128)(2,1)}, bf16[320,640]{1,0:T(8,128)(2,1)}, u32[]{:S(2)}, u32[]{:S(2)}) collective-permute-start(bf16[320,640]{1,0:T(8,128)(2,1)} %get-tuple-element.239), channel_id=1, source_target_pairs={{0,4},{1,5},{2,6},{3,7},{4,0},{5,1},{6,2},{7,3},{8,12},{9,13},{10,... | collective-permute-start | bytes 1228808 | tf_op jit(solution)/shard_map/ppermute | solution.py:387
  114.1 23.8 %collective-permute-start.20 = (bf16[2,80,1024]{2,1,0:T(8,128)(2,1)S(1)}, bf16[2,80,1024]{2,1,0:T(8,128)(2,1)S(1)}, u32[]{:S(2)}, u32[]{:S(2)}) collective-permute-start(bf16[2,80,1024]{2,1,0:T(8,128)(2,1)S(1)} %copy-done.55), channel_id=1, source_target_pairs={{0,4},{1,5},{2,6},{3,7},{4,0},{5,1},{6,2},{7,3},{8,12},{9,13},{10,... | collective-permute-start | bytes 983048 | tf_op jit(solution)/shard_map/ppermute | solution.py:387
  139.8 20.0 %collective-permute-start.24 = (bf16[2,320,640]{2,1,0:T(8,128)(2,1)S(1)}, bf16[2,320,640]{2,1,0:T(8,128)(2,1)S(1)}, u32[]{:S(2)}, u32[]{:S(2)}) collective-permute-start(bf16[2,320,640]{2,1,0:T(8,128)(2,1)S(1)} %pad_maximum_fusion.2.refs_0_.refs_4_), channel_id=1, source_target_pairs={{0,1},{1,0},{2,3},{3,2},{4,5},{5,4},{6,7},{7,6},{8,9},{9,8},{10,11... | collective-permute-start | bytes 2457608 | tf_op jit(solution)/shard_map/ppermute | solution.py:379
  140.1 19.6 %collective-permute-start.25 = (bf16[2,320,640]{2,1,0:T(8,128)(2,1)S(1)}, bf16[2,320,640]{2,1,0:T(8,128)(2,1)}, u32[]{:S(2)}, u32[]{:S(2)}) collective-permute-start(bf16[2,320,640]{2,1,0:T(8,128)(2,1)S(1)} %pad_maximum_fusion.2.refs_0_.refs_4_), channel_id=1, source_target_pairs={{0,16},{8,24},{16,0},{24,8},{1,17},{9,25},{17,1},{25,9},{2,18},{10... | collective-permute-start | bytes 2457608 | tf_op jit(solution)/shard_map/ppermute | solution.py:375
  167.6 19.3 %collective-permute-start.33 = (bf16[2,320,640]{2,1,0:T(8,128)(2,1)S(1)}, bf16[2,320,640]{2,1,0:T(8,128)(2,1)S(1)}, u32[]{:S(2)}, u32[]{:S(2)}) collective-permute-start(bf16[2,320,640]{2,1,0:T(8,128)(2,1)S(1)} %collective-permute-done.18.refs_5_.refs_1_), channel_id=1, source_target_pairs={{0,16},{8,24},{16,0},{24,8},{1,17},{9,25},{17,1},{25,9},{2,18},{10... | collective-permute-start | bytes 2457608 | tf_op jit(solution)/shard_map/ppermute | solution.py:375
  167.9 30.2 %collective-permute-start.26 = (bf16[2,320,640]{2,1,0:T(8,128)(2,1)}, bf16[2,320,640]{2,1,0:T(8,128)(2,1)}, u32[]{:S(2)}, u32[]{:S(2)}) collective-permute-start(bf16[2,320,640]{2,1,0:T(8,128)(2,1)} %collective-permute-done.25.refs_2_.refs_6_), channel_id=1, source_target_pairs={{0,1},{1,0},{2,3},{3,2},{4,5},{5,4},{6,7},{7,6},{8,9},{9,8},{10,11... | collective-permute-start | bytes 2457608 | tf_op jit(solution)/shard_map/ppermute | solution.py:379
  183.9 22.8 %collective-permute-start.34 = (bf16[2,2,80,1024]{3,2,1,0:T(8,128)(2,1)}, bf16[2,2,80,1024]{3,2,1,0:T(8,128)(2,1)}, u32[]{:S(2)}, u32[]{:S(2)}) collective-permute-start(bf16[2,2,80,1024]{3,2,1,0:T(8,128)(2,1)} %place_in.3.refs_0_), channel_id=1, source_target_pairs={{0,2},{1,3},{2,0},{3,1},{4,6},{5,7},{6,4},{7,5},{8,10},{9,11},{10,... | collective-permute-start | bytes 1966088 | tf_op jit(solution)/shard_map/ppermute | solution.py:383
  214.0 19.7 %collective-permute-start.38 = (bf16[2,2,80,1024]{3,2,1,0:T(8,128)(2,1)}, bf16[2,2,80,1024]{3,2,1,0:T(8,128)(2,1)}, u32[]{:S(2)}, u32[]{:S(2)}) collective-permute-start(bf16[2,2,80,1024]{3,2,1,0:T(8,128)(2,1)} %get-tuple-element.424), channel_id=1, source_target_pairs={{0,2},{1,3},{2,0},{3,1},{4,6},{5,7},{6,4},{7,5},{8,10},{9,11},{10,... | collective-permute-start | bytes 1966088 | tf_op jit(solution)/shard_map/ppermute | solution.py:383
  248.0 19.5 %collective-permute-start.44 = (bf16[2,320,640]{2,1,0:T(8,128)(2,1)}, bf16[2,320,640]{2,1,0:T(8,128)(2,1)}, u32[]{:S(2)}, u32[]{:S(2)}) collective-permute-start(bf16[2,320,640]{2,1,0:T(8,128)(2,1)} %get-tuple-element.293), channel_id=1, source_target_pairs={{0,1},{1,0},{2,3},{3,2},{4,5},{5,4},{6,7},{7,6},{8,9},{9,8},{10,11... | collective-permute-start | bytes 2457608 | tf_op jit(solution)/shard_map/ppermute | solution.py:379
  262.4 20.0 %collective-permute-start.47 = (bf16[2,320,640]{2,1,0:T(8,128)(2,1)}, bf16[2,320,640]{2,1,0:T(8,128)(2,1)S(1)}, u32[]{:S(2)}, u32[]{:S(2)}) collective-permute-start(bf16[2,320,640]{2,1,0:T(8,128)(2,1)} %get-tuple-element.296), channel_id=1, source_target_pairs={{0,16},{8,24},{16,0},{24,8},{1,17},{9,25},{17,1},{25,9},{2,18},{10... | collective-permute-start | bytes 2457608 | tf_op jit(solution)/shard_map/ppermute | solution.py:375
  272.3 34.9 %collective-permute-start.50 = (bf16[2,320,640]{2,1,0:T(8,128)(2,1)}, bf16[2,320,640]{2,1,0:T(8,128)(2,1)}, u32[]{:S(2)}, u32[]{:S(2)}) collective-permute-start(bf16[2,320,640]{2,1,0:T(8,128)(2,1)} %fusion.1), channel_id=1, source_target_pairs={{0,16},{8,24},{16,0},{24,8},{1,17},{9,25},{17,1},{25,9},{2,18},{10... | collective-permute-start | bytes 2457608 | tf_op jit(solution)/shard_map/ppermute | solution.py:375
  272.5 34.7 %collective-permute-start.49 = (bf16[2,320,640]{2,1,0:T(8,128)(2,1)}, bf16[2,320,640]{2,1,0:T(8,128)(2,1)}, u32[]{:S(2)}, u32[]{:S(2)}) collective-permute-start(bf16[2,320,640]{2,1,0:T(8,128)(2,1)} %get-tuple-element.322), channel_id=1, source_target_pairs={{0,1},{1,0},{2,3},{3,2},{4,5},{5,4},{6,7},{7,6},{8,9},{9,8},{10,11... | collective-permute-start | bytes 2457608 | tf_op jit(solution)/shard_map/ppermute | solution.py:379
  286.6 20.6 %collective-permute-start.51 = (bf16[2,80,1024]{2,1,0:T(8,128)(2,1)}, bf16[2,80,1024]{2,1,0:T(8,128)(2,1)}, u32[]{:S(2)}, u32[]{:S(2)}) collective-permute-start(bf16[2,80,1024]{2,1,0:T(8,128)(2,1)} %get-tuple-element.312), channel_id=1, source_target_pairs={{0,4},{1,5},{2,6},{3,7},{4,0},{5,1},{6,2},{7,3},{8,12},{9,13},{10,... | collective-permute-start | bytes 983048 | tf_op jit(solution)/shard_map/ppermute | solution.py:387
  289.6 35.1 %collective-permute-start.53 = (bf16[2,320,640]{2,1,0:T(8,128)(2,1)}, bf16[2,320,640]{2,1,0:T(8,128)(2,1)}, u32[]{:S(2)}, u32[]{:S(2)}) collective-permute-start(bf16[2,320,640]{2,1,0:T(8,128)(2,1)} %get-tuple-element.332), channel_id=1, source_target_pairs={{0,16},{8,24},{16,0},{24,8},{1,17},{9,25},{17,1},{25,9},{2,18},{10... | collective-permute-start | bytes 2457608 | tf_op jit(solution)/shard_map/ppermute | solution.py:375
  289.9 34.9 %collective-permute-start.54 = (bf16[2,320,640]{2,1,0:T(8,128)(2,1)}, bf16[2,320,640]{2,1,0:T(8,128)(2,1)}, u32[]{:S(2)}, u32[]{:S(2)}) collective-permute-start(bf16[2,320,640]{2,1,0:T(8,128)(2,1)} %add_convert_fusion), channel_id=1, source_target_pairs={{0,1},{1,0},{2,3},{3,2},{4,5},{5,4},{6,7},{7,6},{8,9},{9,8},{10,11... | collective-permute-start | bytes 2457608 | tf_op jit(solution)/shard_map/ppermute | solution.py:379
  311.7 24.6 %collective-permute-start.55 = (bf16[320,640]{1,0:T(8,128)(2,1)}, bf16[320,640]{1,0:T(8,128)(2,1)}, u32[]{:S(2)}, u32[]{:S(2)}) collective-permute-start(bf16[320,640]{1,0:T(8,128)(2,1)} %fusion.12), channel_id=1, source_target_pairs={{0,4},{1,5},{2,6},{3,7},{4,0},{5,1},{6,2},{7,3},{8,12},{9,13},{10,... | collective-permute-start | bytes 1228808 | tf_op jit(solution)/shard_map/ppermute | solution.py:387
  364.8 22.2 %collective-permute-start.62 = (bf16[2,160,640]{2,1,0:T(8,128)(2,1)}, bf16[2,160,640]{2,1,0:T(8,128)(2,1)S(1)}, u32[]{:S(2)}, u32[]{:S(2)}) collective-permute-start(bf16[2,160,640]{2,1,0:T(8,128)(2,1)} %get-tuple-element.351), channel_id=1, source_target_pairs={{0,1},{1,0},{2,3},{3,2},{4,5},{5,4},{6,7},{7,6},{8,9},{9,8},{10,11... | collective-permute-start | bytes 1228808 | tf_op jit(solution)/shard_map/ppermute | solution.py:379
  365.7 21.3 %collective-permute-start.63 = (bf16[320,640]{1,0:T(8,128)(2,1)S(1)}, bf16[320,640]{1,0:T(8,128)(2,1)}, u32[]{:S(2)}, u32[]{:S(2)}) collective-permute-start(bf16[320,640]{1,0:T(8,128)(2,1)S(1)} %copy-done.49), channel_id=1, source_target_pairs={{0,4},{1,5},{2,6},{3,7},{4,0},{5,1},{6,2},{7,3},{8,12},{9,13},{10,... | collective-permute-start | bytes 1228808 | tf_op jit(solution)/shard_map/ppermute | solution.py:387
  377.9 21.1 %collective-permute-start.72 = (f32[2,960]{1,0:T(2,128)S(1)}, f32[2,960]{1,0:T(2,128)S(1)}, u32[]{:S(2)}, u32[]{:S(2)}) collective-permute-start(f32[2,960]{1,0:T(2,128)S(1)} %fusion.21), channel_id=1, source_target_pairs={{0,4},{1,5},{2,6},{3,7},{4,0},{5,1},{6,2},{7,3},{8,12},{9,13},{10,... | collective-permute-start | bytes 23048 | tf_op jit(solution)/shard_map/ppermute | solution.py:387
  394.8 19.9 %collective-permute-start.65 = (bf16[2,80,1024]{2,1,0:T(8,128)(2,1)}, bf16[2,80,1024]{2,1,0:T(8,128)(2,1)}, u32[]{:S(2)}, u32[]{:S(2)}) collective-permute-start(bf16[2,80,1024]{2,1,0:T(8,128)(2,1)} %get-tuple-element.356), channel_id=1, source_target_pairs={{0,4},{1,5},{2,6},{3,7},{4,0},{5,1},{6,2},{7,3},{8,12},{9,13},{10,... | collective-permute-start | bytes 983048 | tf_op jit(solution)/shard_map/ppermute | solution.py:387
  407.4 28.7 %collective-permute-start.77 = (bf16[160,640]{1,0:T(8,128)(2,1)}, bf16[160,640]{1,0:T(8,128)(2,1)}, u32[]{:S(2)}, u32[]{:S(2)}) collective-permute-start(bf16[160,640]{1,0:T(8,128)(2,1)} %fusion.17), channel_id=1, source_target_pairs={{0,4},{1,5},{2,6},{3,7},{4,0},{5,1},{6,2},{7,3},{8,12},{9,13},{10,... | collective-permute-start | bytes 614408 | tf_op jit(solution)/shard_map/ppermute | solution.py:387
  414.1 19.2 %collective-permute-start.78 = (f32[320,640]{1,0:T(8,128)}, f32[320,640]{1,0:T(8,128)}, u32[]{:S(2)}, u32[]{:S(2)}) collective-permute-start(f32[320,640]{1,0:T(8,128)} %get-tuple-element.376), channel_id=1, source_target_pairs={{0,8},{8,0},{16,24},{24,16},{1,9},{9,1},{17,25},{25,17},{2,10},{10... | collective-permute-start | bytes 2457608 | tf_op jit(solution)/shard_map/ppermute | solution.py:371
  (118 other events, 943.6 us)

commit v4 on v3

--- a/solution.py
+++ b/solution.py
@@ -1341,7 +1341,7 @@
         sums, meanwhile = lax.optimization_barrier((sum(group_round(sums)) / D, meanwhile))
         return inv * (scaled - sums[0] - normed * sums[1]), meanwhile
 
-    norm_two_grad, down_first = norm_back(grad_two, own_two, inv_two, gain_two, down_first)
+    norm_two_grad, _ = norm_back(grad_two, own_two, inv_two, gain_two)
     mid_own = cot_own.astype(F32) + norm_two_grad
     mid_low = mid_own.astype(BF)
     mid_z = swap_zl(mid_low)

time: 463 us -> 468 us (1.011)
  waiting for transfers between devices: 116 us -> 125 us
    ppermute x16, waiting for transfers between devices: 43 us -> 55.8 us  [swap_x(): return lax.ppermute(values, 'col', [(i, i ^ 1) for i in range(8)])]
    unnamed x140 -> x142, local copies, waits for them, and re-layouts: 13 us -> 12.9 us
  transfers between devices with their start and end apart: 80 -> 80, of which waited for: 28 -> 25; matrix products, arithmetic and copies ran while one was open for 12% -> 11% of each run, Pallas kernels for 37% -> 36%
where the time goes in v4:
time: 468 us; the launch traced here: 461 us
  Pallas kernels  178 us (38%)
  waiting for transfers between devices  125 us (27%)
  starting transfers between devices  77.4 us (17%)
  other arithmetic  46.2 us (10%)
  local copies, waits for them, and re-layouts  33.6 us (7%)
    ppermute x16, waiting for transfers between devices, swap_x(): return lax.ppermute(values, 'col', [(i, i ^ 1) for i in range(8)])  55.8 us
    ppermute x12, waiting for transfers between devices, swap_zh(): return lax.ppermute(values, 'col', [(i, i ^ 4) for i in range(8)])  41.5 us
    pallas_call x4, Pallas kernels, fold(): pl.pallas_call(functools.partial(fold_kernel, fill, (len(sources), len(va...  31.8 us
    ppermute x24, starting transfers between devices, swap_core(): return lax.ppermute(values, 'row', [(i, i ^ 1) for i in range(4)])  25.8 us
    pallas_call x2, Pallas kernels, attend_clip_back(): pl.pallas_call(attend_back_kernel, grid_spec=pltpu.PrefetchScalarGridSpec...  20.9 us
    pallas_call x2, Pallas kernels, grad_x_first(): pl.pallas_call(functools.partial(pair_x_kernel, len(lefts)), grid=(2,), i...  18.1 us
    pallas_call x2, Pallas kernels, grad_y_first(): pl.pallas_call(pair_y_kernel, grid=(4,), in_specs=[pl.BlockSpec((1, rows,...  15.1 us
    ppermute x12, waiting for transfers between devices, swap_zl(): return lax.ppermute(values, 'col', [(i, i ^ 2) for i in range(8)])  14.4 us
  transfers between devices with their start and end apart: 80, of which 25 were waited for; matrix products, arithmetic and copies ran while one was open for 11% of the time, Pallas kernels for 36%

profile of v4, /device:TPU:1, one launch (start us, length us, event | category | flops | bytes accessed | tf_op | source)
XLA Modules:
  0.0 461.5 jit_solution(9116399095629438198)
XLA Ops:
  1.4 4.4 prepare_weights.1
  7.3 3.8 split_in.1
  24.6 6.2 %collective-permute-done.2.there_ref = bf16[2,88,1024]{2,1,0:T(8,128)(2,1)S(1)} collective-permute-done((bf16[2,88,1024]{2,1,0:T(8,128)(2,1)}, bf16[2,88,1024]{2,1,0:T(8,128)(2,1)S(1)}, u32[]{:S(2)}, u32[]{:S(2)}) %collective-permute-start.2) | collective-permute-done | bytes 360480 | tf_op jit(solution)/shard_map/ppermute | solution.py:379
  30.8 6.2 %collective-permute-done.3 = bf16[320,640]{1,0:T(8,128)(2,1)S(1)} collective-permute-done((bf16[320,640]{1,0:T(8,128)(2,1)}, bf16[320,640]{1,0:T(8,128)(2,1)S(1)}, u32[]{:S(2)}, u32[]{:S(2)}) %collective-permute-start.3) | collective-permute-done | bytes 409632 | tf_op jit(solution)/shard_map/ppermute | solution.py:387
  42.5 6.1 %collective-permute-done.6.there_ref = bf16[2,80,1024]{2,1,0:T(8,128)(2,1)} collective-permute-done((bf16[2,80,1024]{2,1,0:T(8,128)(2,1)}, bf16[2,80,1024]{2,1,0:T(8,128)(2,1)}, u32[]{:S(2)}, u32[]{:S(2)}) %collective-permute-start.6) | collective-permute-done | bytes 327712 | tf_op jit(solution)/shard_map/ppermute | solution.py:379
  48.6 6.1 %collective-permute-done.4.far_ref = bf16[2,88,1024]{2,1,0:T(8,128)(2,1)S(1)} collective-permute-done((bf16[2,88,1024]{2,1,0:T(8,128)(2,1)S(1)}, bf16[2,88,1024]{2,1,0:T(8,128)(2,1)S(1)}, u32[]{:S(2)}, u32[]{:S(2)}) %collective-permute-start.4) | collective-permute-done | bytes 360480 | tf_op jit(solution)/shard_map/ppermute | solution.py:387
  69.1 4.3 collective-permute-start.12
  79.8 15.1 %collective-permute-done.15 = bf16[320,640]{1,0:T(8,128)(2,1)S(1)} collective-permute-done((bf16[320,640]{1,0:T(8,128)(2,1)}, bf16[320,640]{1,0:T(8,128)(2,1)S(1)}, u32[]{:S(2)}, u32[]{:S(2)}) %collective-permute-start.15) | collective-permute-done | bytes 409632 | tf_op jit(solution)/shard_map/ppermute | solution.py:387
  106.5 7.5 %project.1 = (bf16[4,2,80,1024]{3,2,1,0:T(8,128)(2,1)}, bf16[4,80,1024]{2,1,0:T(8,128)(2,1)}, bf16[1280,1024]{1,0:T(8,128)(2,1)}) custom-call(bf16[2,2,80,1024]{3,2,1,0:T(8,128)(2,1)} %add_convert_fusion.6.refs_0_, bf16[2,2,80,1024]{3,2,1,0:T(8,128)(2,1)} %collective-permute-done.16.refs_1_, bf16[2,2,80,1024]{3,2,1,0:T(8,128)(2,1)} %collective-permute-done.12.refs_2_, ...), custom_call_target="tpu_custom_call" | custom-call | flops 1 | bytes 1 | tf_op jit(solution)/shard_map/project/pallas_call | solution.py:945
  114.7 10.3 %attend_clip.1 = (bf16[4,80,1024]{2,1,0:T(8,128)(2,1)}, f32[4,1,1024]{2,1,0:T(1,128)}) custom-call(s32[1]{0:T(128)} %dynamic_slice.3.len_ref, bf16[4,2,80,1024]{3,2,1,0:T(8,128)(2,1)} %get-tuple-element.247.q_ref.k_ref, bf16[4,2,80,1024]{3,2,1,0:T(8,128)(2,1)} %get-tuple-element.247.q_ref.k_ref, bf16[4,80,1024]{2,1,0:T(8,128)(2,1)} %get-tuple-element.248.v_ref), custom_call_target="tpu_custom_call" | custom-call | flops 1 | bytes 1 | tf_op jit(solution)/shard_map/attend_clip/pallas_call | solution.py:443
  125.1 6.6 %fold_out.1 = (f32[2,2,2,80,1024]{4,3,2,1,0:T(8,128)}, bf16[2,2,2,80,1024]{4,3,2,1,0:T(8,128)(2,1)}) custom-call(bf16[2,320,640]{2,1,0:T(8,128)(2,1)} %copy-done.3, bf16[2,320,640]{2,1,0:T(8,128)(2,1)} %copy-done.4, bf16[2,320,640]{2,1,0:T(8,128)(2,1)} %copy-done.5, bf16[2,160,640]{2,1,0:T(8,128)(2,1)} %copy-done.14, ...), custom_call_target="tpu_custom_call" | custom-call | flops 1 | bytes 1 | tf_op jit(solution)/shard_map/fold_out/pallas_call | solution.py:1062
  131.7 6.1 %collective-permute-done.20.far_ref = bf16[2,80,1024]{2,1,0:T(8,128)(2,1)S(1)} collective-permute-done((bf16[2,80,1024]{2,1,0:T(8,128)(2,1)S(1)}, bf16[2,80,1024]{2,1,0:T(8,128)(2,1)S(1)}, u32[]{:S(2)}, u32[]{:S(2)}) %collective-permute-start.20) | collective-permute-done | bytes 327712 | tf_op jit(solution)/shard_map/ppermute | solution.py:387
  143.3 16.4 %collective-permute-done.24.refs_1_.refs_5_ = bf16[2,320,640]{2,1,0:T(8,128)(2,1)S(1)} collective-permute-done((bf16[2,320,640]{2,1,0:T(8,128)(2,1)S(1)}, bf16[2,320,640]{2,1,0:T(8,128)(2,1)S(1)}, u32[]{:S(2)}, u32[]{:S(2)}) %collective-permute-start.24) | collective-permute-done | bytes 819232 | tf_op jit(solution)/shard_map/ppermute | solution.py:379
  172.9 9.7 %collective-permute-done.31.refs_2_ = bf16[2,2,80,1024]{3,2,1,0:T(8,128)(2,1)} collective-permute-done((bf16[2,2,80,1024]{3,2,1,0:T(8,128)(2,1)}, bf16[2,2,80,1024]{3,2,1,0:T(8,128)(2,1)}, u32[]{:S(2)}, u32[]{:S(2)}) %collective-permute-start.31) | collective-permute-done | bytes 655392 | tf_op jit(solution)/shard_map/ppermute | solution.py:383
  187.8 10.3 %up_project.1 = (bf16[1280,1024]{1,0:T(8,128)(2,1)}, f32[1280,1024]{1,0:T(8,128)}, bf16[1280,1024]{1,0:T(8,128)(2,1)}) custom-call(bf16[2,2,80,1024]{3,2,1,0:T(8,128)(2,1)} %add_convert_fusion.4.refs_0_, bf16[2,2,80,1024]{3,2,1,0:T(8,128)(2,1)} %collective-permute-done.30.refs_1_, bf16[2,2,80,1024]{3,2,1,0:T(8,128)(2,1)} %collective-permute-done.31.refs_2_, ...), custom_call_target="tpu_custom_call" | custom-call | flops 1 | bytes 1 | tf_op jit(solution)/shard_map/up_project/pallas_call | solution.py:975
  198.1 8.6 %fold_down.1 = (f32[2,2,2,80,1024]{4,3,2,1,0:T(8,128)}, bf16[2,2,2,80,1024]{4,3,2,1,0:T(8,128)(2,1)}) custom-call(bf16[2,320,640]{2,1,0:T(8,128)(2,1)} %copy-done.13, bf16[2,320,640]{2,1,0:T(8,128)(2,1)} %copy-done.27, bf16[2,320,640]{2,1,0:T(8,128)(2,1)} %collective-permute-done.25.refs_2_.refs_6_, ...), custom_call_target="tpu_custom_call" | custom-call | flops 1 | bytes 1 | tf_op jit(solution)/shard_map/fold_down/pallas_call | solution.py:1062
  216.1 9.1 %grad_act.1 = (bf16[1280,1024]{1,0:T(8,128)(2,1)}, bf16[1280,1024]{1,0:T(8,128)(2,1)}) custom-call(bf16[2,2,80,1024]{3,2,1,0:T(8,128)(2,1)} %place_in.3.refs_0_, bf16[2,2,80,1024]{3,2,1,0:T(8,128)(2,1)} %copy-done.45, bf16[2,2,80,1024]{3,2,1,0:T(8,128)(2,1)} %collective-permute-done.34.refs_2_, bf16[2,2,80,1024]{3,2,1,0:T(8,128)(2,1)} %copy-done.46, ...), custom_call_target="tpu_custom_call" | custom-call | flops 1 | bytes 1 | tf_op jit(solution)/shard_map/grad_act/pallas_call | solution.py:1002
  225.2 8.7 %fold_up.1 = (f32[2,2,2,80,1024]{4,3,2,1,0:T(8,128)}, bf16[2,2,2,80,1024]{4,3,2,1,0:T(8,128)(2,1)}) custom-call(bf16[2,320,640]{2,1,0:T(8,128)(2,1)} %copy-done.12, bf16[2,320,640]{2,1,0:T(8,128)(2,1)} %copy-done.24, bf16[2,320,640]{2,1,0:T(8,128)(2,1)} %copy-done.23, bf16[2,320,640]{2,1,0:T(8,128)(2,1)} %copy-done.25, ...), custom_call_target="tpu_custom_call" | custom-call | flops 1 | bytes 1 | tf_op jit(solution)/shard_map/fold_up/pallas_call | solution.py:1062
  240.7 7.4 %grad_down.1 = (f32[2,2,320,640]{3,2,1,0:T(8,128)}, bf16[2,320,640]{2,1,0:T(8,128)(2,1)}, bf16[2,320,640]{2,1,0:T(8,128)(2,1)}) custom-call(bf16[2,2,320,1024]{3,2,1,0:T(8,128)(2,1)} %bitcast.142, bf16[1280,1024]{1,0:T(8,128)(2,1)} %get-tuple-element.290.refs_1_), custom_call_target="tpu_custom_call" | custom-call | flops 1 | bytes 1 | tf_op jit(solution)/shard_map/grad_down/pallas_call | solution.py:1141
  248.1 8.0 %grad_up.1 = (f32[4,320,640]{2,1,0:T(8,128)}, bf16[2,320,640]{2,1,0:T(8,128)(2,1)}, bf16[2,320,640]{2,1,0:T(8,128)(2,1)}) custom-call(bf16[4,320,1024]{2,1,0:T(8,128)(2,1)} %bitcast.139, bf16[1280,1024]{1,0:T(8,128)(2,1)} %get-tuple-element.293.right_ref), custom_call_target="tpu_custom_call" | custom-call | flops 1 | bytes 1 | tf_op jit(solution)/shard_map/grad_up/pallas_call | solution.py:1107
  266.0 15.0 %collective-permute-done.47 = bf16[2,320,640]{2,1,0:T(8,128)(2,1)S(1)} collective-permute-done((bf16[2,320,640]{2,1,0:T(8,128)(2,1)S(1)}, bf16[2,320,640]{2,1,0:T(8,128)(2,1)S(1)}, u32[]{:S(2)}, u32[]{:S(2)}) %collective-permute-start.47) | collective-permute-done | bytes 819232 | tf_op jit(solution)/shard_map/ppermute | solution.py:379
  296.2 5.6 %grad_attended.1 = (bf16[4,80,1024]{2,1,0:T(8,128)(2,1)}, bf16[1280,1024]{1,0:T(8,128)(2,1)}) custom-call(bf16[2,2,80,1024]{3,2,1,0:T(8,128)(2,1)} %copy-done.30, bf16[2,2,80,1024]{3,2,1,0:T(8,128)(2,1)} %copy-done.44, bf16[2,2,80,1024]{3,2,1,0:T(8,128)(2,1)} %collective-permute-done.45.refs_2_, bf16[2,2,80,1024]{3,2,1,0:T(8,128)(2,1)} %copy-done.47, ...), custom_call_target="tpu_custom_call" | custom-call | flops 1 | bytes 1 | tf_op jit(solution)/shard_map/grad_attended/pallas_call | solution.py:1027
  301.8 10.5 %attend_clip_back.2 = (bf16[4,2,80,1024]{3,2,1,0:T(8,128)(2,1)}, bf16[4,80,1024]{2,1,0:T(8,128)(2,1)}) custom-call(s32[1]{0:T(128)} %dynamic_slice.3.len_ref, bf16[4,2,80,1024]{3,2,1,0:T(8,128)(2,1)} %get-tuple-element.247.q_ref.k_ref, bf16[4,2,80,1024]{3,2,1,0:T(8,128)(2,1)} %get-tuple-element.247.q_ref.k_ref, ...), custom_call_target="tpu_custom_call" | custom-call | flops 1 | bytes 1 | tf_op jit(solution)/shard_map/attend_clip_back/pallas_call | solution.py:491
  318.4 10.4 %attend_clip_back.3 = (bf16[4,2,80,1024]{3,2,1,0:T(8,128)(2,1)}, bf16[4,80,1024]{2,1,0:T(8,128)(2,1)}) custom-call(s32[1]{0:T(128)} %dynamic_slice.3.len_ref, bf16[4,2,80,1024]{3,2,1,0:T(8,128)(2,1)} %get-tuple-element.247.q_ref.k_ref, bf16[4,2,80,1024]{3,2,1,0:T(8,128)(2,1)} %get-tuple-element.247.q_ref.k_ref, ...), custom_call_target="tpu_custom_call", output_to_operand_aliasing={{0}: (6, {}), {1}: (7, {})} | custom-call | flops 1 | bytes 1 | tf_op jit(solution)/shard_map/attend_clip_back/pallas_call | solution.py:491
  332.6 7.9 %fold_project.1 = (f32[2,2,2,80,1024]{4,3,2,1,0:T(8,128)}, bf16[2,2,2,80,1024]{4,3,2,1,0:T(8,128)(2,1)}) custom-call(bf16[2,320,640]{2,1,0:T(8,128)(2,1)} %copy-done.3, bf16[2,320,640]{2,1,0:T(8,128)(2,1)} %copy-done.4, bf16[2,320,640]{2,1,0:T(8,128)(2,1)} %copy-done.5, bf16[2,160,640]{2,1,0:T(8,128)(2,1)} %copy-done.33, bf16[2,160,640]{2,1,0:T(8,128)(2,1)} %copy-done.14, ...), custom_call_target="tpu_custom_call" | custom-call | flops 1 | bytes 1 | tf_op jit(solution)/shard_map/fold_project/pallas_call | solution.py:1062
  349.4 10.7 %grad_vo.1 = (f32[2,2,160,640]{3,2,1,0:T(8,128)}, bf16[2,160,640]{2,1,0:T(8,128)(2,1)}, bf16[2,160,640]{2,1,0:T(8,128)(2,1)}) custom-call(bf16[2,2,80,1024]{3,2,1,0:T(8,128)(2,1)} %bitcast.141, bf16[2,2,80,1024]{3,2,1,0:T(8,128)(2,1)} %bitcast.143, bf16[1280,1024]{1,0:T(8,128)(2,1)} %get-tuple-element.340.refs_2_.right_ref, ...), custom_call_target="tpu_custom_call" | custom-call | flops 1 | bytes 1 | tf_op jit(solution)/shard_map/grad_vo/pallas_call | solution.py:1141
  371.9 7.1 %grad_qk.1 = (f32[4,160,640]{2,1,0:T(8,128)}, bf16[2,160,640]{2,1,0:T(8,128)(2,1)}, bf16[2,160,640]{2,1,0:T(8,128)(2,1)}) custom-call(bf16[4,160,1024]{2,1,0:T(8,128)(2,1)} %bitcast.140, bf16[1280,1024]{1,0:T(8,128)(2,1)} %get-tuple-element.340.refs_2_.right_ref), custom_call_target="tpu_custom_call" | custom-call | flops 1 | bytes 1 | tf_op jit(solution)/shard_map/grad_qk/pallas_call | solution.py:1107
  383.0 7.9 %collective-permute-done.63 = bf16[320,640]{1,0:T(8,128)(2,1)} collective-permute-done((bf16[320,640]{1,0:T(8,128)(2,1)S(1)}, bf16[320,640]{1,0:T(8,128)(2,1)}, u32[]{:S(2)}, u32[]{:S(2)}) %collective-permute-start.63) | collective-permute-done | bytes 409632 | tf_op jit(solution)/shard_map/ppermute | solution.py:387
  404.6 4.0 finish.2
  414.3 4.0 store_ff.1
  422.2 7.5 %collective-permute-done.70.there_ref = bf16[2,80,1024]{2,1,0:T(8,128)(2,1)} collective-permute-done((bf16[2,80,1024]{2,1,0:T(8,128)(2,1)S(1)}, bf16[2,80,1024]{2,1,0:T(8,128)(2,1)}, u32[]{:S(2)}, u32[]{:S(2)}) %collective-permute-start.70) | collective-permute-done | bytes 327712 | tf_op jit(solution)/shard_map/ppermute | solution.py:379
  454.4 3.9 finish.3
  (430 shorter events, 204.3 us)
Async XLA Ops:
  15.3 21.7 %collective-permute-start.3 = (bf16[320,640]{1,0:T(8,128)(2,1)}, bf16[320,640]{1,0:T(8,128)(2,1)S(1)}, u32[]{:S(2)}, u32[]{:S(2)}) collective-permute-start(bf16[320,640]{1,0:T(8,128)(2,1)} %get-tuple-element.207), channel_id=1, source_target_pairs={{0,4},{1,5},{2,6},{3,7},{4,0},{5,1},{6,2},{7,3},{8,12},{9,13},{10,... | collective-permute-start | bytes 1228808 | tf_op jit(solution)/shard_map/ppermute | solution.py:387
  41.0 25.0 %collective-permute-start.10 = (bf16[2,320,640]{2,1,0:T(8,128)(2,1)S(1)}, bf16[2,320,640]{2,1,0:T(8,128)(2,1)S(1)}, u32[]{:S(2)}, u32[]{:S(2)}) collective-permute-start(bf16[2,320,640]{2,1,0:T(8,128)(2,1)S(1)} %pad_maximum_fusion.refs_4_.refs_0_), channel_id=1, source_target_pairs={{0,1},{1,0},{2,3},{3,2},{4,5},{5,4},{6,7},{7,6},{8,9},{9,8},{10,11... | collective-permute-start | bytes 2457608 | tf_op jit(solution)/shard_map/ppermute | solution.py:379
  41.6 24.5 %collective-permute-start.11 = (bf16[2,320,640]{2,1,0:T(8,128)(2,1)S(1)}, bf16[2,320,640]{2,1,0:T(8,128)(2,1)S(1)}, u32[]{:S(2)}, u32[]{:S(2)}) collective-permute-start(bf16[2,320,640]{2,1,0:T(8,128)(2,1)S(1)} %pad_maximum_fusion.refs_4_.refs_0_), channel_id=1, source_target_pairs={{0,16},{8,24},{16,0},{24,8},{1,17},{9,25},{17,1},{25,9},{2,18},{10... | collective-permute-start | bytes 2457608 | tf_op jit(solution)/shard_map/ppermute | solution.py:375
  69.1 26.9 %collective-permute-start.12 = (bf16[2,2,80,1024]{3,2,1,0:T(8,128)(2,1)}, bf16[2,2,80,1024]{3,2,1,0:T(8,128)(2,1)}, u32[]{:S(2)}, u32[]{:S(2)}) collective-permute-start(bf16[2,2,80,1024]{3,2,1,0:T(8,128)(2,1)} %add_convert_fusion.6.refs_0_), channel_id=1, source_target_pairs={{0,2},{1,3},{2,0},{3,1},{4,6},{5,7},{6,4},{7,5},{8,10},{9,11},{10,... | collective-permute-start | bytes 1966088 | tf_op jit(solution)/shard_map/ppermute | solution.py:383
  73.4 21.6 %collective-permute-start.15 = (bf16[320,640]{1,0:T(8,128)(2,1)}, bf16[320,640]{1,0:T(8,128)(2,1)S(1)}, u32[]{:S(2)}, u32[]{:S(2)}) collective-permute-start(bf16[320,640]{1,0:T(8,128)(2,1)} %get-tuple-element.231), channel_id=1, source_target_pairs={{0,4},{1,5},{2,6},{3,7},{4,0},{5,1},{6,2},{7,3},{8,12},{9,13},{10,... | collective-permute-start | bytes 1228808 | tf_op jit(solution)/shard_map/ppermute | solution.py:387
  73.7 21.2 %collective-permute-start.13 = (bf16[2,160,640]{2,1,0:T(8,128)(2,1)S(1)}, bf16[2,160,640]{2,1,0:T(8,128)(2,1)S(1)}, u32[]{:S(2)}, u32[]{:S(2)}) collective-permute-start(bf16[2,160,640]{2,1,0:T(8,128)(2,1)S(1)} %slice.290), channel_id=1, source_target_pairs={{0,16},{8,24},{16,0},{24,8},{1,17},{9,25},{17,1},{25,9},{2,18},{10... | collective-permute-start | bytes 1228808 | tf_op jit(solution)/shard_map/ppermute | solution.py:375
  75.1 19.9 %collective-permute-start.14 = (bf16[2,160,640]{2,1,0:T(8,128)(2,1)S(1)}, bf16[2,160,640]{2,1,0:T(8,128)(2,1)S(1)}, u32[]{:S(2)}, u32[]{:S(2)}) collective-permute-start(bf16[2,160,640]{2,1,0:T(8,128)(2,1)S(1)} %slice.291), channel_id=1, source_target_pairs={{0,1},{1,0},{2,3},{3,2},{4,5},{5,4},{6,7},{7,6},{8,9},{9,8},{10,11... | collective-permute-start | bytes 1228808 | tf_op jit(solution)/shard_map/ppermute | solution.py:379
  77.3 29.2 %collective-permute-start.16 = (bf16[2,2,80,1024]{3,2,1,0:T(8,128)(2,1)}, bf16[2,2,80,1024]{3,2,1,0:T(8,128)(2,1)}, u32[]{:S(2)}, u32[]{:S(2)}) collective-permute-start(bf16[2,2,80,1024]{3,2,1,0:T(8,128)(2,1)} %add_convert_fusion.6.refs_0_), channel_id=1, source_target_pairs={{0,8},{8,0},{16,24},{24,16},{1,9},{9,1},{17,25},{25,17},{2,10},{10... | collective-permute-start | bytes 1966088 | tf_op jit(solution)/shard_map/ppermute | solution.py:371
  99.3 25.8 %collective-permute-start.19 = (bf16[2,320,640]{2,1,0:T(8,128)(2,1)S(1)}, bf16[2,320,640]{2,1,0:T(8,128)(2,1)S(1)}, u32[]{:S(2)}, u32[]{:S(2)}) collective-permute-start(bf16[2,320,640]{2,1,0:T(8,128)(2,1)S(1)} %pad_maximum_fusion.1.refs_4_.refs_0_), channel_id=1, source_target_pairs={{0,16},{8,24},{16,0},{24,8},{1,17},{9,25},{17,1},{25,9},{2,18},{10... | collective-permute-start | bytes 2457608 | tf_op jit(solution)/shard_map/ppermute | solution.py:375
  100.6 24.5 %collective-permute-start.18 = (bf16[2,320,640]{2,1,0:T(8,128)(2,1)S(1)}, bf16[2,320,640]{2,1,0:T(8,128)(2,1)S(1)}, u32[]{:S(2)}, u32[]{:S(2)}) collective-permute-start(bf16[2,320,640]{2,1,0:T(8,128)(2,1)S(1)} %pad_maximum_fusion.1.refs_4_.refs_0_), channel_id=1, source_target_pairs={{0,1},{1,0},{2,3},{3,2},{4,5},{5,4},{6,7},{7,6},{8,9},{9,8},{10,11... | collective-permute-start | bytes 2457608 | tf_op jit(solution)/shard_map/ppermute | solution.py:379
  102.5 29.2 %collective-permute-start.21 = (bf16[320,640]{1,0:T(8,128)(2,1)}, bf16[320,640]{1,0:T(8,128)(2,1)}, u32[]{:S(2)}, u32[]{:S(2)}) collective-permute-start(bf16[320,640]{1,0:T(8,128)(2,1)} %get-tuple-element.237), channel_id=1, source_target_pairs={{0,4},{1,5},{2,6},{3,7},{4,0},{5,1},{6,2},{7,3},{8,12},{9,13},{10,... | collective-permute-start | bytes 1228808 | tf_op jit(solution)/shard_map/ppermute | solution.py:387
  114.0 23.8 %collective-permute-start.20 = (bf16[2,80,1024]{2,1,0:T(8,128)(2,1)S(1)}, bf16[2,80,1024]{2,1,0:T(8,128)(2,1)S(1)}, u32[]{:S(2)}, u32[]{:S(2)}) collective-permute-start(bf16[2,80,1024]{2,1,0:T(8,128)(2,1)S(1)} %copy-done.55), channel_id=1, source_target_pairs={{0,4},{1,5},{2,6},{3,7},{4,0},{5,1},{6,2},{7,3},{8,12},{9,13},{10,... | collective-permute-start | bytes 983048 | tf_op jit(solution)/shard_map/ppermute | solution.py:387
  139.7 20.0 %collective-permute-start.24 = (bf16[2,320,640]{2,1,0:T(8,128)(2,1)S(1)}, bf16[2,320,640]{2,1,0:T(8,128)(2,1)S(1)}, u32[]{:S(2)}, u32[]{:S(2)}) collective-permute-start(bf16[2,320,640]{2,1,0:T(8,128)(2,1)S(1)} %pad_maximum_fusion.2.refs_0_.refs_4_), channel_id=1, source_target_pairs={{0,1},{1,0},{2,3},{3,2},{4,5},{5,4},{6,7},{7,6},{8,9},{9,8},{10,11... | collective-permute-start | bytes 2457608 | tf_op jit(solution)/shard_map/ppermute | solution.py:379
  140.1 19.6 %collective-permute-start.25 = (bf16[2,320,640]{2,1,0:T(8,128)(2,1)S(1)}, bf16[2,320,640]{2,1,0:T(8,128)(2,1)}, u32[]{:S(2)}, u32[]{:S(2)}) collective-permute-start(bf16[2,320,640]{2,1,0:T(8,128)(2,1)S(1)} %pad_maximum_fusion.2.refs_0_.refs_4_), channel_id=1, source_target_pairs={{0,16},{8,24},{16,0},{24,8},{1,17},{9,25},{17,1},{25,9},{2,18},{10... | collective-permute-start | bytes 2457608 | tf_op jit(solution)/shard_map/ppermute | solution.py:375
  167.8 30.2 %collective-permute-start.26 = (bf16[2,320,640]{2,1,0:T(8,128)(2,1)}, bf16[2,320,640]{2,1,0:T(8,128)(2,1)}, u32[]{:S(2)}, u32[]{:S(2)}) collective-permute-start(bf16[2,320,640]{2,1,0:T(8,128)(2,1)} %collective-permute-done.25.refs_2_.refs_6_), channel_id=1, source_target_pairs={{0,1},{1,0},{2,3},{3,2},{4,5},{5,4},{6,7},{7,6},{8,9},{9,8},{10,11... | collective-permute-start | bytes 2457608 | tf_op jit(solution)/shard_map/ppermute | solution.py:379
  183.9 22.8 %collective-permute-start.34 = (bf16[2,2,80,1024]{3,2,1,0:T(8,128)(2,1)}, bf16[2,2,80,1024]{3,2,1,0:T(8,128)(2,1)}, u32[]{:S(2)}, u32[]{:S(2)}) collective-permute-start(bf16[2,2,80,1024]{3,2,1,0:T(8,128)(2,1)} %place_in.3.refs_0_), channel_id=1, source_target_pairs={{0,2},{1,3},{2,0},{3,1},{4,6},{5,7},{6,4},{7,5},{8,10},{9,11},{10,... | collective-permute-start | bytes 1966088 | tf_op jit(solution)/shard_map/ppermute | solution.py:383
  214.1 19.8 %collective-permute-start.38 = (bf16[2,2,80,1024]{3,2,1,0:T(8,128)(2,1)}, bf16[2,2,80,1024]{3,2,1,0:T(8,128)(2,1)}, u32[]{:S(2)}, u32[]{:S(2)}) collective-permute-start(bf16[2,2,80,1024]{3,2,1,0:T(8,128)(2,1)} %get-tuple-element.420), channel_id=1, source_target_pairs={{0,2},{1,3},{2,0},{3,1},{4,6},{5,7},{6,4},{7,5},{8,10},{9,11},{10,... | collective-permute-start | bytes 1966088 | tf_op jit(solution)/shard_map/ppermute | solution.py:383
  261.2 19.8 %collective-permute-start.47 = (bf16[2,320,640]{2,1,0:T(8,128)(2,1)S(1)}, bf16[2,320,640]{2,1,0:T(8,128)(2,1)S(1)}, u32[]{:S(2)}, u32[]{:S(2)}) collective-permute-start(bf16[2,320,640]{2,1,0:T(8,128)(2,1)S(1)} %copy-done.68), channel_id=1, source_target_pairs={{0,1},{1,0},{2,3},{3,2},{4,5},{5,4},{6,7},{7,6},{8,9},{9,8},{10,11... | collective-permute-start | bytes 2457608 | tf_op jit(solution)/shard_map/ppermute | solution.py:379
  262.3 27.6 %collective-permute-start.46 = (bf16[2,320,640]{2,1,0:T(8,128)(2,1)}, bf16[2,320,640]{2,1,0:T(8,128)(2,1)S(1)}, u32[]{:S(2)}, u32[]{:S(2)}) collective-permute-start(bf16[2,320,640]{2,1,0:T(8,128)(2,1)} %get-tuple-element.294), channel_id=1, source_target_pairs={{0,16},{8,24},{16,0},{24,8},{1,17},{9,25},{17,1},{25,9},{2,18},{10... | collective-permute-start | bytes 2457608 | tf_op jit(solution)/shard_map/ppermute | solution.py:375
  265.6 24.3 %collective-permute-start.45 = (bf16[2,2,80,1024]{3,2,1,0:T(8,128)(2,1)S(1)}, bf16[2,2,80,1024]{3,2,1,0:T(8,128)(2,1)}, u32[]{:S(2)}, u32[]{:S(2)}) collective-permute-start(bf16[2,2,80,1024]{3,2,1,0:T(8,128)(2,1)S(1)} %fusion.4.refs_0_), channel_id=1, source_target_pairs={{0,2},{1,3},{2,0},{3,1},{4,6},{5,7},{6,4},{7,5},{8,10},{9,11},{10,... | collective-permute-start | bytes 1966088 | tf_op jit(solution)/shard_map/ppermute | solution.py:383
  282.1 30.2 %collective-permute-start.50 = (bf16[2,320,640]{2,1,0:T(8,128)(2,1)}, bf16[2,320,640]{2,1,0:T(8,128)(2,1)}, u32[]{:S(2)}, u32[]{:S(2)}) collective-permute-start(bf16[2,320,640]{2,1,0:T(8,128)(2,1)} %fusion.1), channel_id=1, source_target_pairs={{0,16},{8,24},{16,0},{24,8},{1,17},{9,25},{17,1},{25,9},{2,18},{10... | collective-permute-start | bytes 2457608 | tf_op jit(solution)/shard_map/ppermute | solution.py:375
  282.3 29.9 %collective-permute-start.49 = (bf16[2,320,640]{2,1,0:T(8,128)(2,1)}, bf16[2,320,640]{2,1,0:T(8,128)(2,1)}, u32[]{:S(2)}, u32[]{:S(2)}) collective-permute-start(bf16[2,320,640]{2,1,0:T(8,128)(2,1)} %get-tuple-element.318), channel_id=1, source_target_pairs={{0,1},{1,0},{2,3},{3,2},{4,5},{5,4},{6,7},{7,6},{8,9},{9,8},{10,11... | collective-permute-start | bytes 2457608 | tf_op jit(solution)/shard_map/ppermute | solution.py:379
  290.0 22.2 %collective-permute-start.51 = (bf16[2,80,1024]{2,1,0:T(8,128)(2,1)}, bf16[2,80,1024]{2,1,0:T(8,128)(2,1)}, u32[]{:S(2)}, u32[]{:S(2)}) collective-permute-start(bf16[2,80,1024]{2,1,0:T(8,128)(2,1)} %get-tuple-element.308), channel_id=1, source_target_pairs={{0,4},{1,5},{2,6},{3,7},{4,0},{5,1},{6,2},{7,3},{8,12},{9,13},{10,... | collective-permute-start | bytes 983048 | tf_op jit(solution)/shard_map/ppermute | solution.py:387
  294.1 34.8 %collective-permute-start.53 = (bf16[2,320,640]{2,1,0:T(8,128)(2,1)}, bf16[2,320,640]{2,1,0:T(8,128)(2,1)}, u32[]{:S(2)}, u32[]{:S(2)}) collective-permute-start(bf16[2,320,640]{2,1,0:T(8,128)(2,1)} %get-tuple-element.328), channel_id=1, source_target_pairs={{0,16},{8,24},{16,0},{24,8},{1,17},{9,25},{17,1},{25,9},{2,18},{10... | collective-permute-start | bytes 2457608 | tf_op jit(solution)/shard_map/ppermute | solution.py:375
  295.3 33.5 %collective-permute-start.54 = (bf16[2,320,640]{2,1,0:T(8,128)(2,1)}, bf16[2,320,640]{2,1,0:T(8,128)(2,1)}, u32[]{:S(2)}, u32[]{:S(2)}) collective-permute-start(bf16[2,320,640]{2,1,0:T(8,128)(2,1)} %add_convert_fusion), channel_id=1, source_target_pairs={{0,1},{1,0},{2,3},{3,2},{4,5},{5,4},{6,7},{7,6},{8,9},{9,8},{10,11... | collective-permute-start | bytes 2457608 | tf_op jit(solution)/shard_map/ppermute | solution.py:379
  316.8 23.7 %collective-permute-start.55 = (bf16[320,640]{1,0:T(8,128)(2,1)}, bf16[320,640]{1,0:T(8,128)(2,1)}, u32[]{:S(2)}, u32[]{:S(2)}) collective-permute-start(bf16[320,640]{1,0:T(8,128)(2,1)} %fusion.12), channel_id=1, source_target_pairs={{0,4},{1,5},{2,6},{3,7},{4,0},{5,1},{6,2},{7,3},{8,12},{9,13},{10,... | collective-permute-start | bytes 1228808 | tf_op jit(solution)/shard_map/ppermute | solution.py:387
  369.1 21.9 %collective-permute-start.62 = (bf16[2,160,640]{2,1,0:T(8,128)(2,1)}, bf16[2,160,640]{2,1,0:T(8,128)(2,1)S(1)}, u32[]{:S(2)}, u32[]{:S(2)}) collective-permute-start(bf16[2,160,640]{2,1,0:T(8,128)(2,1)} %get-tuple-element.347), channel_id=1, source_target_pairs={{0,1},{1,0},{2,3},{3,2},{4,5},{5,4},{6,7},{7,6},{8,9},{9,8},{10,11... | collective-permute-start | bytes 1228808 | tf_op jit(solution)/shard_map/ppermute | solution.py:379
  370.4 20.6 %collective-permute-start.63 = (bf16[320,640]{1,0:T(8,128)(2,1)S(1)}, bf16[320,640]{1,0:T(8,128)(2,1)}, u32[]{:S(2)}, u32[]{:S(2)}) collective-permute-start(bf16[320,640]{1,0:T(8,128)(2,1)S(1)} %copy-done.49), channel_id=1, source_target_pairs={{0,4},{1,5},{2,6},{3,7},{4,0},{5,1},{6,2},{7,3},{8,12},{9,13},{10,... | collective-permute-start | bytes 1228808 | tf_op jit(solution)/shard_map/ppermute | solution.py:387
  382.1 20.1 %collective-permute-start.72 = (f32[2,960]{1,0:T(2,128)S(1)}, f32[2,960]{1,0:T(2,128)S(1)}, u32[]{:S(2)}, u32[]{:S(2)}) collective-permute-start(f32[2,960]{1,0:T(2,128)S(1)} %fusion.21), channel_id=1, source_target_pairs={{0,4},{1,5},{2,6},{3,7},{4,0},{5,1},{6,2},{7,3},{8,12},{9,13},{10,... | collective-permute-start | bytes 23048 | tf_op jit(solution)/shard_map/ppermute | solution.py:387
  397.3 22.0 %collective-permute-start.65 = (bf16[2,80,1024]{2,1,0:T(8,128)(2,1)}, bf16[2,80,1024]{2,1,0:T(8,128)(2,1)}, u32[]{:S(2)}, u32[]{:S(2)}) collective-permute-start(bf16[2,80,1024]{2,1,0:T(8,128)(2,1)} %get-tuple-element.352), channel_id=1, source_target_pairs={{0,4},{1,5},{2,6},{3,7},{4,0},{5,1},{6,2},{7,3},{8,12},{9,13},{10,... | collective-permute-start | bytes 983048 | tf_op jit(solution)/shard_map/ppermute | solution.py:387
  411.8 29.0 %collective-permute-start.77 = (bf16[160,640]{1,0:T(8,128)(2,1)}, bf16[160,640]{1,0:T(8,128)(2,1)}, u32[]{:S(2)}, u32[]{:S(2)}) collective-permute-start(bf16[160,640]{1,0:T(8,128)(2,1)} %fusion.17), channel_id=1, source_target_pairs={{0,4},{1,5},{2,6},{3,7},{4,0},{5,1},{6,2},{7,3},{8,12},{9,13},{10,... | collective-permute-start | bytes 614408 | tf_op jit(solution)/shard_map/ppermute | solution.py:387
  418.4 19.4 %collective-permute-start.78 = (f32[320,640]{1,0:T(8,128)}, f32[320,640]{1,0:T(8,128)}, u32[]{:S(2)}, u32[]{:S(2)}) collective-permute-start(f32[320,640]{1,0:T(8,128)} %get-tuple-element.372), channel_id=1, source_target_pairs={{0,8},{8,0},{16,24},{24,16},{1,9},{9,1},{17,25},{25,17},{2,10},{10... | collective-permute-start | bytes 2457608 | tf_op jit(solution)/shard_map/ppermute | solution.py:371
  (119 other events, 985.0 us)
